TPU v7x, 32 devices: a whole 2x2x4 slice. The times are simulated.
32 devices in a mesh: row: 8 (over y, x, core), col: 4 (over z).
Axes of the slice: x: 2, y: 2, z: 4, core: 2. Of those that a mesh axis runs over, the one named last changes fastest.
Arguments:
- hidden_in: bfloat16 [16384, 1024], P('row', 'col'), may hold values from -6 to 6
- query_weight: bfloat16 [1024, 1024], P('row', 'col'), may hold values from -0.1875 to 0.1875
- key_weight: bfloat16 [1024, 1024], P('row', 'col'), may hold values from -0.1875 to 0.1875
- value_weight: bfloat16 [1024, 1024], P('row', 'col'), may hold values from -0.1875 to 0.1875
- query_bias: float32 [1024], P('col'), may hold values from -3 to 3
- value_bias: float32 [1024], P('col'), may hold values from -3 to 3
- proj_weight: bfloat16 [1024, 1024], P('col', 'row'), may hold values from -1 to 1
- proj_bias: float32 [1024], P('col'), may hold values from -3 to 3
- attn_gain: float32 [1024], P('col'), may hold values from 0.25 to 1.75
- attn_shift: float32 [1024], P('col'), may hold values from -3 to 3
- inner_weight: bfloat16 [1024, 4096], P('row', 'col'), may hold values from -0.1875 to 0.1875
- inner_bias: float32 [4096], P('col'), may hold values from -3 to 3
- outer_weight: bfloat16 [4096, 1024], P('col', 'row'), may hold values from -0.09375 to 0.09375
- outer_bias: float32 [1024], P('col'), may hold values from -3 to 3
- ffn_gain: float32 [1024], P('col'), may hold values from 0.25 to 1.75
- ffn_shift: float32 [1024], P('col'), may hold values from -3 to 3
- segment_ids: int32 [8, 2048], P('row'), may hold values from 0 to 15, never falling along the last dimension, each value on 1 to 1024 neighbouring positions
- grad_out: bfloat16 [16384, 1024], P('row', 'col'), may hold values from -6 to 6
Outputs:
- hidden_out: float32 [16384, 1024], P('row', 'col')
- grad_in: float32 [16384, 1024], P('row', 'col')
- grad_query_weight: float32 [1024, 1024], P('row', 'col')
- grad_key_weight: float32 [1024, 1024], P('row', 'col')
- grad_value_weight: float32 [1024, 1024], P('row', 'col')
- grad_query_bias: float32 [1024], P('col')
- grad_value_bias: float32 [1024], P('col')
- grad_proj_weight: float32 [1024, 1024], P('col', 'row')
- grad_proj_bias: float32 [1024], P('col')
- grad_attn_gain: float32 [1024], P('col')
- grad_attn_shift: float32 [1024], P('col')
- grad_inner_weight: float32 [1024, 4096], P('row', 'col')
- grad_inner_bias: float32 [4096], P('col')
- grad_outer_weight: float32 [4096, 1024], P('col', 'row')
- grad_outer_bias: float32 [1024], P('col')
- grad_ffn_gain: float32 [1024], P('col')
- grad_ffn_shift: float32 [1024], P('col')
Inputs may be any that keep to these rules, and one draw needn't show every extreme that they name: `segment_ids`: each row is one packed sequence of 2048 tokens: the numbers never fall along it, every number from 0 to 15 appears, each document has 1 to 1024 tokens and one has exactly 1024.
All inputs are finite; a program needn't handle non-finite values.
Results may differ from a plain program's by a relative error of at most 0.035.
Values may be sent and summed in bfloat16 or wider, within the bound.
A program may use at most 256 MiB of HBM per device.

v0:
```python
import jax
import jax.numpy as jnp
from jax import lax
from jax.sharding import PartitionSpec as P

D = 1024
HEAD_DIM = 64
LEN = 2048
QBLOCK = 512
SEQS = 1


EPSILON = 1e-06
NEG_FILL = -1e30


def rounded(values):
    return values.astype(jnp.bfloat16)


def matmul(left, right):
    return jnp.dot(left, right, preferred_element_type=jnp.float32)


def over_tokens(left, right):
    return lax.dot_general(
        left, right, (((0,), (0,)), ((), ())), preferred_element_type=jnp.float32
    )


def against(left, right):
    return lax.dot_general(
        left, right, (((1,), (1,)), ((), ())), preferred_element_type=jnp.float32
    )


def token_sum(values):
    return jnp.sum(values, axis=0, dtype=jnp.float32)


def exact_gelu(inputs):
    return jax.nn.gelu(inputs, approximate=False)


def gather_weights(shards):
    front_set = (
        lax.all_gather(shards[0], "row", axis=0, tiled=True),
        lax.all_gather(shards[1], "row", axis=0, tiled=True),
        lax.all_gather(shards[2], "row", axis=0, tiled=True),
        lax.all_gather(shards[3], "row", axis=0, tiled=True),
    )
    back_set = (
        lax.all_gather(shards[4], "row", axis=1, tiled=True),
        lax.all_gather(shards[5], "row", axis=1, tiled=True),
    )
    proj_cols = back_set[0]
    return (
        front_set[0],
        front_set[1],
        front_set[2],
        front_set[3],
        back_set[0],
        back_set[1],
        proj_cols,
    )


def spread_features(values):
    return lax.all_gather(rounded(values), "col", axis=1, tiled=True)


def sum_partials(partial_terms):
    return lax.psum_scatter(
        partial_terms.astype(jnp.bfloat16), "col", scatter_dimension=1, tiled=True
    ).astype(jnp.float32)


def spread_grads(values):
    return lax.all_gather(values, "col", axis=1, tiled=True)


def sum_grad_partials(partial_terms):
    return lax.psum_scatter(
        partial_terms.astype(jnp.bfloat16), "col", scatter_dimension=1, tiled=True
    ).astype(jnp.float32)


def norm_forward(summed, norm_gain, norm_shift):
    totals = lax.psum((jnp.sum(summed, axis=1), jnp.sum(summed * summed, axis=1)), "col")
    center = totals[0][:, None] / D
    spread = totals[1][:, None] / D - center * center
    inverse = lax.rsqrt(spread + EPSILON)
    normed = (summed - center) * inverse
    return (normed * norm_gain + norm_shift, normed, inverse)


def norm_backward(grad_output, normed, inverse, norm_gain):
    scaled = grad_output * norm_gain
    totals = lax.psum((jnp.sum(scaled, axis=1), jnp.sum(scaled * normed, axis=1)), "col")
    grad_input = inverse * (scaled - totals[0][:, None] / D - normed * (totals[1][:, None] / D))
    return (grad_input, jnp.sum(grad_output * normed, axis=0), jnp.sum(grad_output, axis=0))


def split_heads(values):
    return values.reshape(SEQS, LEN, values.shape[1] // HEAD_DIM, HEAD_DIM)


def attend_forward(queries, key_rows, value_rows, segments):
    score_scale = HEAD_DIM ** (-0.5)
    blocks = LEN // QBLOCK
    query_heads = split_heads(queries)
    key_heads = split_heads(key_rows)
    value_heads = split_heads(value_rows)

    def attend_one_block(block_index):
        sequence = block_index // blocks
        offset = block_index % blocks * QBLOCK
        seq_queries = lax.dynamic_index_in_dim(query_heads, sequence, 0, keepdims=False)
        seq_keys = lax.dynamic_index_in_dim(key_heads, sequence, 0, keepdims=False)
        seq_values = lax.dynamic_index_in_dim(value_heads, sequence, 0, keepdims=False)
        seq_segments = lax.dynamic_index_in_dim(segments, sequence, 0, keepdims=False)
        block_queries = lax.dynamic_slice_in_dim(seq_queries, offset, QBLOCK, 0)
        block_segments = lax.dynamic_slice_in_dim(seq_segments, offset, QBLOCK, 0)
        scores = (
            jnp.einsum("qhd,khd->hqk", block_queries, seq_keys, preferred_element_type=jnp.float32)
            * score_scale
        )
        same_doc = block_segments[:, None] == seq_segments[None, :]
        scores = jnp.where(same_doc[None], scores, NEG_FILL)
        highest = jnp.max(scores, axis=2, keepdims=True)
        weights = jnp.exp(scores - highest)
        totals = jnp.sum(weights, axis=2, keepdims=True)
        mixture = jnp.einsum(
            "hqk,khd->qhd",
            rounded(weights / totals),
            seq_values,
            preferred_element_type=jnp.float32,
        )
        return (mixture, (highest + jnp.log(totals))[:, :, 0])

    mixture, log_total = lax.map(attend_one_block, jnp.arange(SEQS * blocks))
    return (mixture.reshape(queries.shape), log_total)


def attend_backward(queries, key_rows, value_rows, segments, log_total, grad_mixed):
    score_scale = HEAD_DIM ** (-0.5)
    blocks = LEN // QBLOCK
    heads_here = queries.shape[1] // HEAD_DIM
    query_heads = split_heads(queries)
    key_heads = split_heads(key_rows)
    value_heads = split_heads(value_rows)
    grad_heads = split_heads(grad_mixed)
    lse_rows = log_total.reshape(SEQS, blocks, heads_here, QBLOCK)

    def one_sequence(sequence):
        seq_queries = lax.dynamic_index_in_dim(query_heads, sequence, 0, keepdims=False)
        seq_keys = lax.dynamic_index_in_dim(key_heads, sequence, 0, keepdims=False)
        seq_values = lax.dynamic_index_in_dim(value_heads, sequence, 0, keepdims=False)
        seq_grads = lax.dynamic_index_in_dim(grad_heads, sequence, 0, keepdims=False)
        seq_segments = lax.dynamic_index_in_dim(segments, sequence, 0, keepdims=False)
        seq_lse = lax.dynamic_index_in_dim(lse_rows, sequence, 0, keepdims=False)

        def one_one_block(carry, block_index):
            offset = block_index * QBLOCK
            block_queries = lax.dynamic_slice_in_dim(seq_queries, offset, QBLOCK, 0)
            block_grads = lax.dynamic_slice_in_dim(seq_grads, offset, QBLOCK, 0)
            block_segments = lax.dynamic_slice_in_dim(seq_segments, offset, QBLOCK, 0)
            block_lse = lax.dynamic_index_in_dim(seq_lse, block_index, 0, keepdims=False)
            scores = (
                jnp.einsum(
                    "qhd,khd->hqk", block_queries, seq_keys, preferred_element_type=jnp.float32
                )
                * score_scale
            )
            same_doc = block_segments[:, None] == seq_segments[None, :]
            scores = jnp.where(same_doc[None], scores, NEG_FILL)
            probs = jnp.exp(scores - block_lse[:, :, None])
            grad_probs = jnp.einsum(
                "qhd,khd->hqk", block_grads, seq_values, preferred_element_type=jnp.float32
            )
            grad_scores = rounded(
                probs * (grad_probs - jnp.sum(probs * grad_probs, axis=2, keepdims=True))
            )
            grad_query = (
                jnp.einsum(
                    "hqk,khd->qhd", grad_scores, seq_keys, preferred_element_type=jnp.float32
                )
                * score_scale
            )
            key_sum = (
                carry[0]
                + jnp.einsum(
                    "hqk,qhd->khd", grad_scores, block_queries, preferred_element_type=jnp.float32
                )
                * score_scale
            )
            value_sum = carry[1] + jnp.einsum(
                "hqk,qhd->khd", rounded(probs), block_grads, preferred_element_type=jnp.float32
            )
            return ((key_sum, value_sum), rounded(grad_query))

        zeros_init = jnp.zeros((LEN, heads_here, HEAD_DIM), jnp.float32)
        (key_sum, value_sum), grad_query = lax.scan(
            one_one_block, (zeros_init, zeros_init), jnp.arange(blocks)
        )
        return (grad_query.reshape(LEN, heads_here, HEAD_DIM), rounded(key_sum), rounded(value_sum))

    grad_query, grad_key, grad_value = lax.map(one_sequence, jnp.arange(SEQS))
    return (
        grad_query.reshape(queries.shape),
        grad_key.reshape(queries.shape),
        grad_value.reshape(queries.shape),
    )


def layer_forward(hidden, params, gathered, segments):
    query_w, key_w, value_w, inner_w, proj_w, outer_w, proj_cols = gathered
    whole_in = spread_features(hidden)
    queries = rounded(matmul(whole_in, query_w) + params[0])
    key_rows = rounded(matmul(whole_in, key_w))
    value_rows = rounded(matmul(whole_in, value_w) + params[1])
    mixture, log_total = attend_forward(queries, key_rows, value_rows, segments)
    attended = rounded(mixture)
    attn_branch = sum_partials(matmul(attended, proj_w)) + params[2]
    first_norm, normed_one, inverse_one = norm_forward(hidden + attn_branch, params[3], params[4])
    whole_mid = spread_features(first_norm)
    inner_act = matmul(whole_mid, inner_w) + params[5]
    active = rounded(exact_gelu(inner_act))
    ffn_branch = sum_partials(matmul(active, outer_w)) + params[6]
    output, normed_two, inverse_two = norm_forward(first_norm + ffn_branch, params[7], params[8])
    kept_values = (
        whole_in,
        queries,
        key_rows,
        value_rows,
        log_total,
        attended,
        normed_one,
        inverse_one,
        whole_mid,
        inner_act,
        active,
        normed_two,
        inverse_two,
    )
    return (output, kept_values)


def layer_backward(grad_output, kept_values, gathered, params, segments):
    (
        whole_in,
        queries,
        key_rows,
        value_rows,
        log_total,
        attended,
        normed_one,
        inverse_one,
        whole_mid,
        inner_act,
        active,
        normed_two,
        inverse_two,
    ) = kept_values
    query_w, key_w, value_w, inner_w, proj_w, outer_w, proj_cols = gathered
    grad_second, ffn_gain_sum, ffn_shift_sum = norm_backward(
        grad_output, normed_two, inverse_two, params[7]
    )
    ffn_low = rounded(grad_second)
    whole_second = spread_grads(ffn_low)
    outer_term = over_tokens(active, whole_second)
    active_grad = against(whole_second, outer_w)
    unused, pullback = jax.vjp(exact_gelu, inner_act)
    inner_low = rounded(pullback(active_grad)[0])
    inner_term = over_tokens(whole_mid, inner_low)
    grad_first = grad_second + sum_grad_partials(against(inner_low, inner_w))
    grad_attn, attn_gain_sum, attn_shift_sum = norm_backward(
        grad_first, normed_one, inverse_one, params[3]
    )
    attn_low = rounded(grad_attn)
    whole_attn = spread_grads(attn_low)
    proj_term = over_tokens(attended, whole_attn)
    mixed_grad = rounded(against(whole_attn, proj_w))
    query_low, key_low, value_low = attend_backward(
        queries, key_rows, value_rows, segments, log_total, mixed_grad
    )
    input_terms = (
        against(query_low, query_w) + against(key_low, key_w) + against(value_low, value_w)
    )
    grad_input = grad_attn + sum_grad_partials(input_terms)
    row_terms = (
        over_tokens(whole_in, query_low),
        over_tokens(whole_in, key_low),
        over_tokens(whole_in, value_low),
        inner_term,
    )
    col_terms = (proj_term, outer_term)
    small_terms = (
        token_sum(query_low),
        token_sum(value_low),
        token_sum(attn_low),
        attn_gain_sum,
        attn_shift_sum,
        token_sum(inner_low),
        token_sum(ffn_low),
        ffn_gain_sum,
        ffn_shift_sum,
    )
    return (grad_input, row_terms, col_terms, small_terms)


def per_device(
    hidden_in,
    query_weight,
    key_weight,
    value_weight,
    query_bias,
    value_bias,
    proj_weight,
    proj_bias,
    attn_gain,
    attn_shift,
    inner_weight,
    inner_bias,
    outer_weight,
    outer_bias,
    ffn_gain,
    ffn_shift,
    segment_ids,
    grad_out,
):
    shards = (query_weight, key_weight, value_weight, inner_weight, proj_weight, outer_weight)
    params = (
        query_bias,
        value_bias,
        proj_bias,
        attn_gain,
        attn_shift,
        inner_bias,
        outer_bias,
        ffn_gain,
        ffn_shift,
    )
    gathered = gather_weights(shards)
    start_in = hidden_in.astype(jnp.float32)
    middle, kept_one = layer_forward(start_in, params, gathered, segment_ids)
    final_out, kept_two = layer_forward(middle, params, gathered, segment_ids)
    inputs = (start_in, middle)
    final_out, inputs, shards = lax.optimization_barrier((final_out, inputs, shards))
    gathered = gather_weights(shards)
    grad_flow = grad_out.astype(jnp.float32)
    row_parts = []
    col_parts = []
    small_parts = []
    for layer_index in (1, 0):
        unused, kept_values = layer_forward(inputs[layer_index], params, gathered, segment_ids)
        grad_flow, row_terms, col_terms, small_terms = layer_backward(
            grad_flow, kept_values, gathered, params, segment_ids
        )
        row_parts.append(row_terms)
        col_parts.append(col_terms)
        small_parts.append(small_terms)
    row_sum = jax.tree.map(jnp.add, tuple(row_parts[0]), tuple(row_parts[1]))
    col_sum = jax.tree.map(jnp.add, tuple(col_parts[0]), tuple(col_parts[1]))
    small_sum = jax.tree.map(jnp.add, small_parts[0], small_parts[1])
    row_sum = (
        lax.psum_scatter(
            row_sum[0].astype(jnp.bfloat16), "row", scatter_dimension=0, tiled=True
        ).astype(jnp.float32),
        lax.psum_scatter(
            row_sum[1].astype(jnp.bfloat16), "row", scatter_dimension=0, tiled=True
        ).astype(jnp.float32),
        lax.psum_scatter(
            row_sum[2].astype(jnp.bfloat16), "row", scatter_dimension=0, tiled=True
        ).astype(jnp.float32),
        lax.psum_scatter(
            row_sum[3].astype(jnp.bfloat16), "row", scatter_dimension=0, tiled=True
        ).astype(jnp.float32),
    )
    col_sum = (
        lax.psum_scatter(
            col_sum[0].astype(jnp.bfloat16), "row", scatter_dimension=1, tiled=True
        ).astype(jnp.float32),
        lax.psum_scatter(
            col_sum[1].astype(jnp.bfloat16), "row", scatter_dimension=1, tiled=True
        ).astype(jnp.float32),
    )
    small_sum = lax.psum(
        (
            small_sum[0],
            small_sum[1],
            small_sum[2],
            small_sum[3],
            small_sum[4],
            small_sum[5],
            small_sum[6],
            small_sum[7],
            small_sum[8],
        ),
        "row",
    )
    return (
        final_out,
        grad_flow,
        row_sum[0],
        row_sum[1],
        row_sum[2],
        small_sum[0],
        small_sum[1],
        col_sum[0],
        small_sum[2],
        small_sum[3],
        small_sum[4],
        row_sum[3],
        small_sum[5],
        col_sum[1],
        small_sum[6],
        small_sum[7],
        small_sum[8],
    )


def solution(mesh):
    in_specs = (
        P("row", "col"),
        P("row", "col"),
        P("row", "col"),
        P("row", "col"),
        P("col"),
        P("col"),
        P("col", "row"),
        P("col"),
        P("col"),
        P("col"),
        P("row", "col"),
        P("col"),
        P("col", "row"),
        P("col"),
        P("col"),
        P("col"),
        P("row", None),
        P("row", "col"),
    )
    out_specs = (
        P("row", "col"),
        P("row", "col"),
        P("row", "col"),
        P("row", "col"),
        P("row", "col"),
        P("col"),
        P("col"),
        P("col", "row"),
        P("col"),
        P("col"),
        P("col"),
        P("row", "col"),
        P("col"),
        P("col", "row"),
        P("col"),
        P("col"),
        P("col"),
    )
    return jax.shard_map(
        per_device, mesh=mesh, in_specs=in_specs, out_specs=out_specs, check_vma=False
    )
```

profile of v0, /device:TPU:0, one launch (start us, length us, event | category | flops | bytes accessed | tf_op | source)
XLA Modules:
  0.0 3072.2 jit_solution(2928875130260558061)
XLA Ops:
  8.8 11.6 all_gather.73
  48.8 45.0 %all-gather.17.cloned.1.call-done = bf16[2048,1024]{1,0:T(8,128)(2,1)} async-done(((bf16[2048,256]{1,0:T(8,128)(2,1)}), bf16[2048,1024]{1,0:T(8,128)(2,1)}) %all-gather.17.cloned.1.call-update) | async-done | bytes 4194320 | tf_op jit(solution)/shard_map/all_gather | solution.py:69
  103.0 90.1 %while.104 = (s32[]{:T(128)}, bf16[4,512,4,64]{1,3,2,0:T(8,128)(2,1)S(1)}, s32[4]{0:T(128)S(1)}, s32[1,2048]{1,0:T(1,128)S(1)}, bf16[1,2048,4,64]{1,3,2,0:T(8,12...) while((s32[]{:T(128)}, ...), condition=%wide.region_3.4_spmd, body=%wide.region_0.3_spmd.sunk | while | flops 1099958272 | bytes 38566200 | solution.py:141
  198.8 73.9 %reduce-scatter.23.cloned.1.call-done = bf16[2048,256]{1,0:T(8,128)(2,1)} async-done(((bf16[2048,1024]{1,0:T(8,128)(2,1)}), bf16[2048,256]{1,0:T(8,128)(2,1)}) %reduce-scatter.23.cloned.1.call-update) | async-done | bytes 1048592 | tf_op jit(solution)/shard_map/reduce_scatter | solution.py:73
  274.6 18.0 all-reduce.10
  295.3 78.8 %all-gather.19.cloned.1.call-done = bf16[2048,1024]{1,0:T(8,128)(2,1)} async-done(((bf16[2048,256]{1,0:T(8,128)(2,1)}), bf16[2048,1024]{1,0:T(8,128)(2,1)}) %all-gather.19.cloned.1.call-update) | async-done | bytes 4194320 | tf_op jit(solution)/shard_map/all_gather | solution.py:69
  374.1 29.6 fusion.180
  403.8 75.0 %reduce-scatter.25.cloned.1.call-done = bf16[2048,256]{1,0:T(8,128)(2,1)} async-done(((bf16[2048,1024]{1,0:T(8,128)(2,1)}), bf16[2048,256]{1,0:T(8,128)(2,1)}) %reduce-scatter.25.cloned.1.call-update) | async-done | bytes 1048592 | tf_op jit(solution)/shard_map/reduce_scatter | solution.py:73
  482.3 17.9 all-reduce.9
  503.0 79.0 %all-gather.25.cloned.1.call-done = bf16[2048,1024]{1,0:T(8,128)(2,1)} async-done(((bf16[2048,256]{1,0:T(8,128)(2,1)}), bf16[2048,1024]{1,0:T(8,128)(2,1)}) %all-gather.25.cloned.1.call-update) | async-done | bytes 4194320 | tf_op jit(solution)/shard_map/all_gather | solution.py:69
  592.4 92.6 %while.105 = (s32[]{:T(128)}, bf16[4,512,4,64]{1,3,2,0:T(8,128)(2,1)}, s32[4]{0:T(128)S(1)}, s32[1,2048]{1,0:T(1,128)S(1)}, bf16[1,2048,4,64]{1,3,2,0:T(8,128)(2...) while((s32[]{:T(128)}, ...), condition=%wide.region_17.18_spmd, body=%wide.region_14.17_spmd.sunk | while | flops 1099958272 | bytes 38566200 | solution.py:141
  691.7 75.0 %reduce-scatter.27.cloned.1.call-done = bf16[2048,256]{1,0:T(8,128)(2,1)} async-done(((bf16[2048,1024]{1,0:T(8,128)(2,1)}), bf16[2048,256]{1,0:T(8,128)(2,1)}) %reduce-scatter.27.cloned.1.call-update) | async-done | bytes 1048592 | tf_op jit(solution)/shard_map/reduce_scatter | solution.py:73
  768.6 18.0 all-reduce.8
  789.2 78.8 %all-gather.27.cloned.1.call-done = bf16[2048,1024]{1,0:T(8,128)(2,1)} async-done(((bf16[2048,256]{1,0:T(8,128)(2,1)}), bf16[2048,1024]{1,0:T(8,128)(2,1)}) %all-gather.27.cloned.1.call-update) | async-done | bytes 4194320 | tf_op jit(solution)/shard_map/all_gather | solution.py:69
  868.0 29.4 fusion.183
  899.4 73.1 %reduce-scatter.29.cloned.1.call-done = bf16[2048,256]{1,0:T(8,128)(2,1)} async-done(((bf16[2048,1024]{1,0:T(8,128)(2,1)}), bf16[2048,256]{1,0:T(8,128)(2,1)}) %reduce-scatter.29.cloned.1.call-update) | async-done | bytes 1048592 | tf_op jit(solution)/shard_map/reduce_scatter | solution.py:73
  975.9 18.0 all-reduce.7
  1041.4 35.6 %all-gather.37.cloned.1.call-done = bf16[2048,1024]{1,0:T(8,128)(2,1)} async-done(((bf16[2048,256]{1,0:T(8,128)(2,1)}), bf16[2048,1024]{1,0:T(8,128)(2,1)}) %all-gather.37.cloned.1.call-update) | async-done | bytes 4194320 | tf_op jit(solution)/shard_map/all_gather | solution.py:69
  1084.5 66.4 %while.107 = (s32[]{:T(128)}, bf16[4,512,4,64]{1,3,2,0:T(8,128)(2,1)}, f32[4,4,512]{2,1,0:T(4,128)S(1)}, s32[4]{0:T(128)S(1)}, s32[1,2048]{1,0:T(1,128)S(1)}, /*...) while((s32[]{:T(128)}, ...), condition=%wide.region_45.46_spmd, body=%wide.region_42.45_spmd.sunk | while | flops 1125120000 | bytes 65878396 | solution.py:141
  1167.1 66.6 %while.106 = (s32[]{:T(128)}, bf16[4,512,4,64]{1,3,2,0:T(8,128)(2,1)}, f32[4,4,512]{2,1,0:T(4,128)S(1)}, s32[4]{0:T(128)S(1)}, s32[1,2048]{1,0:T(1,128)S(1)}, /*...) while((s32[]{:T(128)}, ...), condition=%wide.region_31.32_spmd, body=%wide.region_28.31_spmd.sunk | while | flops 1125120000 | bytes 65878396 | solution.py:141
  1244.5 74.4 %reduce-scatter.31.cloned.1.call-done = bf16[2048,256]{1,0:T(8,128)(2,1)} async-done(((bf16[2048,1024]{1,0:T(8,128)(2,1)}), bf16[2048,256]{1,0:T(8,128)(2,1)}) %reduce-scatter.31.cloned.1.call-update) | async-done | bytes 1048592 | tf_op jit(solution)/shard_map/reduce_scatter | solution.py:73
  1323.5 17.9 all-reduce.6
  1348.9 82.0 %all-gather.39.cloned.1.call-done = bf16[2048,1024]{1,0:T(8,128)(2,1)} async-done(((bf16[2048,256]{1,0:T(8,128)(2,1)}), bf16[2048,1024]{1,0:T(8,128)(2,1)}) %all-gather.39.cloned.1.call-update) | async-done | bytes 4194320 | tf_op jit(solution)/shard_map/all_gather | solution.py:69
  1430.9 26.4 multiply_convert_fusion.2
  1468.4 76.9 %reduce-scatter.37.cloned.1.call-done = bf16[2048,256]{1,0:T(8,128)(2,1)} async-done(((bf16[2048,1024]{1,0:T(8,128)(2,1)}), bf16[2048,256]{1,0:T(8,128)(2,1)}) %reduce-scatter.37.cloned.1.call-update) | async-done | bytes 1048592 | tf_op jit(solution)/shard_map/reduce_scatter | solution.py:73
  1548.9 18.0 all-reduce.5
  1570.0 15.8 all-reduce.4
  1593.0 74.7 %all-gather.31.cloned.1.call-done = bf16[2048,1024]{1,0:T(8,128)(2,1)} async-done(((bf16[2048,256]{1,0:T(8,128)(2,1)}), bf16[2048,1024]{1,0:T(8,128)(2,1)}) %all-gather.31.cloned.1.call-update) | async-done | bytes 4194320 | tf_op jit(solution)/shard_map/all_gather | solution.py:69
  1678.4 69.8 %all-gather.41.cloned.1.call-done = bf16[2048,1024]{1,0:T(8,128)(2,1)} async-done(((bf16[2048,256]{1,0:T(8,128)(2,1)}), bf16[2048,1024]{1,0:T(8,128)(2,1)}) %all-gather.41.cloned.1.call-update) | async-done | bytes 4194320 | tf_op jit(solution)/shard_map/all_gather | solution.py:79
  1748.2 31.7 %convert_reduce_fusion.1 = (f32[1024]{0:T(1024)}, bf16[2048,1024]{1,0:T(8,128)(2,1)S(1)}, bf16[2048,1024]{1,0:T(8,128)(2,1)}, f32[2048,1024]{1,0:T(8,128)}) fusion(f32[2048,1024]{1,0:T(8,128)} %get-tuple-element.877, f32[2048,1024]{1,0:T(8,128)} %get-tuple-element.920, f32[1024]{0:T(1024)S(1)} %copy-done.110, f32[2048,1024]{1,0:T(8,128)} %fusion.302, ...), kind=kOutput, calls=%fused_computation.161 | convolution fusion | flops 4469029888 | bytes 48242688 | tf_op jit(solution)/shard_map/dot_general | solution.py:32
  1798.2 65.2 %reduce-scatter.39.cloned.1.call-done = bf16[2048,256]{1,0:T(8,128)(2,1)} async-done(((bf16[2048,1024]{1,0:T(8,128)(2,1)}), bf16[2048,256]{1,0:T(8,128)(2,1)}) %reduce-scatter.39.cloned.1.call-update) | async-done | bytes 1048592 | tf_op jit(solution)/shard_map/reduce_scatter | solution.py:83
  1863.4 79.6 %reduce-scatter.33.cloned.1.call-done = bf16[2048,256]{1,0:T(8,128)(2,1)} async-done(((bf16[2048,1024]{1,0:T(8,128)(2,1)}), bf16[2048,256]{1,0:T(8,128)(2,1)}) %reduce-scatter.33.cloned.1.call-update) | async-done | bytes 1048592 | tf_op jit(solution)/shard_map/reduce_scatter | solution.py:73
  1948.8 18.8 all-reduce.3
  1973.8 78.9 %all-gather.43.cloned.1.call-done = bf16[2048,1024]{1,0:T(8,128)(2,1)} async-done(((bf16[2048,256]{1,0:T(8,128)(2,1)}), bf16[2048,1024]{1,0:T(8,128)(2,1)}) %all-gather.43.cloned.1.call-update) | async-done | bytes 4194320 | tf_op jit(solution)/shard_map/all_gather | solution.py:79
  2058.3 199.5 %while.108 = (s32[]{:T(128)}, f32[2048,4,64]{0,2,1:T(8,128)}, f32[2048,4,64]{0,2,1:T(8,128)}, bf16[4,512,4,64]{1,3,2,0:T(8,128)(2,1)}, s32[4]{0:T(128)S(1)}, /*i...) while((s32[]{:T(128)}, f32[2048,4,64]{0,2,1:T(8,128)}, ...), condition=%wide.region_67.68_spmd.clone, body=%wide.region_65.67_spmd.clone.sunk | while | flops 2751199232 | bytes 176527696 | solution.py:203
  2270.9 75.0 %reduce-scatter.41.cloned.1.call-done = bf16[2048,256]{1,0:T(8,128)(2,1)} async-done(((bf16[2048,1024]{1,0:T(8,128)(2,1)}), bf16[2048,256]{1,0:T(8,128)(2,1)}) %reduce-scatter.41.cloned.1.call-update) | async-done | bytes 1048592 | tf_op jit(solution)/shard_map/reduce_scatter | solution.py:83
  2349.1 17.9 all-reduce.2
  2372.8 79.0 %all-gather.45.cloned.1.call-done = bf16[2048,1024]{1,0:T(8,128)(2,1)} async-done(((bf16[2048,256]{1,0:T(8,128)(2,1)}), bf16[2048,1024]{1,0:T(8,128)(2,1)}) %all-gather.45.cloned.1.call-update) | async-done | bytes 4194320 | tf_op jit(solution)/shard_map/all_gather | solution.py:79
  2451.9 14.5 convert_reduce_fusion
  2474.8 75.0 %reduce-scatter.43.cloned.1.call-done = bf16[2048,256]{1,0:T(8,128)(2,1)} async-done(((bf16[2048,1024]{1,0:T(8,128)(2,1)}), bf16[2048,256]{1,0:T(8,128)(2,1)}) %reduce-scatter.43.cloned.1.call-update) | async-done | bytes 1048592 | tf_op jit(solution)/shard_map/reduce_scatter | solution.py:83
  2553.1 17.9 all-reduce.1
  2620.2 35.7 %all-gather.47.cloned.1.call-done = bf16[2048,1024]{1,0:T(8,128)(2,1)} async-done(((bf16[2048,256]{1,0:T(8,128)(2,1)}), bf16[2048,1024]{1,0:T(8,128)(2,1)}) %all-gather.47.cloned.1.call-update) | async-done | bytes 4194320 | tf_op jit(solution)/shard_map/all_gather | solution.py:79
  2666.4 199.8 %while.109 = (s32[]{:T(128)}, f32[2048,4,64]{0,2,1:T(8,128)}, f32[2048,4,64]{0,2,1:T(8,128)}, bf16[4,512,4,64]{1,3,2,0:T(8,128)(2,1)}, s32[4]{0:T(128)S(1)}, /*i...) while((s32[]{:T(128)}, f32[2048,4,64]{0,2,1:T(8,128)}, ...), condition=%wide.region_80.81_spmd.clone, body=%wide.region_78.80_spmd.clone.sunk | while | flops 2751199232 | bytes 176527696 | solution.py:203
  2682.1 11.4 multiply_reduce_fusion.22
  2781.6 11.4 multiply_reduce_fusion.22
  2911.1 24.5 all-reduce
  2946.4 35.8 %reduce-scatter.51.cloned.1.call-done = bf16[128,256]{1,0:T(8,128)(2,1)} async-done(((bf16[1024,256]{1,0:T(8,128)(2,1)}), bf16[128,256]{1,0:T(8,128)(2,1)}) %reduce-scatter.51.cloned.1.call-update) | async-done | bytes 65552 | tf_op jit(solution)/shard_map/reduce_scatter | solution.py:373
  2983.7 77.6 %reduce-scatter.45.cloned.1.call-done = bf16[2048,256]{1,0:T(8,128)(2,1)} async-done(((bf16[2048,1024]{1,0:T(8,128)(2,1)}), bf16[2048,256]{1,0:T(8,128)(2,1)}) %reduce-scatter.45.cloned.1.call-update) | async-done | bytes 1048592 | tf_op jit(solution)/shard_map/reduce_scatter | solution.py:83
  (693 shorter events, 1037.8 us)
Async XLA Ops:
  8.0 85.7 %all-gather.17.cloned.1.call-start = ((), (), s32[]{:S(2)}) async-start(), calls=%async_computation.18 | async-start | bytes 5242880 | tf_op jit(solution)/shard_map/all_gather | solution.py:69
  8.8 263.9 %reduce-scatter.23.cloned.1.call-start = ((), (), s32[]{:S(2)}) async-start(), calls=%async_computation.19 | async-start | bytes 5242880 | tf_op jit(solution)/shard_map/reduce_scatter | solution.py:73
  48.8 145.5 %copy-start.40 = (bf16[256,1024]{1,0:T(8,128)(2,1)}, bf16[256,1024]{1,0:T(8,128)(2,1)S(1)}, u32[]{:S(2)}) copy-start(bf16[256,1024]{1,0:T(8,128)(2,1)S(1)} %all_gather.76) | copy-start | bytes 1572868
  194.3 179.8 %copy-start.108 = (f32[1024]{0:T(1024)S(1)}, f32[1024]{0:T(1024)}, u32[]{:S(2)}) copy-start(f32[1024]{0:T(1024)} %param.41) | copy-start | bytes 12292
  197.6 97.7 %all-gather.21.cloned.1.call-start = ((), (), s32[]{:S(2)}) async-start(), calls=%async_computation.21 | async-start | bytes 2359296 | tf_op jit(solution)/shard_map/all_gather | solution.py:50
  198.2 97.1 %all-gather.23.cloned.1.call-start = ((), (), s32[]{:S(2)}) async-start(), calls=%async_computation.22 | async-start | bytes 2359296 | tf_op jit(solution)/shard_map/all_gather | solution.py:54
  198.7 175.3 %all-gather.19.cloned.1.call-start = ((), (), s32[]{:S(2)}) async-start(), calls=%async_computation.20 | async-start | bytes 5242880 | tf_op jit(solution)/shard_map/all_gather | solution.py:69
  295.2 183.6 %copy-start.20 = (bf16[2048,256]{1,0:T(8,128)(2,1)S(1)}, bf16[2048,256]{1,0:T(8,128)(2,1)}, u32[]{:S(2)}) copy-start(bf16[2048,256]{1,0:T(8,128)(2,1)} %reduce-scatter.23.cloned.1.call-done) | copy-start | bytes 3145732
  295.2 183.6 %copy-start.77 = (f32[256]{0:T(256)S(1)}, f32[256]{0:T(256)}, u32[]{:S(2)}) copy-start(f32[256]{0:T(256)} %param.43) | copy-start | bytes 3076
  295.2 183.6 %reduce-scatter.25.cloned.1.call-start = ((), (), s32[]{:S(2)}) async-start(), calls=%async_computation.23 | async-start | bytes 5242880 | tf_op jit(solution)/shard_map/reduce_scatter | solution.py:73
  403.7 178.3 %copy-start.55 = (bf16[1024,256]{1,0:T(8,128)(2,1)S(1)}, bf16[1024,256]{1,0:T(8,128)(2,1)}, u32[]{:S(2)}) copy-start(bf16[1024,256]{1,0:T(8,128)(2,1)} %copy-done.54) | copy-start | bytes 1572868
  403.7 178.3 %copy-start.113 = (f32[256]{0:T(256)S(1)}, f32[256]{0:T(256)}, u32[]{:S(2)}) copy-start(f32[256]{0:T(256)} %param.35) | copy-start | bytes 3076
  403.8 178.3 %all-gather.25.cloned.1.call-start = ((), (), s32[]{:S(2)}) async-start(), calls=%async_computation.24 | async-start | bytes 5242880 | tf_op jit(solution)/shard_map/all_gather | solution.py:69
  502.9 494.0 %copy-start.4 = (f32[2048,256]{1,0:T(8,128)}, f32[2048,256]{1,0:T(8,128)S(1)}, u32[]{:S(2)}) copy-start(f32[2048,256]{1,0:T(8,128)S(1)} %get-tuple-element.601) | copy-start | bytes 6291460
  502.9 263.8 %reduce-scatter.27.cloned.1.call-start = ((), (), s32[]{:S(2)}) async-start(), calls=%async_computation.25 | async-start | bytes 5242880 | tf_op jit(solution)/shard_map/reduce_scatter | solution.py:73
  691.6 176.4 %copy-start.109 = (f32[1024]{0:T(1024)S(1)}, f32[1024]{0:T(1024)}, u32[]{:S(2)}) copy-start(f32[1024]{0:T(1024)} %param.41) | copy-start | bytes 12292
  691.6 176.4 %all-gather.27.cloned.1.call-start = ((), (), s32[]{:S(2)}) async-start(), calls=%async_computation.26 | async-start | bytes 5242880 | tf_op jit(solution)/shard_map/all_gather | solution.py:69
  789.1 183.4 %copy-start.78 = (f32[256]{0:T(256)S(1)}, f32[256]{0:T(256)}, u32[]{:S(2)}) copy-start(f32[256]{0:T(256)} %param.43) | copy-start | bytes 3076
  789.2 183.3 %reduce-scatter.29.cloned.1.call-start = ((), (), s32[]{:S(2)}) async-start(), calls=%async_computation.27 | async-start | bytes 5242880 | tf_op jit(solution)/shard_map/reduce_scatter | solution.py:73
  897.4 179.6 %all-gather.37.cloned.1.call-start = ((), (), s32[]{:S(2)}) async-start(), calls=%async_computation.34 | async-start | bytes 5242880 | tf_op jit(solution)/shard_map/all_gather | solution.py:69
  899.4 131.1 %copy-start.59 = (bf16[256,128]{1,0:T(8,128)(2,1)S(1)}, bf16[256,128]{1,0:T(8,128)(2,1)}, u32[]{:S(2)}) copy-start(bf16[256,128]{1,0:T(8,128)(2,1)} %param.36) | copy-start | bytes 196612
  998.0 161.5 %all-gather.29.cloned.1.call-start = ((), (), s32[]{:S(2)}) async-start(), calls=%async_computation.28 | async-start | bytes 5242880 | tf_op jit(solution)/shard_map/all_gather | solution.py:69
  1041.4 203.1 %reduce-scatter.35.cloned.1.call-start = ((), (), s32[]{:S(2)}) async-start(), calls=%async_computation.35 | async-start | bytes 5242880 | tf_op jit(solution)/shard_map/reduce_scatter | solution.py:73
  1159.4 159.5 %reduce-scatter.31.cloned.1.call-start = ((), (), s32[]{:S(2)}) async-start(), calls=%async_computation.29 | async-start | bytes 5242880 | tf_op jit(solution)/shard_map/reduce_scatter | solution.py:73
  1243.9 187.1 %copy-start.110 = (f32[1024]{0:T(1024)S(1)}, f32[1024]{0:T(1024)}, u32[]{:S(2)}) copy-start(f32[1024]{0:T(1024)} %param.41) | copy-start | bytes 12292
  1243.9 105.0 %all-gather.33.cloned.1.call-start = ((), (), s32[]{:S(2)}) async-start(), calls=%async_computation.31 | async-start | bytes 2359296 | tf_op jit(solution)/shard_map/all_gather | solution.py:50
  1244.5 186.5 %all-gather.39.cloned.1.call-start = ((), (), s32[]{:S(2)}) async-start(), calls=%async_computation.36 | async-start | bytes 5242880 | tf_op jit(solution)/shard_map/all_gather | solution.py:69
  1344.2 114.7 %all-gather.35.cloned.1.call-start = ((), (), s32[]{:S(2)}) async-start(), calls=%async_computation.32 | async-start | bytes 2359296 | tf_op jit(solution)/shard_map/all_gather | solution.py:54
  1344.8 200.4 %reduce-scatter.37.cloned.1.call-start = ((), (), s32[]{:S(2)}) async-start(), calls=%async_computation.37 | async-start | bytes 5242880 | tf_op jit(solution)/shard_map/reduce_scatter | solution.py:73
  1468.3 199.4 %all-gather.31.cloned.1.call-start = ((), (), s32[]{:S(2)}) async-start(), calls=%async_computation.30 | async-start | bytes 5242880 | tf_op jit(solution)/shard_map/all_gather | solution.py:69
  1585.8 357.1 %copy-start.60 = (f32[2048]{0:T(1024)}, f32[2048]{0:T(1024)S(1)}, u32[]{:S(2)}) copy-start(f32[2048]{0:T(1024)S(1)} %get-tuple-element.898) | copy-start | bytes 24580
  1585.8 357.1 %copy-start.62 = (f32[2048]{0:T(1024)}, f32[2048]{0:T(1024)S(1)}, u32[]{:S(2)}) copy-start(f32[2048]{0:T(1024)S(1)} %get-tuple-element.899) | copy-start | bytes 24580
  1587.4 160.8 %all-gather.41.cloned.1.call-start = ((), (), s32[]{:S(2)}) async-start(), calls=%async_computation.38 | async-start | bytes 5242880 | tf_op jit(solution)/shard_map/all_gather | solution.py:79
  1592.8 270.6 %reduce-scatter.39.cloned.1.call-start = ((), (), s32[]{:S(2)}) async-start(), calls=%async_computation.39 | async-start | bytes 5242880 | tf_op jit(solution)/shard_map/reduce_scatter | solution.py:83
  1788.3 154.7 %reduce-scatter.33.cloned.1.call-start = ((), (), s32[]{:S(2)}) async-start(), calls=%async_computation.33 | async-start | bytes 5242880 | tf_op jit(solution)/shard_map/reduce_scatter | solution.py:73
  1798.1 254.6 %all-gather.43.cloned.1.call-start = ((), (), s32[]{:S(2)}) async-start(), calls=%async_computation.40 | async-start | bytes 5242880 | tf_op jit(solution)/shard_map/all_gather | solution.py:79
  1973.8 372.1 %reduce-scatter.41.cloned.1.call-start = ((), (), s32[]{:S(2)}) async-start(), calls=%async_computation.41 | async-start | bytes 5242880 | tf_op jit(solution)/shard_map/reduce_scatter | solution.py:83
  2270.8 181.1 %copy-start.111 = (f32[1024]{0:T(1024)S(1)}, f32[1024]{0:T(1024)}, u32[]{:S(2)}) copy-start(f32[1024]{0:T(1024)} %param.41) | copy-start | bytes 12292
  2270.8 181.0 %all-gather.45.cloned.1.call-start = ((), (), s32[]{:S(2)}) async-start(), calls=%async_computation.42 | async-start | bytes 5242880 | tf_op jit(solution)/shard_map/all_gather | solution.py:79
  2372.8 177.1 %reduce-scatter.43.cloned.1.call-start = ((), (), s32[]{:S(2)}) async-start(), calls=%async_computation.43 | async-start | bytes 5242880 | tf_op jit(solution)/shard_map/reduce_scatter | solution.py:83
  2474.7 181.1 %all-gather.47.cloned.1.call-start = ((), (), s32[]{:S(2)}) async-start(), calls=%async_computation.44 | async-start | bytes 5242880 | tf_op jit(solution)/shard_map/all_gather | solution.py:79
  2576.8 330.0 %reduce-scatter.57.cloned.1.call-start = ((), (), s32[]{:S(2)}) async-start(), calls=%async_computation.51 | async-start | bytes 2359296
  2592.0 316.8 %reduce-scatter.53.cloned.1.call-start = ((), (), s32[]{:S(2)}) async-start(), calls=%async_computation.49 | async-start | bytes 2359296 | tf_op jit(solution)/shard_map/reduce_scatter | solution.py:376
  2605.9 329.7 %reduce-scatter.55.cloned.1.call-start = ((), (), s32[]{:S(2)}) async-start(), calls=%async_computation.50 | async-start | bytes 589824
  2660.7 276.5 %reduce-scatter.47.cloned.1.call-start = ((), (), s32[]{:S(2)}) async-start(), calls=%async_computation.46 | async-start | bytes 589824 | tf_op jit(solution)/shard_map/reduce_scatter | solution.py:367
  2874.9 70.0 %reduce-scatter.49.cloned.1.call-start = ((), (), s32[]{:S(2)}) async-start(), calls=%async_computation.47 | async-start | bytes 589824 | tf_op jit(solution)/shard_map/reduce_scatter | solution.py:370
  2887.0 95.2 %reduce-scatter.51.cloned.1.call-start = ((), (), s32[]{:S(2)}) async-start(), calls=%async_computation.48 | async-start | bytes 589824 | tf_op jit(solution)/shard_map/reduce_scatter | solution.py:373
  2896.7 164.6 %reduce-scatter.45.cloned.1.call-start = ((), (), s32[]{:S(2)}) async-start(), calls=%async_computation.45 | async-start | bytes 5242880 | tf_op jit(solution)/shard_map/reduce_scatter | solution.py:83
  (134 other events, 3904.5 us)
Sparse Core Ops, SparseCore 0:
  10.4 83.2 all-gather.16
  197.7 74.9 reduce-scatter.22
  503.1 78.9 all-gather.24
  691.7 74.9 reduce-scatter.26
  998.1 78.9 all-gather.36
  1078.6 78.7 all-gather.28
  1468.4 76.7 reduce-scatter.36
  1587.5 80.2 all-gather.30
  1669.4 78.7 all-gather.40
  1788.4 74.9 reduce-scatter.38
  1865.7 77.2 reduce-scatter.32
  2372.9 78.8 all-gather.44
  2576.9 78.9 all-gather.46
Sparse Core Ops, SparseCore 1:
  199.9 25.9 all-gather.20
  227.6 28.0 all-gather.22
  295.3 78.8 all-gather.18
  403.8 74.9 reduce-scatter.24
  789.2 78.7 all-gather.26
  897.5 74.9 reduce-scatter.28
  1159.5 75.0 reduce-scatter.34
  1243.9 75.0 reduce-scatter.30
  1320.7 28.1 all-gather.32
  1350.5 80.4 all-gather.38
  1432.7 26.2 all-gather.34
  1973.8 78.8 all-gather.42
  2270.9 74.9 reduce-scatter.40
  2474.8 75.0 reduce-scatter.42
  2592.1 39.5 reduce-scatter.56
  2634.9 41.1 reduce-scatter.52
  2679.5 34.1 reduce-scatter.54
  2875.0 32.5 reduce-scatter.46
  2910.8 34.1 reduce-scatter.48
  2948.0 34.1 reduce-scatter.50
  2984.5 76.7 reduce-scatter.44
where the time goes:
time: 3080 us; the launch traced here: 3070 us
  waiting for transfers between devices  1610 us (52%)
  matrix products  808 us (26%)
  blocking collectives  283 us (9%)
  other arithmetic  236 us (8%)
  local copies, waits for them, and re-layouts  61.7 us (2%)
  loops' own time  54.5 us (2%)
    reduce_scatter x8, waiting for transfers between devices, sum_partials(): lax.psum_scatter(partial_terms.astype(jnp.bfloat16), 'col', scatter_dimen...  528 us
    all_gather x8, waiting for transfers between devices, spread_features(): return lax.all_gather(rounded(values), 'col', axis=1, tiled=True)  474 us
    reduce_scatter x4, waiting for transfers between devices, sum_grad_partials(): lax.psum_scatter(partial_terms.astype(jnp.bfloat16), 'col', scatter_dimen...  293 us
    all_gather x4, waiting for transfers between devices, spread_grads(): return lax.all_gather(values, 'col', axis=1, tiled=True)  263 us
    dot_general x22, matrix products, matmul(): return jnp.dot(left, right, preferred_element_type=jnp.float32)  162 us
    psum x8, blocking collectives, norm_forward(): lax.psum((jnp.sum(summed, axis=1), jnp.sum(summed * summed, axis=1)), 'col')  142 us
    dot_general x16, matrix products, attend_one_block(): jnp.einsum('hqk,khd->qhd', rounded(weights / totals), seq_values, preferr...  111 us
    convert_element_type x17, other arithmetic, rounded(): return values.astype(jnp.bfloat16)  107 us
  transfers between devices with their start and end apart: 34, of which 26 were waited for; matrix products, arithmetic and copies ran while one was open for 16% of the time, Pallas kernels for 0%

commit v1 on v0

--- a/solution.py
+++ b/solution.py
@@ -1,17 +1,21 @@
+import functools
+
 import jax
 import jax.numpy as jnp
 from jax import lax
+from jax.experimental import pallas as pl
+from jax.experimental.pallas import tpu as pltpu
 from jax.sharding import PartitionSpec as P
 
+NEG_FILL = -1e30
+HEAD_DIM = 64
 D = 1024
-HEAD_DIM = 64
 LEN = 2048
 QBLOCK = 512
 SEQS = 1
 
 
 EPSILON = 1e-06
-NEG_FILL = -1e30
 
 
 def rounded(values):
@@ -309,7 +313,7 @@
     return (grad_input, row_terms, col_terms, small_terms)
 
 
-def per_device(
+def general_device(
     hidden_in,
     query_weight,
     key_weight,
@@ -345,17 +349,14 @@
     start_in = hidden_in.astype(jnp.float32)
     middle, kept_one = layer_forward(start_in, params, gathered, segment_ids)
     final_out, kept_two = layer_forward(middle, params, gathered, segment_ids)
-    inputs = (start_in, middle)
-    final_out, inputs, shards = lax.optimization_barrier((final_out, inputs, shards))
-    gathered = gather_weights(shards)
+    kept = (kept_one, kept_two)
     grad_flow = grad_out.astype(jnp.float32)
     row_parts = []
     col_parts = []
     small_parts = []
     for layer_index in (1, 0):
-        unused, kept_values = layer_forward(inputs[layer_index], params, gathered, segment_ids)
         grad_flow, row_terms, col_terms, small_terms = layer_backward(
-            grad_flow, kept_values, gathered, params, segment_ids
+            grad_flow, kept[layer_index], gathered, params, segment_ids
         )
         row_parts.append(row_terms)
         col_parts.append(col_terms)
@@ -420,6 +421,932 @@
     )
 
 
+ANY = pl.BlockSpec(memory_space=pl.ANY)
+VMEM = pl.BlockSpec(memory_space=pltpu.VMEM)
+MESH = pl.DeviceIdType.MESH
+DMA = pltpu.SemaphoreType.DMA
+BF16 = jnp.bfloat16
+F32 = jnp.float32
+
+
+def place():
+    row = lax.axis_index("row")
+    depth = lax.axis_index("col")
+    core = row % 2
+    chip = row // 2
+    x = chip % 2
+    y = chip // 2
+    return row, depth, core, chip, x, y
+
+
+def remote(src, dst, send_sem, recv_sem, row, depth):
+    return pltpu.make_async_remote_copy(
+        src_ref=src,
+        dst_ref=dst,
+        send_sem=send_sem,
+        recv_sem=recv_sem,
+        device_id={"row": row, "col": depth},
+        device_id_type=MESH,
+    )
+
+
+def span(start, size):
+    return pl.ds(pl.multiple_of(start, 128), size)
+
+
+def greet(row, depth, core, chip, x, y):
+    barrier = pltpu.get_barrier_semaphore()
+    mate = chip * 2 + (1 - core)
+    friends = [(mate, depth)]
+    for step in (1, 2, 3):
+        friends.append((row, (depth + step) % 4))
+        friends.append((mate, (depth + step) % 4))
+    friends.append(((y * 2 + 1 - x) * 2 + core, depth))
+    friends.append((((1 - y) * 2 + x) * 2 + core, depth))
+    for r, d in friends:
+        pl.semaphore_signal(
+            barrier, inc=1, device_id={"row": r, "col": d}, device_id_type=MESH
+        )
+    pl.semaphore_wait(barrier, len(friends))
+
+
+def gather_kernel(
+    q_ref, k_ref, v_ref, proj_ref, inner_ref, outer_ref, small_ref, x_ref, g_ref,
+    wqkv, wproj, winner, wouter, smalls, u_out, g_out,
+    swap_s, swap_r, local_s, z_s, z_r, sm_s, sm_r, p1_s, p1_r, p2_s, p2_r, t_s, t_r, t_l,
+):
+    row, depth, core, chip, x, y = place()
+    mate = chip * 2 + (1 - core)
+    x_chip = y * 2 + 1 - x
+    y_chip = (1 - y) * 2 + x
+    x_row = x_chip * 2 + core
+    y_row = y_chip * 2 + core
+    greet(row, depth, core, chip, x, y)
+
+    def swap_src(piece, half):
+        if piece < 3:
+            return (q_ref, k_ref, v_ref)[piece].at[:, span(half * 128, 128)]
+        if piece == 3:
+            return proj_ref.at[span(half * 128, 128), :]
+        if piece == 4:
+            return inner_ref.at[:, span(half * 512, 512)]
+        return outer_ref.at[span(half * 512, 512), :]
+
+    def swap_dst(piece, owner):
+        if piece < 3:
+            return wqkv.at[span(owner * 128, 128), span(piece * 512 + depth * 128, 128)]
+        if piece == 3:
+            return wproj.at[span(depth * 128, 128), span(owner * 128, 128)]
+        if piece == 4:
+            return winner.at[span(owner * 128, 128), span(depth * 512, 512)]
+        return wouter.at[span(depth * 512, 512), span(owner * 128, 128)]
+
+    def unit(piece):
+        if piece < 3:
+            return wqkv.at[span(chip * 256, 256), span(piece * 512 + depth * 128, 128)]
+        if piece == 3:
+            return wproj.at[span(depth * 128, 128), span(chip * 256, 256)]
+        if piece == 4:
+            return winner.at[span(chip * 256, 256), span(depth * 512, 512)]
+        return wouter.at[span(depth * 512, 512), span(chip * 256, 256)]
+
+    def region(group, part, block):
+        if group == 0:
+            return wqkv.at[span(block * 256 + part * 128, 128), :]
+        if group == 1:
+            return wproj.at[pl.ds(part * 256, 256), span(block * 256, 256)]
+        if group == 2:
+            return winner.at[span(block * 256 + part * 128, 128), :]
+        return wouter.at[pl.ds(part * 1024, 1024), span(block * 256, 256)]
+
+    waits = []
+    swaps, locals_ = [], []
+    for piece in range(6):
+        cp = remote(
+            swap_src(piece, 1 - core), swap_dst(piece, row),
+            swap_s.at[piece], swap_r.at[piece], mate, depth,
+        )
+        cp.start()
+        swaps.append(cp)
+        lc = pltpu.make_async_copy(swap_src(piece, core), swap_dst(piece, row), local_s.at[piece])
+        lc.start()
+        locals_.append(lc)
+    small_local = pltpu.make_async_copy(small_ref, smalls.at[depth], local_s.at[6])
+    small_local.start()
+
+    zs = {}
+
+    def start_z(pieces):
+        for piece in pieces:
+            swaps[piece].wait_recv()
+            locals_[piece].wait()
+            for k in (1, 2, 3):
+                cp = remote(
+                    unit(piece), unit(piece), z_s.at[piece, k - 1], z_r.at[piece, k - 1],
+                    row, (depth + k) % 4,
+                )
+                cp.start()
+                zs[piece, k] = cp
+
+    def token_copies(index, src, dst):
+        for j in range(4):
+            to_core, to_depth = j % 2, core * 2 + j // 2
+            mine = (to_core == core) & (to_depth == depth)
+            source = src.at[pl.ds(j * 512, 512), :]
+            target = dst.at[:, span(depth * 256, 256)]
+
+            @pl.when(mine)
+            def _():
+                pltpu.make_async_copy(source, target, t_l.at[index]).start()
+
+            @pl.when(jnp.logical_not(mine))
+            def _():
+                remote(
+                    source, target, t_s.at[index, j], t_r.at[index, depth],
+                    chip * 2 + to_core, to_depth,
+                ).start()
+
+    def token_waits(index, src, dst):
+        from_core = depth // 2
+        for s in range(4):
+            mine = (from_core == core) & (s == depth)
+            target = dst.at[:, pl.ds(s * 256, 256)]
+            source = src.at[pl.ds(0, 512), :]
+
+            @pl.when(mine)
+            def _():
+                pltpu.make_async_copy(source, target, t_l.at[index]).wait()
+
+            @pl.when(jnp.logical_not(mine))
+            def _():
+                remote(
+                    source, target, t_s.at[index, 0], t_r.at[index, s], mate, depth
+                ).wait_recv()
+        for j in range(4):
+            to_core, to_depth = j % 2, core * 2 + j // 2
+            mine = (to_core == core) & (to_depth == depth)
+
+            @pl.when(jnp.logical_not(mine))
+            def _():
+                remote(
+                    src.at[pl.ds(j * 512, 512), :], dst.at[:, pl.ds(0, 256)],
+                    t_s.at[index, j], t_r.at[index, 0], mate, depth,
+                ).wait_send()
+
+    start_z((0, 1, 2))
+    token_copies(0, x_ref, u_out)
+    start_z((3, 4, 5))
+    small_copies = []
+    for k in (1, 2, 3):
+        cp = remote(
+            small_ref, smalls.at[depth], sm_s.at[k - 1], sm_r.at[k - 1], row, (depth + k) % 4
+        )
+        cp.start()
+        small_copies.append(cp)
+    token_copies(1, g_ref, g_out)
+
+    first, second = {}, {}
+
+    def start_first(group):
+        for part, target in ((0, x_row), (1, y_row)):
+            cp = remote(
+                region(group, part, chip), region(group, part, chip),
+                p1_s.at[group, part], p1_r.at[group, part], target, depth,
+            )
+            cp.start()
+            first[group, part] = cp
+
+    def start_second(group):
+        for part, target, other in ((0, y_row, x_chip), (1, x_row, y_chip)):
+            first[group, part].wait_recv()
+            for i, block in enumerate((chip, other)):
+                cp = remote(
+                    region(group, part, block), region(group, part, block),
+                    p2_s.at[group, part, i], p2_r.at[group, part, i], target, depth,
+                )
+                cp.start()
+                second[group, part, i] = cp
+
+    members = ((0, 1, 2), (3,), (4,), (5,))
+    for group in range(4):
+        for piece in members[group]:
+            for k in (1, 2, 3):
+                zs[piece, k].wait_recv()
+        start_first(group)
+        if group > 0:
+            start_second(group - 1)
+    start_second(3)
+    token_waits(0, x_ref, u_out)
+    token_waits(1, g_ref, g_out)
+    for cp in small_copies:
+        cp.wait()
+    small_local.wait()
+    for cp in second.values():
+        cp.wait()
+    for cp in first.values():
+        cp.wait_send()
+    for cp in zs.values():
+        cp.wait_send()
+    for cp in swaps:
+        cp.wait_send()
+
+
+def gather_all(q, k, v, proj, inner, outer, small, x_rolled, g_rolled):
+    sd = jax.ShapeDtypeStruct
+    return pl.pallas_call(
+        gather_kernel,
+        out_shape=(
+            sd((1024, 1536), BF16),
+            sd((512, 1024), BF16),
+            sd((1024, 2048), BF16),
+            sd((2048, 1024), BF16),
+            sd((4,) + small.shape, F32),
+            sd((512, 1024), BF16),
+            sd((512, 1024), BF16),
+        ),
+        in_specs=[ANY] * 9,
+        out_specs=[ANY] * 7,
+        scratch_shapes=[
+            DMA((6,)), DMA((6,)), DMA((7,)), DMA((6, 3)), DMA((6, 3)), DMA((3,)), DMA((3,)),
+            DMA((4, 2)), DMA((4, 2)), DMA((4, 2, 2)), DMA((4, 2, 2)),
+            DMA((2, 4)), DMA((2, 4)), DMA((2,)),
+        ],
+        compiler_params=pltpu.CompilerParams(collective_id=1, has_side_effects=True),
+    )(q, k, v, proj, inner, outer, small, x_rolled, g_rolled)
+
+
+SHAPES = ((1024, 256), (128, 2048), (256, 256), (128, 512), (128, 512), (128, 512))
+UNITS = ((512, 256), (256, 512), (128, 256), (256, 128), (256, 128), (256, 128))
+FULLS = ((2048, 256), (256, 2048), (512, 256), (256, 512), (256, 512), (256, 512))
+OUTS = ((1024, 128), (128, 1024), (256, 128), (128, 256), (128, 256), (128, 256))
+HALVES = ((512, 128), (128, 512), (128, 128), (128, 128), (128, 128), (128, 128))
+BY_COLS = (True, False, True, False, False, False)
+
+
+def add_rows(dst, terms):
+    rows = dst.shape[0]
+    step = 32
+
+    def body(i, carry):
+        sl = pl.ds(pl.multiple_of(i * step, step), step)
+        total = terms[0][sl, :].astype(F32)
+        for term in terms[1:]:
+            total = total + term[sl, :].astype(F32)
+        dst[sl, :] = total.astype(dst.dtype)
+        return carry
+
+    lax.fori_loop(0, rows // step, body, 0)
+
+
+def scatter_kernel(*refs):
+    grads = refs[0:6]
+    small_ref, ho_ref, gi_ref = refs[6:9]
+    outs = refs[9:15]
+    small_out, ho_out, gi_out = refs[15:18]
+    rest = list(refs[18:])
+    own = [[rest.pop(0) for _ in range(2)] for _ in range(6)]
+    got1 = [[rest.pop(0) for _ in range(2)] for _ in range(6)]
+    got2 = [[rest.pop(0) for _ in range(2)] for _ in range(6)]
+    full = [rest.pop(0) for _ in range(6)]
+    zgot = [rest.pop(0) for _ in range(6)]
+    fin = [rest.pop(0) for _ in range(6)]
+    cgot = [rest.pop(0) for _ in range(6)]
+    sb = rest.pop(0)
+    sg = rest.pop(0)
+    (o_s, p1_s, p1_r, p2_s, p2_r, z_s, z_r, c_s, c_r, sm_s, sm_r, t_s, t_r, t_l) = rest
+
+    row, depth, core, chip, x, y = place()
+    mate = chip * 2 + (1 - core)
+    x_row = (y * 2 + 1 - x) * 2 + core
+    y_row = ((1 - y) * 2 + x) * 2 + core
+    greet(row, depth, core, chip, x, y)
+
+    def region(group, part, block):
+        rows = SHAPES[group][0]
+        if BY_COLS[group]:
+            return grads[group].at[pl.ds(part * rows, rows), span(block * 256, 256)]
+        return grads[group].at[span(block * 256 + part * 128, 128), :]
+
+    def unit(group, z):
+        if BY_COLS[group]:
+            return full[group].at[span(z * UNITS[group][0], UNITS[group][0]), :]
+        return full[group].at[:, span(z * UNITS[group][1], UNITS[group][1])]
+
+    def side(group, half):
+        if BY_COLS[group]:
+            return fin[group].at[:, span(half * 128, 128)]
+        return fin[group].at[span(half * 128, 128), :]
+
+    def out_side(group, half):
+        size = HALVES[group]
+        if BY_COLS[group]:
+            return outs[group].at[span(half * size[0], size[0]), :]
+        return outs[group].at[:, span(half * size[1], size[1])]
+
+    copies = {}
+
+    def start_first(group):
+        for part in (0, 1):
+            target = y_row if part == 0 else x_row
+            for i in (0, 1):
+                kept = y * 2 + i if part == 0 else i * 2 + x
+                sent = (1 - y) * 2 + i if part == 0 else i * 2 + (1 - x)
+                lc = pltpu.make_async_copy(
+                    region(group, part, kept), own[group][part].at[i], o_s.at[group, part, i]
+                )
+                lc.start()
+                cp = remote(
+                    region(group, part, sent), got1[group][part].at[i],
+                    p1_s.at[group, part, i], p1_r.at[group, part, i], target, depth,
+                )
+                cp.start()
+                copies["o", group, part, i] = lc
+                copies["p1", group, part, i] = cp
+
+    def start_second(group):
+        for part in (0, 1):
+            target = x_row if part == 0 else y_row
+            mine = x if part == 0 else y
+            for i in (0, 1):
+                copies["o", group, part, i].wait()
+                copies["p1", group, part, i].wait_recv()
+            other = own[group][part].at[1 - mine]
+            add_rows(other, (other, got1[group][part].at[1 - mine]))
+            cp = remote(
+                other, got2[group][part], p2_s.at[group, part], p2_r.at[group, part], target, depth
+            )
+            cp.start()
+            copies["p2", group, part] = cp
+
+    def start_depth(group):
+        rows = SHAPES[group][0]
+        for part in (0, 1):
+            mine = x if part == 0 else y
+            copies["p2", group, part].wait_recv()
+            add_rows(
+                full[group].at[pl.ds(part * rows, rows), :],
+                (own[group][part].at[mine], got1[group][part].at[mine], got2[group][part]),
+            )
+        for k in (1, 2, 3):
+            cp = remote(
+                unit(group, (depth + k) % 4), zgot[group].at[k - 1],
+                z_s.at[group, k - 1], z_r.at[group, k - 1], row, (depth + k) % 4,
+            )
+            cp.start()
+            copies["z", group, k] = cp
+
+    def start_core(group):
+        for k in (1, 2, 3):
+            copies["z", group, k].wait_recv()
+        add_rows(
+            fin[group],
+            (unit(group, depth), zgot[group].at[0], zgot[group].at[1], zgot[group].at[2]),
+        )
+        cp = remote(
+            side(group, 1 - core), cgot[group], c_s.at[group], c_r.at[group], mate, depth
+        )
+        cp.start()
+        copies["c", group] = cp
+
+    def finish(group):
+        add_rows(out_side(group, core), (side(group, core),))
+        copies["c", group].wait_recv()
+        add_rows(out_side(group, 1 - core), (cgot[group],))
+
+    def token_copies(index, src, dst):
+        j = (depth % 2) * 2 + core
+        to_core = depth // 2
+        for z in range(4):
+            mine = (to_core == core) & (z == depth)
+            source = src.at[:, pl.ds(z * 256, 256)]
+            target = dst.at[span(j * 512, 512), :]
+
+            @pl.when(mine)
+            def _():
+                pltpu.make_async_copy(source, target, t_l.at[index]).start()
+
+            @pl.when(jnp.logical_not(mine))
+            def _():
+                remote(
+                    source, target, t_s.at[index, z], t_r.at[index, j], chip * 2 + to_core, z
+                ).start()
+
+    def token_waits(index, src, dst):
+        to_core = depth // 2
+        j_own = (depth % 2) * 2 + core
+        for j in range(4):
+            from_core, from_depth = j % 2, core * 2 + j // 2
+            mine = (from_core == core) & (from_depth == depth)
+            target = dst.at[pl.ds(j * 512, 512), :]
+            source = src.at[:, pl.ds(0, 256)]
+
+            @pl.when(mine)
+            def _():
+                pltpu.make_async_copy(source, target, t_l.at[index]).wait()
+
+            @pl.when(jnp.logical_not(mine))
+            def _():
+                remote(
+                    source, target, t_s.at[index, 0], t_r.at[index, j], mate, depth
+                ).wait_recv()
+        for z in range(4):
+            mine = (to_core == core) & (z == depth)
+
+            @pl.when(jnp.logical_not(mine))
+            def _():
+                remote(
+                    src.at[:, pl.ds(z * 256, 256)], dst.at[pl.ds(0, 512), :],
+                    t_s.at[index, z], t_r.at[index, 0], mate, depth,
+                ).wait_send()
+
+    def small_send(step, slot, target_row, target_depth):
+        cp = remote(
+            sb.at[step], sg.at[slot], sm_s.at[slot], sm_r.at[slot], target_row, target_depth
+        )
+        cp.start()
+        copies["s", slot] = cp
+
+    def small_add(step, slot):
+        copies["s", slot].wait_recv()
+        sb[step + 1] = sb[step] + sg[slot]
+
+    sb[0] = small_ref[...]
+    small_send(0, 0, mate, depth)
+    start_first(0)
+    start_first(1)
+    token_copies(0, ho_ref, ho_out)
+    token_copies(1, gi_ref, gi_out)
+    small_add(0, 0)
+    small_send(1, 1, x_row, depth)
+    for group in range(6):
+        start_second(group)
+        if group + 2 < 6:
+            start_first(group + 2)
+        if group == 0:
+            small_add(1, 1)
+            small_send(2, 2, y_row, depth)
+        if group == 1:
+            small_add(2, 2)
+            for k in (1, 2, 3):
+                small_send(3, 2 + k, row, (depth + k) % 4)
+        if group > 0:
+            start_depth(group - 1)
+        if group > 1:
+            start_core(group - 2)
+    start_depth(5)
+    start_core(4)
+    for k in (1, 2, 3):
+        copies["s", 2 + k].wait_recv()
+    small_out[...] = ((sb[3] + sg[3]) + sg[4]) + sg[5]
+    for group in range(5):
+        finish(group)
+    token_waits(0, ho_ref, ho_out)
+    token_waits(1, gi_ref, gi_out)
+    start_core(5)
+    finish(5)
+    for key, cp in copies.items():
+        if key[0] != "o":
+            cp.wait_send()
+
+
+def scatter_all(outer, inner, proj, q, k, v, small, ho, gi):
+    sd = jax.ShapeDtypeStruct
+    scratch = []
+    for size in SHAPES:
+        scratch += [pltpu.VMEM((2,) + size, BF16)] * 2
+    for size in SHAPES:
+        scratch += [pltpu.VMEM((2,) + size, BF16)] * 2
+    for size in SHAPES:
+        scratch += [pltpu.VMEM(size, BF16)] * 2
+    scratch += [pltpu.VMEM(size, BF16) for size in FULLS]
+    scratch += [pltpu.VMEM((3,) + size, BF16) for size in UNITS]
+    scratch += [pltpu.VMEM(size, BF16) for size in UNITS]
+    scratch += [pltpu.VMEM(size, BF16) for size in HALVES]
+    scratch += [pltpu.VMEM((4,) + small.shape, F32), pltpu.VMEM((6,) + small.shape, F32)]
+    scratch += [
+        DMA((6, 2, 2)), DMA((6, 2, 2)), DMA((6, 2, 2)), DMA((6, 2)), DMA((6, 2)),
+        DMA((6, 3)), DMA((6, 3)), DMA((6,)), DMA((6,)), DMA((6,)), DMA((6,)),
+        DMA((2, 4)), DMA((2, 4)), DMA((2,)),
+    ]
+    return pl.pallas_call(
+        scatter_kernel,
+        out_shape=tuple(sd(size, F32) for size in OUTS)
+        + (sd(small.shape, F32), sd((2048, 256), BF16), sd((2048, 256), BF16)),
+        in_specs=[ANY] * 6 + [VMEM] + [ANY] * 2,
+        out_specs=[VMEM] * 7 + [ANY] * 2,
+        scratch_shapes=scratch,
+        compiler_params=pltpu.CompilerParams(
+            collective_id=2, has_side_effects=True, vmem_limit_bytes=56 * 1024 * 1024
+        ),
+    )(outer, inner, proj, q, k, v, small, ho, gi)
+
+
+def attend_kernel(flag_ref, q_ref, k_ref, v_ref, idq_ref, idk_ref, o_ref, lse_ref):
+    rows = q_ref.shape[0]
+    lane = lax.broadcasted_iota(jnp.int32, (1, 128), 1)
+    low_half = lane < HEAD_DIM
+
+    def compute(masked):
+        scaled = q_ref[...] * jnp.asarray(HEAD_DIM**-0.5, BF16)
+        keys = k_ref[...]
+        values = v_ref[...]
+        outs, logs = [], []
+        for head in (0, 1):
+            here = low_half if head == 0 else jnp.logical_not(low_half)
+            queries = jnp.where(here, scaled, jnp.zeros_like(scaled))
+            scores = against(queries, keys)
+            if masked:
+                scores = jnp.where(idq_ref[...] == idk_ref[...], scores, NEG_FILL)
+            top = jnp.max(scores, axis=1, keepdims=True)
+            weights = jnp.exp(scores - top)
+            total = jnp.sum(weights, axis=1, keepdims=True)
+            mixed = matmul(weights.astype(BF16), values)
+            outs.append(mixed / total)
+            logs.append(top + jnp.log(total))
+        o_ref[...] = jnp.where(low_half, outs[0], outs[1]).astype(o_ref.dtype)
+        lse_ref[...] = jnp.where(low_half, logs[0], logs[1])
+
+    @pl.when(flag_ref[0] == 1)
+    def _():
+        compute(False)
+
+    @pl.when(flag_ref[0] != 1)
+    def _():
+        compute(True)
+
+
+def attend(flag, qkv, id_col, id_row):
+    tokens, width = qkv.shape[0], qkv.shape[1] // 3
+    pairs = width // 128
+    block = 256
+    return pl.pallas_call(
+        attend_kernel,
+        out_shape=(
+            jax.ShapeDtypeStruct((tokens, width), BF16),
+            jax.ShapeDtypeStruct((tokens, width), F32),
+        ),
+        grid_spec=pltpu.PrefetchScalarGridSpec(
+            num_scalar_prefetch=1,
+            grid=(width // 128, tokens // block),
+            in_specs=[
+                pl.BlockSpec((block, 128), lambda h, i, f: (i, h)),
+                pl.BlockSpec((tokens, 128), lambda h, i, f: (0, h + pairs)),
+                pl.BlockSpec((tokens, 128), lambda h, i, f: (0, h + 2 * pairs)),
+                pl.BlockSpec((block, 1), lambda h, i, f: (i, 0)),
+                pl.BlockSpec((1, tokens), lambda h, i, f: (0, 0)),
+            ],
+            out_specs=[
+                pl.BlockSpec((block, 128), lambda h, i, f: (i, h)),
+                pl.BlockSpec((block, 128), lambda h, i, f: (i, h)),
+            ],
+        ),
+        compiler_params=pltpu.CompilerParams(
+            dimension_semantics=("arbitrary", "arbitrary"), vmem_limit_bytes=48 * 1024 * 1024
+        ),
+        name="attend",
+    )(flag, qkv, qkv, qkv, id_col, id_row)
+
+
+def attend_back_kernel(
+    flag_ref, q_ref, k_ref, v_ref, do_ref, lse_ref, idk_ref, idq_ref,
+    dq_ref, dk_ref, dv_ref, dk_acc, dv_acc,
+):
+    step = pl.program_id(1)
+    last = pl.num_programs(1) - 1
+    scale = HEAD_DIM**-0.5
+    lane = lax.broadcasted_iota(jnp.int32, (1, 128), 1)
+    low_half = lane < HEAD_DIM
+
+    @pl.when(step == 0)
+    def _():
+        dk_acc[...] = jnp.zeros_like(dk_acc)
+        dv_acc[...] = jnp.zeros_like(dv_acc)
+
+    def compute(masked):
+        queries = q_ref[...]
+        scaled = queries * jnp.asarray(scale, BF16)
+        keys = k_ref[...]
+        values = v_ref[...]
+        grads = do_ref[...]
+        lse_t = lse_ref[...].T
+        dqs, dks, dvs = [], [], []
+        for head in (0, 1):
+            here = low_half if head == 0 else jnp.logical_not(low_half)
+            zero = jnp.zeros_like(keys)
+            scores = against(jnp.where(here, keys, zero), scaled)
+            if masked:
+                scores = jnp.where(idk_ref[...] == idq_ref[...], scores, NEG_FILL)
+            log_row = lse_t[head * HEAD_DIM : head * HEAD_DIM + 1, :]
+            probs = jnp.exp(scores - log_row)
+            grad_probs = against(jnp.where(here, values, zero), grads)
+            moved = probs * grad_probs
+            delta = jnp.sum(moved, axis=0, keepdims=True)
+            grad_scores = (moved - probs * delta).astype(BF16)
+            dvs.append(matmul(probs.astype(BF16), grads))
+            dks.append(matmul(grad_scores, queries))
+            dqs.append(over_tokens(grad_scores, keys))
+        dq_ref[...] = (jnp.where(low_half, dqs[0], dqs[1]) * scale).astype(BF16)
+        dk_acc[...] += jnp.where(low_half, dks[0], dks[1]) * scale
+        dv_acc[...] += jnp.where(low_half, dvs[0], dvs[1])
+
+    @pl.when(flag_ref[0] == 1)
+    def _():
+        compute(False)
+
+    @pl.when(flag_ref[0] != 1)
+    def _():
+        compute(True)
+
+    @pl.when(step == last)
+    def _():
+        dk_ref[...] = dk_acc[...].astype(BF16)
+        dv_ref[...] = dv_acc[...].astype(BF16)
+
+
+def attend_back(flag, qkv, do, lse, id_col, id_row):
+    tokens, width = qkv.shape[0], qkv.shape[1] // 3
+    pairs = width // 128
+    block = 256
+    shape = jax.ShapeDtypeStruct((tokens, width), BF16)
+    rows = pl.BlockSpec((block, 128), lambda h, i, f: (i, h))
+    full = pl.BlockSpec((tokens, 128), lambda h, i, f: (0, h))
+    return pl.pallas_call(
+        attend_back_kernel,
+        out_shape=(shape, shape, shape),
+        grid_spec=pltpu.PrefetchScalarGridSpec(
+            num_scalar_prefetch=1,
+            grid=(width // 128, tokens // block),
+            in_specs=[
+                rows,
+                pl.BlockSpec((tokens, 128), lambda h, i, f: (0, h + pairs)),
+                pl.BlockSpec((tokens, 128), lambda h, i, f: (0, h + 2 * pairs)),
+                rows, rows,
+                pl.BlockSpec((tokens, 1), lambda h, i, f: (0, 0)),
+                pl.BlockSpec((1, block), lambda h, i, f: (0, i)),
+            ],
+            out_specs=[rows, full, full],
+            scratch_shapes=[pltpu.VMEM((tokens, 128), F32)] * 2,
+        ),
+        compiler_params=pltpu.CompilerParams(
+            dimension_semantics=("arbitrary", "arbitrary"), vmem_limit_bytes=48 * 1024 * 1024
+        ),
+        name="attend_back",
+    )(flag, qkv, qkv, qkv, do, lse, id_col, id_row)
+
+
+def ffn_in_kernel(x_ref, w_ref, b_ref, active_ref, slope_ref):
+    inner = matmul(x_ref[...], w_ref[...]) + b_ref[...]
+    size = jnp.abs(inner) * (0.5**0.5)
+    bell = jnp.exp(-0.5 * inner * inner)
+    t = 1.0 / (1.0 + 0.3275911 * size)
+    poly = 1.061405429 * t - 1.453152027
+    poly = poly * t + 1.421413741
+    poly = poly * t - 0.284496736
+    poly = poly * t + 0.254829592
+    tail = 0.5 * (poly * t) * bell
+    below = jnp.where(inner >= 0.0, 1.0 - tail, tail)
+    active_ref[...] = (inner * below).astype(BF16)
+    slope_ref[...] = (below + inner * bell * 0.3989422804014327).astype(BF16)
+
+
+def ffn_in(x, w, bias):
+    tokens, depth = x.shape
+    hidden = w.shape[1]
+    rows, cols = 256, 512
+    shape = jax.ShapeDtypeStruct((tokens, hidden), BF16)
+    out = pl.BlockSpec((rows, cols), lambda n, m: (m, n))
+    return pl.pallas_call(
+        ffn_in_kernel,
+        out_shape=(shape, shape),
+        grid=(hidden // cols, tokens // rows),
+        in_specs=[
+            pl.BlockSpec((rows, depth), lambda n, m: (m, 0)),
+            pl.BlockSpec((depth, cols), lambda n, m: (0, n)),
+            pl.BlockSpec((1, cols), lambda n, m: (0, n)),
+        ],
+        out_specs=[out, out],
+        compiler_params=pltpu.CompilerParams(
+            dimension_semantics=("arbitrary", "arbitrary"), vmem_limit_bytes=48 * 1024 * 1024
+        ),
+        name="ffn_in",
+    )(x, w, bias)
+
+
+def exchange(values):
+    pairs = [(r, r + 1 - 2 * (r % 2)) for r in range(8)]
+    return lax.ppermute(values, "row", pairs)
+
+
+def both(own):
+    return jnp.concatenate([own, exchange(own)], axis=0)
+
+
+def share_sum(left, weight, product):
+    mate_part = rounded(product(left[512:], weight))
+    other = exchange(mate_part)
+    return product(left[:512], weight) + other.astype(F32)
+
+
+def norm_rows(summed, gain, shift):
+    center = jnp.mean(summed, axis=1, keepdims=True)
+    spread = jnp.mean(summed * summed, axis=1, keepdims=True) - center * center
+    inverse = lax.rsqrt(spread + EPSILON)
+    normed = (summed - center) * inverse
+    return normed * gain + shift, normed, inverse
+
+
+def norm_rows_back(grad_output, normed, inverse, gain):
+    scaled = grad_output * gain
+    mean_one = jnp.mean(scaled, axis=1, keepdims=True)
+    mean_two = jnp.mean(scaled * normed, axis=1, keepdims=True)
+    grad_input = inverse * (scaled - mean_one - normed * mean_two)
+    return grad_input, token_sum(grad_output * normed), token_sum(grad_output)
+
+
+def fast_forward(hidden, weights, vectors, ids):
+    wqkv, wproj, winner, wouter = weights
+    flag, id_col, id_row = ids
+    whole_in = both(rounded(hidden))
+    qkv = rounded(matmul(whole_in, wqkv) + vectors["qkv"])
+    attended, lse = attend(flag, qkv, id_col, id_row)
+    branch = share_sum(attended, wproj, matmul) + vectors["proj"]
+    first, normed_one, inverse_one = norm_rows(
+        hidden + branch, vectors["attn_gain"], vectors["attn_shift"]
+    )
+    whole_mid = both(rounded(first))
+    active, slope = ffn_in(whole_mid, winner, vectors["inner"])
+    ffn = share_sum(active, wouter, matmul) + vectors["outer"]
+    output, normed_two, inverse_two = norm_rows(
+        first + ffn, vectors["ffn_gain"], vectors["ffn_shift"]
+    )
+    kept = (
+        whole_in, qkv, lse, attended, normed_one, inverse_one,
+        whole_mid, active, slope, normed_two, inverse_two,
+    )
+    return output, kept
+
+
+def fast_backward(grad_output, kept, weights, vectors, ids):
+    (
+        whole_in, qkv, lse, attended, normed_one, inverse_one,
+        whole_mid, active, slope, normed_two, inverse_two,
+    ) = kept
+    wqkv, wproj, winner, wouter = weights
+    flag, id_col, id_row = ids
+    grad_second, ffn_gain_sum, ffn_shift_sum = norm_rows_back(
+        grad_output, normed_two, inverse_two, vectors["ffn_gain"]
+    )
+    ffn_low = rounded(grad_second)
+    whole_second = both(ffn_low)
+    inner_low = rounded(against(whole_second, wouter) * slope.astype(F32))
+    outer_term = over_tokens(active, whole_second)
+    grad_first = grad_second + share_sum(inner_low, winner, against)
+    inner_term = over_tokens(whole_mid, inner_low)
+    grad_attn, attn_gain_sum, attn_shift_sum = norm_rows_back(
+        grad_first, normed_one, inverse_one, vectors["attn_gain"]
+    )
+    attn_low = rounded(grad_attn)
+    whole_attn = both(attn_low)
+    mixed_grad = rounded(against(whole_attn, wproj))
+    proj_term = over_tokens(attended, whole_attn)
+    grads = attend_back(flag, qkv, mixed_grad, lse, id_col, id_row)
+    grad_qkv = jnp.concatenate(grads, axis=1)
+    grad_input = grad_attn + share_sum(grad_qkv, wqkv, against)
+    terms = (outer_term, inner_term, proj_term) + tuple(
+        over_tokens(whole_in, part) for part in grads
+    )
+    small = (
+        token_sum(grads[0]), token_sum(grads[2]), token_sum(attn_low),
+        attn_gain_sum, attn_shift_sum, token_sum(inner_low), token_sum(ffn_low),
+        ffn_gain_sum, ffn_shift_sum,
+    )
+    return grad_input, terms, small
+
+
+VECTORS = (
+    ("q", 256), ("v", 256), ("proj", 256), ("attn_gain", 256), ("attn_shift", 256),
+    ("inner", 1024), ("outer", 256), ("ffn_gain", 256), ("ffn_shift", 256),
+)
+SPLIT = ("q", "v", "inner")
+
+
+def fast_device(
+    hidden_in,
+    query_weight,
+    key_weight,
+    value_weight,
+    query_bias,
+    value_bias,
+    proj_weight,
+    proj_bias,
+    attn_gain,
+    attn_shift,
+    inner_weight,
+    inner_bias,
+    outer_weight,
+    outer_bias,
+    ffn_gain,
+    ffn_shift,
+    segment_ids,
+    grad_out,
+):
+    core = lax.axis_index("row") % 2
+    depth = lax.axis_index("col")
+    own_ids = segment_ids[0]
+    mate_ids = exchange(own_ids)
+
+    def big_start(ids):
+        found = ids[:1025] == ids[1023:]
+        return jnp.sum(jnp.where(found, jnp.arange(1025, dtype=jnp.int32), 0))
+
+    own_start = big_start(own_ids)
+    ids = jnp.where(depth // 2 == core, own_ids, mate_ids)
+    ids = lax.dynamic_slice(
+        jnp.concatenate([ids, ids[:1024]]), (big_start(ids),), (2048,)
+    ).reshape(2, 2, 512)
+    ids = lax.dynamic_index_in_dim(ids, depth % 2, 0, keepdims=False)
+    ids = jnp.where(core == 0, ids, ids[::-1]).reshape(1024)
+    flag = (1 - depth % 2).reshape(1).astype(jnp.int32)
+    ids = (flag, ids[:, None], ids[None, :])
+
+    def turned(values):
+        longer = jnp.concatenate([values, values[:1024]], axis=0)
+        return lax.dynamic_slice(longer, (own_start, 0), (2048, 256))
+
+    def turned_back(values):
+        longer = jnp.concatenate([values[1024:], values], axis=0)
+        return lax.dynamic_slice(longer, (1024 - own_start, 0), (2048, 256)).astype(F32)
+
+    small = jnp.concatenate(
+        [
+            query_bias, value_bias, proj_bias, attn_gain, attn_shift,
+            inner_bias, outer_bias, ffn_gain, ffn_shift,
+        ]
+    ).reshape(24, 128)
+    wqkv, wproj, winner, wouter, smalls, start_low, grad_low = gather_all(
+        query_weight, key_weight, value_weight, proj_weight, inner_weight, outer_weight,
+        small, turned(hidden_in), turned(grad_out),
+    )
+    weights = (wqkv, wproj, winner, wouter)
+    smalls = smalls.reshape(4, 3072)
+    vectors, offset = {}, 0
+    for name, size in VECTORS:
+        part = smalls[:, offset : offset + size]
+        offset += size
+        if name in SPLIT:
+            part = jnp.where(core == 0, part[:, : size // 2], part[:, size // 2 :])
+        vectors[name] = part.reshape(1, -1)
+    vectors["qkv"] = jnp.concatenate(
+        [vectors["q"], jnp.zeros_like(vectors["q"]), vectors["v"]], axis=1
+    )
+
+    middle, kept_one = fast_forward(start_low.astype(F32), weights, vectors, ids)
+    final_out, kept_two = fast_forward(middle, weights, vectors, ids)
+    grad_flow = grad_low.astype(F32)
+    grad_flow, terms_two, small_two = fast_backward(grad_flow, kept_two, weights, vectors, ids)
+    grad_flow, terms_one, small_one = fast_backward(grad_flow, kept_one, weights, vectors, ids)
+    terms = [rounded(a + b) for a, b in zip(terms_two, terms_one)]
+    pieces = []
+    for (name, size), a, b in zip(VECTORS, small_two, small_one):
+        total = a + b
+        if name in SPLIT:
+            half = total.reshape(4, 1, size // 2)
+            zero = jnp.zeros_like(half)
+            total = jnp.where(
+                core == 0,
+                jnp.concatenate([half, zero], axis=1),
+                jnp.concatenate([zero, half], axis=1),
+            )
+        pieces.append(total.reshape(-1))
+    small_sum = jnp.concatenate(pieces).reshape(96, 128)
+    results = scatter_all(*terms, small_sum, rounded(final_out), rounded(grad_flow))
+    outer_g, inner_g, proj_g, q_g, k_g, v_g, small_all, out_turned, grad_turned = results
+    small_all = small_all.reshape(-1)
+    sums, offset = {}, 0
+    for name, size in VECTORS:
+        sums[name] = lax.dynamic_slice(small_all, (offset + depth * size,), (size,))
+        offset += 4 * size
+    return (
+        turned_back(out_turned),
+        turned_back(grad_turned),
+        q_g,
+        k_g,
+        v_g,
+        sums["q"],
+        sums["v"],
+        proj_g,
+        sums["proj"],
+        sums["attn_gain"],
+        sums["attn_shift"],
+        inner_g,
+        sums["inner"],
+        outer_g,
+        sums["outer"],
+        sums["ffn_gain"],
+        sums["ffn_shift"],
+    )
+
+
 def solution(mesh):
     in_specs = (
         P("row", "col"),
@@ -460,6 +1387,7 @@
         P("col"),
         P("col"),
     )
+    same = dict(mesh.shape) == {"row": 8, "col": 4}
     return jax.shard_map(
-        per_device, mesh=mesh, in_specs=in_specs, out_specs=out_specs, check_vma=False
-    )
+        fast_device if same else general_device, mesh=mesh, in_specs=in_specs, out_specs=out_specs, check_vma=False
+    )

time: 3080 us -> 691 us (0.22)
  waiting for transfers between devices: 1610 us -> 26.1 us
  matrix products: 808 us -> 123 us
  Pallas kernels: 0 us -> 474 us
  blocking collectives: 283 us -> 0 us
  other arithmetic: 236 us -> 23.5 us
  loops' own time: 54.5 us -> 0 us
  local copies, waits for them, and re-layouts: 61.7 us -> 23.8 us
    reduce_scatter x16 -> x0, waiting for transfers between devices: 863 us -> none  [the longest x8 528 us: sum_partials(): lax.psum_scatter(partial_terms.astype(jnp.bfloat16), 'col', scatter_dimen...]
    all_gather x16 -> x0, waiting for transfers between devices: 743 us -> none  [the longest x8 474 us: spread_features(): return lax.all_gather(rounded(values), 'col', axis=1, tiled=True)]
    pallas_call x0 -> x8, Pallas kernels: none -> 474 us  [the longest x1 168 us: scatter_all(): pl.pallas_call(scatter_kernel, out_shape=tuple((sd(size, F32) for size in...]
    dot_general x64 -> x0, matrix products: 411 us -> none  [the longest x16 111 us: attend_one_block(): jnp.einsum('hqk,khd->qhd', rounded(weights / totals), seq_values, preferr...]
    psum x11 -> x0, blocking collectives: 203 us -> none  [the longest x8 142 us: norm_forward(): lax.psum((jnp.sum(summed, axis=1), jnp.sum(summed * summed, axis=1)), 'col')]
    dot_general x22 -> x10, matrix products: 162 us -> 32.4 us  [matmul(): return jnp.dot(left, right, preferred_element_type=jnp.float32)]
    convert_element_type x17 -> x3, other arithmetic: 107 us -> 1.21 us  [rounded(): return values.astype(jnp.bfloat16)]
    sub x8 -> x0, matrix products: 84.1 us -> none  [attend_one_block(): weights = jnp.exp(scores - highest)]
  transfers between devices with their start and end apart: 34 -> 17, of which waited for: 26 -> 12; matrix products, arithmetic and copies ran while one was open for 16% -> 9% of each run, Pallas kernels for 0% -> 23%
where the time goes in v1:
time: 691 us; the launch traced here: 685 us
  Pallas kernels  474 us (69%)
  matrix products  123 us (18%)
  waiting for transfers between devices  26.1 us (4%)
  local copies, waits for them, and re-layouts  23.8 us (3%)
  other arithmetic  23.5 us (3%)
  between operations  7.59 us (1%)
    pallas_call x1, Pallas kernels, scatter_all(): pl.pallas_call(scatter_kernel, out_shape=tuple((sd(size, F32) for size in...  168 us
    pallas_call x1, Pallas kernels, gather_all(): pl.pallas_call(gather_kernel, out_shape=(sd((1024, 1536), BF16), sd((512,...  160 us
    pallas_call x2, Pallas kernels, attend_back(): pl.pallas_call(attend_back_kernel, out_shape=(shape, shape, shape), grid_...  69.9 us
    dot_general x12, matrix products, over_tokens(): lax.dot_general(left, right, (((0,), (0,)), ((), ())), preferred_element_...  47.4 us
    dot_general x12, matrix products, against(): lax.dot_general(left, right, (((1,), (1,)), ((), ())), preferred_element_...  43.2 us
    pallas_call x2, Pallas kernels, attend(): pl.pallas_call(attend_kernel, out_shape=(jax.ShapeDtypeStruct((tokens, wi...  40.5 us
    pallas_call x2, Pallas kernels, ffn_in(): pl.pallas_call(ffn_in_kernel, out_shape=(shape, shape), grid=(hidden // c...  36.4 us
    dot_general x10, matrix products, matmul(): return jnp.dot(left, right, preferred_element_type=jnp.float32)  32.4 us
  transfers between devices with their start and end apart: 17, of which 12 were waited for; matrix products, arithmetic and copies ran while one was open for 9% of the time, Pallas kernels for 23%

profile of v1, /device:TPU:0, one launch (start us, length us, event | category | flops | bytes accessed | tf_op | source)
XLA Modules:
  0.0 684.8 jit_solution(10735718543479578223)
XLA Ops:
  4.9 3.4 fusion.66.g_ref
  8.3 3.4 fusion.67.x_ref
  12.5 159.6 %shard_map.305 = (bf16[1024,1536]{1,0:T(8,128)(2,1)}, bf16[512,1024]{1,0:T(8,128)(2,1)}, bf16[1024,2048]{1,0:T(8,128)(2,1)}, bf16[2048,1024]{1,0:T(8,128)(2,1)},...) custom-call(bf16[128,256]{1,0:T(8,128)(2,1)} %q_ref.1, bf16[128,256]{1,0:T(8,128)(2,1)} %k_ref.1, ...), custom_call_target="tpu_custom_call" | custom-call | tf_op jit(solution)/shard_map/pallas_call | solution.py:656
  173.1 2.3 constant_dynamic-update-slice_fusion.2
  179.8 7.6 %add_convert_fusion.3.q_ref.k_ref.v_ref = bf16[1024,1536]{1,0:T(8,128)(2,1)} fusion(bf16[1024,1024]{1,0:T(8,128)(2,1)} %constant_dynamic-update-slice_fusion.1, bf16[1024,1536]{1,0:T(8,128)(2,1)} %get-tuple-element.48, f32[1536]{0:T(1024)S(1)} %fusion.81), kind=kOutput, calls=%fused_computation.7 | convolution fusion | flops 3224371200 | bytes 8394752 | tf_op jit(solution)/shard_map/dot_general | solution.py:26
  187.4 20.3 %attend.2 = (bf16[1024,512]{1,0:T(8,128)(2,1)S(1)}, f32[1024,512]{1,0:T(8,128)S(1)}) custom-call(s32[1]{0:T(128)} %bitcast.1.flag_ref, bf16[1024,1536]{1,0:T(8,128)(2,1)} %add_convert_fusion.3.q_ref.k_ref.v_ref, bf16[1024,1536]{1,0:T(8,128)(2,1)} %add_convert_fusion.3.q_ref.k_ref.v_ref, bf16[1024,1536]{1,0:T(8,128)(2,1)} %add_convert_fusion.3.q_ref.k_ref.v_ref, ...), custom_call_target="tpu_custom_call" | custom-call | tf_op jit(solution)/shard_map/attend/pallas_call | solution.py:982
  209.0 2.3 collective-permute-done.2
  213.4 2.3 collective-permute-done.3
  216.7 18.2 %ffn_in.2 = (bf16[1024,2048]{1,0:T(8,128)(2,1)}, bf16[1024,2048]{1,0:T(8,128)(2,1)}) custom-call(bf16[1024,1024]{1,0:T(8,128)(2,1)S(1)} %pad_maximum_fusion.x_ref, bf16[1024,2048]{1,0:T(8,128)(2,1)} %get-tuple-element.52.w_ref, f32[1,2048]{1,0:T(1,128)S(1)} %bitcast.100), custom_call_target="tpu_custom_call" | custom-call | tf_op jit(solution)/shard_map/ffn_in/pallas_call | solution.py:1118
  234.9 4.1 fusion.40
  239.4 2.3 collective-permute-done.4
  241.7 3.0 fusion.93
  245.6 2.3 collective-permute-done.5
  247.9 5.6 add_convert_fusion.2.q_ref.k_ref.v_ref
  253.5 20.2 %attend.3 = (bf16[1024,512]{1,0:T(8,128)(2,1)S(1)}, f32[1024,512]{1,0:T(8,128)S(1)}) custom-call(s32[1]{0:T(128)} %bitcast.1.flag_ref, bf16[1024,1536]{1,0:T(8,128)(2,1)} %add_convert_fusion.2.q_ref.k_ref.v_ref, bf16[1024,1536]{1,0:T(8,128)(2,1)} %add_convert_fusion.2.q_ref.k_ref.v_ref, bf16[1024,1536]{1,0:T(8,128)(2,1)} %add_convert_fusion.2.q_ref.k_ref.v_ref, ...), custom_call_target="tpu_custom_call" | custom-call | tf_op jit(solution)/shard_map/attend/pallas_call | solution.py:982
  274.9 2.3 collective-permute-done.6
  279.3 2.3 collective-permute-done.7
  282.7 18.2 %ffn_in.3 = (bf16[1024,2048]{1,0:T(8,128)(2,1)}, bf16[1024,2048]{1,0:T(8,128)(2,1)}) custom-call(bf16[1024,1024]{1,0:T(8,128)(2,1)S(1)} %pad_maximum_fusion.2.x_ref, bf16[1024,2048]{1,0:T(8,128)(2,1)} %get-tuple-element.52.w_ref, f32[1,2048]{1,0:T(1,128)S(1)} %bitcast.101), custom_call_target="tpu_custom_call" | custom-call | tf_op jit(solution)/shard_map/ffn_in/pallas_call | solution.py:1118
  300.9 5.3 fusion.43
  306.7 2.3 collective-permute-done.8
  309.0 3.0 multiply_reduce_fusion.6
  311.9 2.2 fusion.6
  315.3 2.3 collective-permute-done.9
  317.6 10.3 %convert_reduce_fusion.1 = (f32[2048]{0:T(1024)S(1)}, bf16[1024,2048]{1,0:T(8,128)(2,1)}) fusion(bf16[1024,2048]{1,0:T(8,128)(2,1)} %get-tuple-element.58, bf16[2048,1024]{1,0:T(8,128)(2,1)} %get-tuple-element.54, bf16[512,1024]{1,0:T(8,128)(2,1)S(1)} %collective-permute-done.9, bf16[512,1024]{1,0:T(8,128)(2,1)S(1)} %get-tuple-element.105), kind=kOutput, calls=%fused_computation.1 | convolution fusion | flops 4309645312 | bytes 14688256 | tf_op jit(solution)/shard_map/dot_general | solution.py:36
  328.0 4.2 fusion.46
  332.7 2.3 collective-permute-done.10
  335.0 3.5 multiply_reduce_fusion.2
  339.7 2.3 collective-permute-done.11
  343.3 35.0 %attend_back.2 = (bf16[1024,512]{1,0:T(8,128)(2,1)S(1)}, bf16[1024,512]{1,0:T(8,128)(2,1)S(1)}, bf16[1024,512]{1,0:T(8,128)(2,1)S(1)}) custom-call(s32[1]{0:T(128)} %bitcast.1.flag_ref, bf16[1024,1536]{1,0:T(8,128)(2,1)} %add_convert_fusion.2.q_ref.k_ref.v_ref, bf16[1024,1536]{1,0:T(8,128)(2,1)} %add_convert_fusion.2.q_ref.k_ref.v_ref, ...), custom_call_target="tpu_custom_call" | custom-call | tf_op jit(solution)/shard_map/attend_back/pallas_call | solution.py:1073
  380.6 1.8 fusion.34
  382.8 2.3 collective-permute-done.12
  385.1 2.6 multiply_reduce_fusion
  387.8 2.4 convert_reduce_fusion.3
  393.1 8.7 %convert_reduce_fusion = (f32[2048]{0:T(1024)S(1)}, bf16[1024,2048]{1,0:T(8,128)(2,1)S(1)}) fusion(bf16[1024,2048]{1,0:T(8,128)(2,1)} %get-tuple-element.63, bf16[2048,1024]{1,0:T(8,128)(2,1)} %get-tuple-element.54, bf16[512,1024]{1,0:T(8,128)(2,1)} %collective-permute-done.13, bf16[512,1024]{1,0:T(8,128)(2,1)} %get-tuple-element.102), kind=kOutput, calls=%fused_computation | convolution fusion | flops 4309645312 | bytes 14688256 | tf_op jit(solution)/shard_map/dot_general | solution.py:36
  401.9 2.4 fusion.49
  404.8 7.3 %fusion.90 = f32[1024,2048]{1,0:T(8,128)} fusion(bf16[1024,2048]{1,0:T(8,128)(2,1)S(1)} %get-tuple-element.147, bf16[512,1024]{1,0:T(8,128)(2,1)S(1)} %copy-done.28, bf16[512,1024]{1,0:T(8,128)(2,1)S(1)} %copy-done.16), kind=kOutput, calls=%fused_computation.205 | convolution fusion | flops 4299161600 | bytes 14680064 | tf_op jit(solution)/shard_map/dot_general | solution.py:30
  412.1 8.5 %add_convert_fusion.refs_1_ = bf16[1024,2048]{1,0:T(8,128)(2,1)} fusion(f32[1024,2048]{1,0:T(8,128)} %fusion.90, bf16[1024,2048]{1,0:T(8,128)(2,1)S(1)} %copy-done.72, bf16[512,1024]{1,0:T(8,128)(2,1)S(1)} %copy-done.34, bf16[512,1024]{1,0:T(8,128)(2,1)S(1)} %copy-done.18), kind=kOutput, calls=%fused_computation.2 | convolution fusion | flops 4303355904 | bytes 18874368 | tf_op jit(solution)/shard_map/dot_general | solution.py:30
  420.6 2.4 fusion.9
  423.1 8.6 %fusion.55 = f32[2048,1024]{1,0:T(8,128)} fusion(bf16[1024,2048]{1,0:T(8,128)(2,1)S(1)} %copy-done.58, bf16[512,1024]{1,0:T(8,128)(2,1)} %collective-permute-done.13, bf16[512,1024]{1,0:T(8,128)(2,1)} %get-tuple-element.102), kind=kOutput, calls=%fused_computation.115 | convolution fusion | flops 4299161600 | bytes 14680064 | tf_op jit(solution)/shard_map/dot_general | solution.py:30
  435.9 8.8 %add_convert_fusion.1.refs_0_ = bf16[2048,1024]{1,0:T(8,128)(2,1)} fusion(f32[2048,1024]{1,0:T(8,128)} %fusion.55, bf16[1024,2048]{1,0:T(8,128)(2,1)S(1)} %copy-done.60, bf16[512,1024]{1,0:T(8,128)(2,1)S(1)} %copy-done.70, bf16[512,1024]{1,0:T(8,128)(2,1)S(1)} %copy-done.32), kind=kOutput, calls=%fused_computation.4 | convolution fusion | flops 4303355904 | bytes 18874368 | tf_op jit(solution)/shard_map/dot_general | solution.py:30
  446.0 35.0 %attend_back.3 = (bf16[1024,512]{1,0:T(8,128)(2,1)S(1)}, bf16[1024,512]{1,0:T(8,128)(2,1)S(1)}, bf16[1024,512]{1,0:T(8,128)(2,1)S(1)}) custom-call(s32[1]{0:T(128)} %bitcast.1.flag_ref, bf16[1024,1536]{1,0:T(8,128)(2,1)} %add_convert_fusion.3.q_ref.k_ref.v_ref, bf16[1024,1536]{1,0:T(8,128)(2,1)} %add_convert_fusion.3.q_ref.k_ref.v_ref, ...), custom_call_target="tpu_custom_call" | custom-call | tf_op jit(solution)/shard_map/attend_back/pallas_call | solution.py:1073
  492.0 2.3 add_convert_fusion.6.refs_5_
  494.3 2.2 add_convert_fusion.9.refs_2_
  496.6 2.3 add_convert_fusion.7.refs_4_
  498.8 2.3 add_convert_fusion.8.refs_3_
  501.1 2.8 add_convert_fusion.4.refs_8_
  503.9 167.7 %shard_map.306 = (f32[1024,128]{1,0:T(8,128)}, f32[128,1024]{1,0:T(8,128)}, f32[256,128]{1,0:T(8,128)}, f32[128,256]{1,0:T(8,128)}, f32[128,256]{1,0:T(8,128)}, ...) custom-call(bf16[2048,1024]{1,0:T(8,128)(2,1)} %add_convert_fusion.1.refs_0_, ...), custom_call_target="tpu_custom_call" | custom-call | tf_op jit(solution)/shard_map/pallas_call | solution.py:931
  675.3 3.6 fusion.63
  (278 shorter events, 51.1 us)
Async XLA Ops:
  0.7 174.7 %collective-permute-start.1 = (s32[2048]{0:T(1024)}, s32[2048]{0:T(1024)S(1)}, u32[]{:S(2)}, u32[]{:S(2)}) collective-permute-start(s32[2048]{0:T(1024)} %bitcast.123), channel_id=1, source_target_pairs={{0,4},{4,0},{8,12},{12,8},{16,20},{20,16},{24,28},{28,24},{1,5},{5... | collective-permute-start | bytes 24584 | tf_op jit(solution)/shard_map/ppermute | solution.py:1137
  4.8 6.9 %copy-start.46 = (f32[256]{0:T(256)S(1)}, f32[256]{0:T(256)}, u32[]{:S(2)}) copy-start(f32[256]{0:T(256)} %param.22) | copy-start | bytes 3076
  4.8 6.9 %copy-start.47 = (f32[256]{0:T(256)S(1)}, f32[256]{0:T(256)}, u32[]{:S(2)}) copy-start(f32[256]{0:T(256)} %param.23) | copy-start | bytes 3076
  4.8 6.9 %copy-start.48 = (f32[256]{0:T(256)S(1)}, f32[256]{0:T(256)}, u32[]{:S(2)}) copy-start(f32[256]{0:T(256)} %param.25) | copy-start | bytes 3076
  4.8 7.0 %copy-start.49 = (f32[256]{0:T(256)S(1)}, f32[256]{0:T(256)}, u32[]{:S(2)}) copy-start(f32[256]{0:T(256)} %param.26) | copy-start | bytes 3076
  4.8 7.0 %copy-start.50 = (f32[256]{0:T(256)S(1)}, f32[256]{0:T(256)}, u32[]{:S(2)}) copy-start(f32[256]{0:T(256)} %param.27) | copy-start | bytes 3076
  4.9 7.0 %copy-start.45 = (f32[1024]{0:T(1024)S(1)}, f32[1024]{0:T(1024)}, u32[]{:S(2)}) copy-start(f32[1024]{0:T(1024)} %param.29) | copy-start | bytes 12292
  4.9 7.0 %copy-start.51 = (f32[256]{0:T(256)S(1)}, f32[256]{0:T(256)}, u32[]{:S(2)}) copy-start(f32[256]{0:T(256)} %param.31) | copy-start | bytes 3076
  4.9 7.0 %copy-start.52 = (f32[256]{0:T(256)S(1)}, f32[256]{0:T(256)}, u32[]{:S(2)}) copy-start(f32[256]{0:T(256)} %param.32) | copy-start | bytes 3076
  4.9 7.0 %copy-start.53 = (f32[256]{0:T(256)S(1)}, f32[256]{0:T(256)}, u32[]{:S(2)}) copy-start(f32[256]{0:T(256)} %param.33) | copy-start | bytes 3076
  12.5 162.9 %copy-start.43 = (s32[1,2048]{1,0:T(1,128)S(1)}, s32[1,2048]{1,0:T(1,128)}, u32[]{:S(2)}) copy-start(s32[1,2048]{1,0:T(1,128)} %param.34) | copy-start | bytes 24580
  172.1 6.6 collective-permute-start
  187.4 20.3 %copy-start.64 = (bf16[512,1024]{1,0:T(8,128)(2,1)S(1)}, bf16[512,1024]{1,0:T(8,128)(2,1)}, u32[]{:S(2)}) copy-start(bf16[512,1024]{1,0:T(8,128)(2,1)} %get-tuple-element.51) | copy-start | bytes 3145732
  208.5 2.8 collective-permute-start.2
  212.5 29.2 %copy-start.8 = (f32[512,1024]{1,0:T(8,128)}, f32[512,1024]{1,0:T(8,128)S(1)}, u32[]{:S(2)}) copy-start(f32[512,1024]{1,0:T(8,128)S(1)} %get-tuple-element.139) | copy-start | bytes 6291460
  212.9 2.7 collective-permute-start.3
  216.7 18.2 %copy-start.54 = (bf16[2048,1024]{1,0:T(8,128)(2,1)S(1)}, bf16[2048,1024]{1,0:T(8,128)(2,1)}, u32[]{:S(2)}) copy-start(bf16[2048,1024]{1,0:T(8,128)(2,1)} %get-tuple-element.54) | copy-start | bytes 12582916
  234.8 6.9 %copy-start.55 = (bf16[2048,1024]{1,0:T(8,128)(2,1)S(1)}, bf16[2048,1024]{1,0:T(8,128)(2,1)}, u32[]{:S(2)}) copy-start(bf16[2048,1024]{1,0:T(8,128)(2,1)} %get-tuple-element.54) | copy-start | bytes 12582916
  234.8 6.9 %copy-start.57 = (bf16[1024,2048]{1,0:T(8,128)(2,1)S(1)}, bf16[1024,2048]{1,0:T(8,128)(2,1)}, u32[]{:S(2)}) copy-start(bf16[1024,2048]{1,0:T(8,128)(2,1)} %get-tuple-element.53) | copy-start | bytes 12582916
  239.0 2.7 collective-permute-start.4
  245.1 8.3 %copy-start.24 = (bf16[512,1024]{1,0:T(8,128)(2,1)}, bf16[512,1024]{1,0:T(8,128)(2,1)S(1)}, u32[]{:S(2)}) copy-start(bf16[512,1024]{1,0:T(8,128)(2,1)S(1)} %fusion.24) | copy-start | bytes 3145732
  245.1 2.7 collective-permute-start.5
  274.4 2.7 collective-permute-start.6
  278.9 2.7 collective-permute-start.7
  300.9 8.1 %copy-start.56 = (bf16[2048,1024]{1,0:T(8,128)(2,1)S(1)}, bf16[2048,1024]{1,0:T(8,128)(2,1)}, u32[]{:S(2)}) copy-start(bf16[2048,1024]{1,0:T(8,128)(2,1)} %get-tuple-element.54) | copy-start | bytes 12582916
  300.9 8.1 %copy-start.59 = (bf16[1024,2048]{1,0:T(8,128)(2,1)S(1)}, bf16[1024,2048]{1,0:T(8,128)(2,1)}, u32[]{:S(2)}) copy-start(bf16[1024,2048]{1,0:T(8,128)(2,1)} %get-tuple-element.56) | copy-start | bytes 12582916
  306.2 2.7 collective-permute-start.8
  314.9 13.1 %copy-start.31 = (bf16[512,1024]{1,0:T(8,128)(2,1)}, bf16[512,1024]{1,0:T(8,128)(2,1)S(1)}, u32[]{:S(2)}) copy-start(bf16[512,1024]{1,0:T(8,128)(2,1)S(1)} %get-tuple-element.105) | copy-start | bytes 3145732
  314.9 2.7 collective-permute-start.9
  317.6 10.4 %copy-start.69 = (bf16[512,1024]{1,0:T(8,128)(2,1)}, bf16[512,1024]{1,0:T(8,128)(2,1)S(1)}, u32[]{:S(2)}) copy-start(bf16[512,1024]{1,0:T(8,128)(2,1)S(1)} %collective-permute-done.9) | copy-start | bytes 3145732
  317.6 10.4 %copy-start.10 = (bf16[1024,2048]{1,0:T(8,128)(2,1)S(1)}, bf16[1024,2048]{1,0:T(8,128)(2,1)}, u32[]{:S(2)}) copy-start(bf16[1024,2048]{1,0:T(8,128)(2,1)} %get-tuple-element.52.w_ref) | copy-start | bytes 12582916
  328.0 7.0 %copy-start.71 = (bf16[1024,2048]{1,0:T(8,128)(2,1)S(1)}, bf16[1024,2048]{1,0:T(8,128)(2,1)}, u32[]{:S(2)}) copy-start(bf16[1024,2048]{1,0:T(8,128)(2,1)} %get-tuple-element.145) | copy-start | bytes 12582916
  332.2 2.7 collective-permute-start.10
  339.3 2.7 collective-permute-start.11
  382.4 2.7 collective-permute-start.12
  390.1 3.0 collective-permute-start.13
  393.1 8.7 %copy-start.11 = (bf16[1024,2048]{1,0:T(8,128)(2,1)S(1)}, bf16[1024,2048]{1,0:T(8,128)(2,1)}, u32[]{:S(2)}) copy-start(bf16[1024,2048]{1,0:T(8,128)(2,1)} %get-tuple-element.52.w_ref) | copy-start | bytes 12582916
  404.3 7.8 %copy-start.18 = (bf16[512,1024]{1,0:T(8,128)(2,1)S(1)}, bf16[512,1024]{1,0:T(8,128)(2,1)}, u32[]{:S(2)}) copy-start(bf16[512,1024]{1,0:T(8,128)(2,1)} %copy-done.17) | copy-start | bytes 3145732
  404.3 7.8 %copy-start.34 = (bf16[512,1024]{1,0:T(8,128)(2,1)S(1)}, bf16[512,1024]{1,0:T(8,128)(2,1)}, u32[]{:S(2)}) copy-start(bf16[512,1024]{1,0:T(8,128)(2,1)} %copy-done.33) | copy-start | bytes 3145732
  404.3 7.8 %copy-start.72 = (bf16[1024,2048]{1,0:T(8,128)(2,1)S(1)}, bf16[1024,2048]{1,0:T(8,128)(2,1)}, u32[]{:S(2)}) copy-start(bf16[1024,2048]{1,0:T(8,128)(2,1)} %get-tuple-element.145) | copy-start | bytes 12582916
  404.3 27.3 %collective-permute-start.14 = (bf16[512,1024]{1,0:T(8,128)(2,1)S(1)}, bf16[512,1024]{1,0:T(8,128)(2,1)S(1)}, u32[]{:S(2)}, u32[]{:S(2)}) collective-permute-start(bf16[512,1024]{1,0:T(8,128)(2,1)S(1)} %fusion.49), channel_id=1, source_target_pairs={{0,4},{4,0},{8,12},{12,8},{16,20},{20,16},{24,28},{28,24},{1,5},{5... | collective-permute-start | bytes 3145736 | tf_op jit(solution)/shard_map/ppermute | solution.py:1137
  423.1 8.6 %copy-start.9 = (f32[512,1024]{1,0:T(8,128)S(1)}, f32[512,1024]{1,0:T(8,128)}, u32[]{:S(2)}) copy-start(f32[512,1024]{1,0:T(8,128)} %copy-done.8) | copy-start | bytes 6291460
  423.1 8.6 %copy-start.12 = (f32[512,1024]{1,0:T(8,128)S(1)}, f32[512,1024]{1,0:T(8,128)}, u32[]{:S(2)}) copy-start(f32[512,1024]{1,0:T(8,128)} %get-tuple-element.103) | copy-start | bytes 6291460
  433.9 10.8 %copy-start.66 = (bf16[512,1024]{1,0:T(8,128)(2,1)S(1)}, bf16[512,1024]{1,0:T(8,128)(2,1)}, u32[]{:S(2)}) copy-start(bf16[512,1024]{1,0:T(8,128)(2,1)} %get-tuple-element.51) | copy-start | bytes 3145732
  433.9 10.8 %collective-permute-start.15 = (bf16[512,1024]{1,0:T(8,128)(2,1)S(1)}, bf16[512,1024]{1,0:T(8,128)(2,1)S(1)}, u32[]{:S(2)}, u32[]{:S(2)}) collective-permute-start(bf16[512,1024]{1,0:T(8,128)(2,1)S(1)} %get-tuple-element.107), channel_id=1, source_target_pairs={{0,4},{4,0},{8,12},{12,8},{16,20},{20,16},{24,28},{28,24},{1,5},{5... | collective-permute-start | bytes 3145736 | tf_op jit(solution)/shard_map/ppermute | solution.py:1137
  490.1 11.0 %collective-permute-start.16 = (bf16[512,1024]{1,0:T(8,128)(2,1)S(1)}, bf16[512,1024]{1,0:T(8,128)(2,1)S(1)}, u32[]{:S(2)}, u32[]{:S(2)}) collective-permute-start(bf16[512,1024]{1,0:T(8,128)(2,1)S(1)} %fusion.37), channel_id=1, source_target_pairs={{0,4},{4,0},{8,12},{12,8},{16,20},{20,16},{24,28},{28,24},{1,5},{5... | collective-permute-start | bytes 3145736 | tf_op jit(solution)/shard_map/ppermute | solution.py:1137
  675.3 7.1 %copy-start.38 = (f32[256,128]{1,0:T(8,128)S(1)}, f32[256,128]{1,0:T(8,128)}, u32[]{:S(2)}) copy-start(f32[256,128]{1,0:T(8,128)} %get-tuple-element.174) | copy-start | bytes 393220
  675.3 7.7 %copy-start.37 = (f32[128,1024]{1,0:T(8,128)S(1)}, f32[128,1024]{1,0:T(8,128)}, u32[]{:S(2)}) copy-start(f32[128,1024]{1,0:T(8,128)} %get-tuple-element.178) | copy-start | bytes 1572868
  (44 other events, 138.5 us)

commit v2 on v1

--- a/solution.py
+++ b/solution.py
@@ -470,10 +470,15 @@
     pl.semaphore_wait(barrier, len(friends))
 
 
+PIECES = 8
+GROUPS = ((3,), (0,), (1,), (2,), (4,), (5,), (6,), (7,))
+
+
 def gather_kernel(
     q_ref, k_ref, v_ref, proj_ref, inner_ref, outer_ref, small_ref, x_ref, g_ref,
     wqkv, wproj, winner, wouter, smalls, u_out, g_out,
-    swap_s, swap_r, local_s, z_s, z_r, sm_s, sm_r, p1_s, p1_r, p2_s, p2_r, t_s, t_r, t_l,
+    swap_s, swap_r, local_s, up_s, up_r, down_s, down_r, sm_s, sm_r,
+    p1_s, p1_r, p2_s, p2_r, t_s, t_r, t_l,
 ):
     row, depth, core, chip, x, y = place()
     mate = chip * 2 + (1 - core)
@@ -488,65 +493,93 @@
             return (q_ref, k_ref, v_ref)[piece].at[:, span(half * 128, 128)]
         if piece == 3:
             return proj_ref.at[span(half * 128, 128), :]
-        if piece == 4:
-            return inner_ref.at[:, span(half * 512, 512)]
-        return outer_ref.at[span(half * 512, 512), :]
-
-    def swap_dst(piece, owner):
+        if piece < 6:
+            return inner_ref.at[:, span(half * 512 + (piece - 4) * 256, 256)]
+        return outer_ref.at[span(half * 512 + (piece - 6) * 256, 256), :]
+
+    def cell(piece, start, size, origin):
         if piece < 3:
-            return wqkv.at[span(owner * 128, 128), span(piece * 512 + depth * 128, 128)]
+            return wqkv.at[span(start, size), span(piece * 512 + origin * 128, 128)]
         if piece == 3:
-            return wproj.at[span(depth * 128, 128), span(owner * 128, 128)]
-        if piece == 4:
-            return winner.at[span(owner * 128, 128), span(depth * 512, 512)]
-        return wouter.at[span(depth * 512, 512), span(owner * 128, 128)]
-
-    def unit(piece):
+            return wproj.at[span(origin * 128, 128), span(start, size)]
+        if piece < 6:
+            return winner.at[
+                span(start, size), span((piece - 4) * 1024 + origin * 256, 256)
+            ]
+        return wouter.at[span((piece - 6) * 1024 + origin * 256, 256), span(start, size)]
+
+    def region(group, part, block):
+        piece = GROUPS[group][0]
         if piece < 3:
-            return wqkv.at[span(chip * 256, 256), span(piece * 512 + depth * 128, 128)]
+            return wqkv.at[span(block * 256 + part * 128, 128), pl.ds(piece * 512, 512)]
         if piece == 3:
-            return wproj.at[span(depth * 128, 128), span(chip * 256, 256)]
-        if piece == 4:
-            return winner.at[span(chip * 256, 256), span(depth * 512, 512)]
-        return wouter.at[span(depth * 512, 512), span(chip * 256, 256)]
-
-    def region(group, part, block):
-        if group == 0:
-            return wqkv.at[span(block * 256 + part * 128, 128), :]
-        if group == 1:
             return wproj.at[pl.ds(part * 256, 256), span(block * 256, 256)]
-        if group == 2:
-            return winner.at[span(block * 256 + part * 128, 128), :]
-        return wouter.at[pl.ds(part * 1024, 1024), span(block * 256, 256)]
-
-    waits = []
+        if piece < 6:
+            return winner.at[
+                span(block * 256 + part * 128, 128), pl.ds((piece - 4) * 1024, 1024)
+            ]
+        return wouter.at[
+            pl.ds((piece - 6) * 1024 + part * 512, 512), span(block * 256, 256)
+        ]
+
     swaps, locals_ = [], []
-    for piece in range(6):
+    for piece in range(PIECES):
+        target = cell(piece, row * 128, 128, depth)
         cp = remote(
-            swap_src(piece, 1 - core), swap_dst(piece, row),
-            swap_s.at[piece], swap_r.at[piece], mate, depth,
+            swap_src(piece, 1 - core), target, swap_s.at[piece], swap_r.at[piece], mate, depth
         )
         cp.start()
         swaps.append(cp)
-        lc = pltpu.make_async_copy(swap_src(piece, core), swap_dst(piece, row), local_s.at[piece])
+        lc = pltpu.make_async_copy(swap_src(piece, core), target, local_s.at[piece])
         lc.start()
         locals_.append(lc)
-    small_local = pltpu.make_async_copy(small_ref, smalls.at[depth], local_s.at[6])
+    small_local = pltpu.make_async_copy(small_ref, smalls.at[depth], local_s.at[PIECES])
     small_local.start()
 
-    zs = {}
-
-    def start_z(pieces):
-        for piece in pieces:
-            swaps[piece].wait_recv()
-            locals_[piece].wait()
-            for k in (1, 2, 3):
-                cp = remote(
-                    unit(piece), unit(piece), z_s.at[piece, k - 1], z_r.at[piece, k - 1],
-                    row, (depth + k) % 4,
-                )
-                cp.start()
-                zs[piece, k] = cp
+    def travel(piece, step, up):
+        origin = depth - step if up else depth + step
+        ref = cell(piece, chip * 256, 256, origin)
+        send, recv = (up_s, up_r) if up else (down_s, down_r)
+        return remote(
+            ref, ref, send.at[piece, step], recv.at[piece, step], row,
+            depth + 1 if up else depth - 1,
+        )
+
+    def depth_step(group, step):
+        for piece in GROUPS[group]:
+            if step == 0:
+                swaps[piece].wait_recv()
+                locals_[piece].wait()
+            for up in (True, False):
+                inside = depth - step >= 0 if up else depth + step <= 3
+                ready = inside & (depth < 3 if up else depth > 0)
+                if step > 0:
+
+                    @pl.when(inside)
+                    def _():
+                        origin = depth - step if up else depth + step
+                        ref = cell(piece, chip * 256, 256, origin)
+                        recv = up_r if up else down_r
+                        remote(
+                            ref, ref, up_s.at[piece, step - 1], recv.at[piece, step - 1],
+                            mate, depth,
+                        ).wait_recv()
+
+                if step < 3:
+
+                    @pl.when(ready)
+                    def _():
+                        travel(piece, step, up).start()
+
+    def depth_done():
+        for piece in range(PIECES):
+            for step in (0, 1, 2):
+                for up in (True, False):
+                    inside = depth - step >= 0 if up else depth + step <= 3
+
+                    @pl.when(inside & (depth < 3 if up else depth > 0))
+                    def _():
+                        travel(piece, step, up).wait_send()
 
     def token_copies(index, src, dst):
         for j in range(4):
@@ -592,18 +625,6 @@
                     src.at[pl.ds(j * 512, 512), :], dst.at[:, pl.ds(0, 256)],
                     t_s.at[index, j], t_r.at[index, 0], mate, depth,
                 ).wait_send()
-
-    start_z((0, 1, 2))
-    token_copies(0, x_ref, u_out)
-    start_z((3, 4, 5))
-    small_copies = []
-    for k in (1, 2, 3):
-        cp = remote(
-            small_ref, smalls.at[depth], sm_s.at[k - 1], sm_r.at[k - 1], row, (depth + k) % 4
-        )
-        cp.start()
-        small_copies.append(cp)
-    token_copies(1, g_ref, g_out)
 
     first, second = {}, {}
 
@@ -627,32 +648,48 @@
                 cp.start()
                 second[group, part, i] = cp
 
-    members = ((0, 1, 2), (3,), (4,), (5,))
-    for group in range(4):
-        for piece in members[group]:
+    count = len(GROUPS)
+    small_copies = []
+    for tick in range(count + 4):
+        for step in (0, 1, 2, 3):
+            group = tick - step
+            if 0 <= group < count:
+                depth_step(group, step)
+                if step == 3:
+                    start_first(group)
+        if 0 <= tick - 4 < count:
+            start_second(tick - 4)
+        if tick == TOKEN_TICK:
+            token_copies(0, x_ref, u_out)
+        if tick == count - 1:
             for k in (1, 2, 3):
-                zs[piece, k].wait_recv()
-        start_first(group)
-        if group > 0:
-            start_second(group - 1)
-    start_second(3)
+                cp = remote(
+                    small_ref, smalls.at[depth], sm_s.at[k - 1], sm_r.at[k - 1],
+                    row, (depth + k) % 4,
+                )
+                cp.start()
+                small_copies.append(cp)
+            token_copies(1, g_ref, g_out)
     token_waits(0, x_ref, u_out)
     token_waits(1, g_ref, g_out)
     for cp in small_copies:
         cp.wait()
     small_local.wait()
+    depth_done()
     for cp in second.values():
         cp.wait()
     for cp in first.values():
         cp.wait_send()
-    for cp in zs.values():
-        cp.wait_send()
     for cp in swaps:
         cp.wait_send()
 
 
+TOKEN_TICK = 7
+
+
 def gather_all(q, k, v, proj, inner, outer, small, x_rolled, g_rolled):
     sd = jax.ShapeDtypeStruct
+    n = len(GROUPS)
     return pl.pallas_call(
         gather_kernel,
         out_shape=(
@@ -664,23 +701,26 @@
             sd((512, 1024), BF16),
             sd((512, 1024), BF16),
         ),
-        in_specs=[ANY] * 9,
+        in_specs=[VMEM] * 7 + [ANY] * 2,
         out_specs=[ANY] * 7,
         scratch_shapes=[
-            DMA((6,)), DMA((6,)), DMA((7,)), DMA((6, 3)), DMA((6, 3)), DMA((3,)), DMA((3,)),
-            DMA((4, 2)), DMA((4, 2)), DMA((4, 2, 2)), DMA((4, 2, 2)),
+            DMA((PIECES,)), DMA((PIECES,)), DMA((PIECES + 1,)),
+            DMA((PIECES, 3)), DMA((PIECES, 3)), DMA((PIECES, 3)), DMA((PIECES, 3)),
+            DMA((3,)), DMA((3,)),
+            DMA((n, 2)), DMA((n, 2)), DMA((n, 2, 2)), DMA((n, 2, 2)),
             DMA((2, 4)), DMA((2, 4)), DMA((2,)),
         ],
         compiler_params=pltpu.CompilerParams(collective_id=1, has_side_effects=True),
     )(q, k, v, proj, inner, outer, small, x_rolled, g_rolled)
 
 
-SHAPES = ((1024, 256), (128, 2048), (256, 256), (128, 512), (128, 512), (128, 512))
-UNITS = ((512, 256), (256, 512), (128, 256), (256, 128), (256, 128), (256, 128))
-FULLS = ((2048, 256), (256, 2048), (512, 256), (256, 512), (256, 512), (256, 512))
-OUTS = ((1024, 128), (128, 1024), (256, 128), (128, 256), (128, 256), (128, 256))
-HALVES = ((512, 128), (128, 512), (128, 128), (128, 128), (128, 128), (128, 128))
-BY_COLS = (True, False, True, False, False, False)
+SHAPES = ((256, 256), (128, 512), (128, 512), (128, 512))
+UNITS = ((128, 256), (256, 128), (256, 128), (256, 128), (256, 256), (256, 256))
+FULLS = ((512, 256), (256, 512), (256, 512), (256, 512))
+OUTS = ((256, 128), (128, 256), (128, 256), (128, 256), (128, 1024), (1024, 128))
+HALVES = ((128, 128), (128, 128), (128, 128), (128, 128), (128, 256), (128, 256), (512, 128))
+BY_COLS = (True, False, False, False, False, False)
+OUTER = 6
 
 
 def add_rows(dst, terms):
@@ -699,18 +739,19 @@
 
 
 def scatter_kernel(*refs):
-    grads = refs[0:6]
-    small_ref, ho_ref, gi_ref = refs[6:9]
+    grads = refs[0:4]
+    inner_ref = refs[4:6]
+    outer_ref, small_ref, gi_ref = refs[6:9]
     outs = refs[9:15]
-    small_out, ho_out, gi_out = refs[15:18]
-    rest = list(refs[18:])
-    own = [[rest.pop(0) for _ in range(2)] for _ in range(6)]
-    got1 = [[rest.pop(0) for _ in range(2)] for _ in range(6)]
-    got2 = [[rest.pop(0) for _ in range(2)] for _ in range(6)]
-    full = [rest.pop(0) for _ in range(6)]
+    small_out, gi_out = refs[15:17]
+    rest = list(refs[17:])
+    own = [[rest.pop(0) for _ in range(2)] for _ in range(4)]
+    got1 = [[rest.pop(0) for _ in range(2)] for _ in range(4)]
+    got2 = [[rest.pop(0) for _ in range(2)] for _ in range(4)]
+    full = [rest.pop(0) for _ in range(4)]
     zgot = [rest.pop(0) for _ in range(6)]
     fin = [rest.pop(0) for _ in range(6)]
-    cgot = [rest.pop(0) for _ in range(6)]
+    cgot = [rest.pop(0) for _ in range(7)]
     sb = rest.pop(0)
     sg = rest.pop(0)
     (o_s, p1_s, p1_r, p2_s, p2_r, z_s, z_r, c_s, c_r, sm_s, sm_r, t_s, t_r, t_l) = rest
@@ -728,16 +769,24 @@
         return grads[group].at[span(block * 256 + part * 128, 128), :]
 
     def unit(group, z):
+        if group >= 4:
+            return inner_ref[group - 4].at[:, span(z * 256, 256)]
         if BY_COLS[group]:
             return full[group].at[span(z * UNITS[group][0], UNITS[group][0]), :]
         return full[group].at[:, span(z * UNITS[group][1], UNITS[group][1])]
 
     def side(group, half):
+        if group == OUTER:
+            return outer_ref.at[:, span(half * 128, 128)]
         if BY_COLS[group]:
             return fin[group].at[:, span(half * 128, 128)]
         return fin[group].at[span(half * 128, 128), :]
 
     def out_side(group, half):
+        if group == OUTER:
+            return outs[5].at[span(half * 512, 512), :]
+        if group >= 4:
+            return outs[4].at[:, span(half * 512 + (group - 4) * 256, 256)]
         size = HALVES[group]
         if BY_COLS[group]:
             return outs[group].at[span(half * size[0], size[0]), :]
@@ -778,6 +827,15 @@
             cp.start()
             copies["p2", group, part] = cp
 
+    def send_depth(group):
+        for k in (1, 2, 3):
+            cp = remote(
+                unit(group, (depth + k) % 4), zgot[group].at[k - 1],
+                z_s.at[group, k - 1], z_r.at[group, k - 1], row, (depth + k) % 4,
+            )
+            cp.start()
+            copies["z", group, k] = cp
+
     def start_depth(group):
         rows = SHAPES[group][0]
         for part in (0, 1):
@@ -787,13 +845,14 @@
                 full[group].at[pl.ds(part * rows, rows), :],
                 (own[group][part].at[mine], got1[group][part].at[mine], got2[group][part]),
             )
-        for k in (1, 2, 3):
-            cp = remote(
-                unit(group, (depth + k) % 4), zgot[group].at[k - 1],
-                z_s.at[group, k - 1], z_r.at[group, k - 1], row, (depth + k) % 4,
-            )
-            cp.start()
-            copies["z", group, k] = cp
+        send_depth(group)
+
+    def send_core(group):
+        cp = remote(
+            side(group, 1 - core), cgot[group], c_s.at[group], c_r.at[group], mate, depth
+        )
+        cp.start()
+        copies["c", group] = cp
 
     def start_core(group):
         for k in (1, 2, 3):
@@ -802,11 +861,7 @@
             fin[group],
             (unit(group, depth), zgot[group].at[0], zgot[group].at[1], zgot[group].at[2]),
         )
-        cp = remote(
-            side(group, 1 - core), cgot[group], c_s.at[group], c_r.at[group], mate, depth
-        )
-        cp.start()
-        copies["c", group] = cp
+        send_core(group)
 
     def finish(group):
         add_rows(out_side(group, core), (side(group, core),))
@@ -833,7 +888,6 @@
 
     def token_waits(index, src, dst):
         to_core = depth // 2
-        j_own = (depth % 2) * 2 + core
         for j in range(4):
             from_core, from_depth = j % 2, core * 2 + j // 2
             mine = (from_core == core) & (from_depth == depth)
@@ -871,45 +925,45 @@
         sb[step + 1] = sb[step] + sg[slot]
 
     sb[0] = small_ref[...]
+    for group in range(4):
+        start_first(group)
     small_send(0, 0, mate, depth)
-    start_first(0)
-    start_first(1)
-    token_copies(0, ho_ref, ho_out)
-    token_copies(1, gi_ref, gi_out)
+    send_core(OUTER)
+    send_depth(4)
+    send_depth(5)
+    token_copies(0, gi_ref, gi_out)
     small_add(0, 0)
     small_send(1, 1, x_row, depth)
-    for group in range(6):
+    finish(OUTER)
+    for group in range(4):
         start_second(group)
-        if group + 2 < 6:
-            start_first(group + 2)
         if group == 0:
             small_add(1, 1)
             small_send(2, 2, y_row, depth)
-        if group == 1:
-            small_add(2, 2)
-            for k in (1, 2, 3):
-                small_send(3, 2 + k, row, (depth + k) % 4)
         if group > 0:
             start_depth(group - 1)
-        if group > 1:
-            start_core(group - 2)
-    start_depth(5)
-    start_core(4)
+    small_add(2, 2)
+    for k in (1, 2, 3):
+        small_send(3, 2 + k, row, (depth + k) % 4)
+    start_depth(3)
+    for group in (4, 5):
+        start_core(group)
+    for group in (0, 1, 2):
+        start_core(group)
     for k in (1, 2, 3):
         copies["s", 2 + k].wait_recv()
     small_out[...] = ((sb[3] + sg[3]) + sg[4]) + sg[5]
-    for group in range(5):
+    for group in (4, 5, 0, 1, 2):
         finish(group)
-    token_waits(0, ho_ref, ho_out)
-    token_waits(1, gi_ref, gi_out)
-    start_core(5)
-    finish(5)
+    start_core(3)
+    token_waits(0, gi_ref, gi_out)
+    finish(3)
     for key, cp in copies.items():
         if key[0] != "o":
             cp.wait_send()
 
 
-def scatter_all(outer, inner, proj, q, k, v, small, ho, gi):
+def scatter_all(proj, q, k, v, inner_a, inner_b, outer, small, gi):
     sd = jax.ShapeDtypeStruct
     scratch = []
     for size in SHAPES:
@@ -924,21 +978,21 @@
     scratch += [pltpu.VMEM(size, BF16) for size in HALVES]
     scratch += [pltpu.VMEM((4,) + small.shape, F32), pltpu.VMEM((6,) + small.shape, F32)]
     scratch += [
-        DMA((6, 2, 2)), DMA((6, 2, 2)), DMA((6, 2, 2)), DMA((6, 2)), DMA((6, 2)),
-        DMA((6, 3)), DMA((6, 3)), DMA((6,)), DMA((6,)), DMA((6,)), DMA((6,)),
-        DMA((2, 4)), DMA((2, 4)), DMA((2,)),
+        DMA((4, 2, 2)), DMA((4, 2, 2)), DMA((4, 2, 2)), DMA((4, 2)), DMA((4, 2)),
+        DMA((6, 3)), DMA((6, 3)), DMA((7,)), DMA((7,)), DMA((6,)), DMA((6,)),
+        DMA((1, 4)), DMA((1, 4)), DMA((1,)),
     ]
     return pl.pallas_call(
         scatter_kernel,
         out_shape=tuple(sd(size, F32) for size in OUTS)
-        + (sd(small.shape, F32), sd((2048, 256), BF16), sd((2048, 256), BF16)),
-        in_specs=[ANY] * 6 + [VMEM] + [ANY] * 2,
-        out_specs=[VMEM] * 7 + [ANY] * 2,
+        + (sd(small.shape, F32), sd((2048, 256), BF16)),
+        in_specs=[ANY] * 4 + [VMEM] * 4 + [ANY],
+        out_specs=[VMEM] * 7 + [ANY],
         scratch_shapes=scratch,
         compiler_params=pltpu.CompilerParams(
-            collective_id=2, has_side_effects=True, vmem_limit_bytes=56 * 1024 * 1024
+            collective_id=2, has_side_effects=True, vmem_limit_bytes=48 * 1024 * 1024
         ),
-    )(outer, inner, proj, q, k, v, small, ho, gi)
+    )(proj, q, k, v, inner_a, inner_b, outer, small, gi)
 
 
 def attend_kernel(flag_ref, q_ref, k_ref, v_ref, idq_ref, idk_ref, o_ref, lse_ref):
@@ -947,24 +1001,40 @@
     low_half = lane < HEAD_DIM
 
     def compute(masked):
-        scaled = q_ref[...] * jnp.asarray(HEAD_DIM**-0.5, BF16)
         keys = k_ref[...]
         values = v_ref[...]
-        outs, logs = [], []
-        for head in (0, 1):
-            here = low_half if head == 0 else jnp.logical_not(low_half)
-            queries = jnp.where(here, scaled, jnp.zeros_like(scaled))
-            scores = against(queries, keys)
+        halves = (low_half, jnp.logical_not(low_half))
+        sub = 256
+        units = [(i, h) for i in range(rows // sub) for h in (0, 1)]
+
+        def score(unit):
+            i, h = unit
+            scaled = q_ref[i * sub : (i + 1) * sub, :] * jnp.asarray(HEAD_DIM**-0.5, BF16)
+            s = against(jnp.where(halves[h], scaled, jnp.zeros_like(scaled)), keys)
             if masked:
-                scores = jnp.where(idq_ref[...] == idk_ref[...], scores, NEG_FILL)
-            top = jnp.max(scores, axis=1, keepdims=True)
-            weights = jnp.exp(scores - top)
-            total = jnp.sum(weights, axis=1, keepdims=True)
-            mixed = matmul(weights.astype(BF16), values)
-            outs.append(mixed / total)
-            logs.append(top + jnp.log(total))
-        o_ref[...] = jnp.where(low_half, outs[0], outs[1]).astype(o_ref.dtype)
-        lse_ref[...] = jnp.where(low_half, logs[0], logs[1])
+                s = jnp.where(idq_ref[i * sub : (i + 1) * sub, :] == idk_ref[...], s, NEG_FILL)
+            return s
+
+        def soft(s):
+            top = jnp.max(s, axis=1, keepdims=True)
+            weights = jnp.exp(s - top)
+            return weights.astype(BF16), jnp.sum(weights, axis=1, keepdims=True), top
+
+        skew = 1
+        pending = [score(u) for u in units[:skew]]
+        done = {}
+        for n, unit in enumerate(units):
+            if n + skew < len(units):
+                pending.append(score(units[n + skew]))
+            low, total, top = soft(pending.pop(0))
+            mixed = matmul(low, values)
+            done[unit] = (mixed / total, top + jnp.log(total))
+            i, h = unit
+            if h == 1:
+                sl = slice(i * sub, (i + 1) * sub)
+                a, b = done[i, 0], done[i, 1]
+                o_ref[sl, :] = jnp.where(low_half, a[0], b[0]).astype(o_ref.dtype)
+                lse_ref[sl, :] = jnp.where(low_half, a[1], b[1])
 
     @pl.when(flag_ref[0] == 1)
     def _():
@@ -978,7 +1048,7 @@
 def attend(flag, qkv, id_col, id_row):
     tokens, width = qkv.shape[0], qkv.shape[1] // 3
     pairs = width // 128
-    block = 256
+    block = tokens
     return pl.pallas_call(
         attend_kernel,
         out_shape=(
@@ -1003,24 +1073,21 @@
         compiler_params=pltpu.CompilerParams(
             dimension_semantics=("arbitrary", "arbitrary"), vmem_limit_bytes=48 * 1024 * 1024
         ),
+        cost_estimate=pl.CostEstimate(
+            flops=20_000_000_000, bytes_accessed=8_000_000, transcendentals=0
+        ),
         name="attend",
     )(flag, qkv, qkv, qkv, id_col, id_row)
 
 
 def attend_back_kernel(
     flag_ref, q_ref, k_ref, v_ref, do_ref, lse_ref, idk_ref, idq_ref,
-    dq_ref, dk_ref, dv_ref, dk_acc, dv_acc,
+    dq_ref, dk_ref, dv_ref,
 ):
-    step = pl.program_id(1)
-    last = pl.num_programs(1) - 1
+    rows = q_ref.shape[0]
     scale = HEAD_DIM**-0.5
     lane = lax.broadcasted_iota(jnp.int32, (1, 128), 1)
     low_half = lane < HEAD_DIM
-
-    @pl.when(step == 0)
-    def _():
-        dk_acc[...] = jnp.zeros_like(dk_acc)
-        dv_acc[...] = jnp.zeros_like(dv_acc)
 
     def compute(masked):
         queries = q_ref[...]
@@ -1029,9 +1096,11 @@
         values = v_ref[...]
         grads = do_ref[...]
         lse_t = lse_ref[...].T
+        q_t, k_t, do_t = queries.T, keys.T, grads.T
         dqs, dks, dvs = [], [], []
         for head in (0, 1):
             here = low_half if head == 0 else jnp.logical_not(low_half)
+            part = slice(head * HEAD_DIM, (head + 1) * HEAD_DIM)
             zero = jnp.zeros_like(keys)
             scores = against(jnp.where(here, keys, zero), scaled)
             if masked:
@@ -1042,12 +1111,13 @@
             moved = probs * grad_probs
             delta = jnp.sum(moved, axis=0, keepdims=True)
             grad_scores = (moved - probs * delta).astype(BF16)
-            dvs.append(matmul(probs.astype(BF16), grads))
+            low = probs.astype(BF16)
+            dvs.append(against(do_t[part], low))
             dks.append(matmul(grad_scores, queries))
-            dqs.append(over_tokens(grad_scores, keys))
-        dq_ref[...] = (jnp.where(low_half, dqs[0], dqs[1]) * scale).astype(BF16)
-        dk_acc[...] += jnp.where(low_half, dks[0], dks[1]) * scale
-        dv_acc[...] += jnp.where(low_half, dvs[0], dvs[1])
+            dqs.append(matmul(k_t[part], grad_scores))
+        dv_ref[...] = jnp.concatenate(dvs, axis=0).T.astype(BF16)
+        dk_ref[...] = (jnp.where(low_half, dks[0], dks[1]) * scale).astype(BF16)
+        dq_ref[...] = (jnp.concatenate(dqs, axis=0) * scale).T.astype(BF16)
 
     @pl.when(flag_ref[0] == 1)
     def _():
@@ -1057,62 +1127,78 @@
     def _():
         compute(True)
 
-    @pl.when(step == last)
-    def _():
-        dk_ref[...] = dk_acc[...].astype(BF16)
-        dv_ref[...] = dv_acc[...].astype(BF16)
-
-
-def attend_back(flag, qkv, do, lse, id_col, id_row):
+
+def attend_back(flag, qkv, do, lse, id_col, id_row, first=0, count=4):
     tokens, width = qkv.shape[0], qkv.shape[1] // 3
     pairs = width // 128
-    block = 256
-    shape = jax.ShapeDtypeStruct((tokens, width), BF16)
-    rows = pl.BlockSpec((block, 128), lambda h, i, f: (i, h))
-    full = pl.BlockSpec((tokens, 128), lambda h, i, f: (0, h))
+    block = tokens
+    shape = jax.ShapeDtypeStruct((tokens, count * 128), BF16)
+    rows = pl.BlockSpec((block, 128), lambda h, i, f: (i, h + first))
     return pl.pallas_call(
         attend_back_kernel,
         out_shape=(shape, shape, shape),
         grid_spec=pltpu.PrefetchScalarGridSpec(
             num_scalar_prefetch=1,
-            grid=(width // 128, tokens // block),
+            grid=(count, tokens // block),
             in_specs=[
                 rows,
-                pl.BlockSpec((tokens, 128), lambda h, i, f: (0, h + pairs)),
-                pl.BlockSpec((tokens, 128), lambda h, i, f: (0, h + 2 * pairs)),
+                pl.BlockSpec((tokens, 128), lambda h, i, f: (0, h + first + pairs)),
+                pl.BlockSpec((tokens, 128), lambda h, i, f: (0, h + first + 2 * pairs)),
                 rows, rows,
                 pl.BlockSpec((tokens, 1), lambda h, i, f: (0, 0)),
                 pl.BlockSpec((1, block), lambda h, i, f: (0, i)),
             ],
-            out_specs=[rows, full, full],
-            scratch_shapes=[pltpu.VMEM((tokens, 128), F32)] * 2,
+            out_specs=[
+                pl.BlockSpec((block, 128), lambda h, i, f: (i, h)),
+                pl.BlockSpec((tokens, 128), lambda h, i, f: (0, h)),
+                pl.BlockSpec((tokens, 128), lambda h, i, f: (0, h)),
+            ],
         ),
         compiler_params=pltpu.CompilerParams(
             dimension_semantics=("arbitrary", "arbitrary"), vmem_limit_bytes=48 * 1024 * 1024
         ),
+        cost_estimate=pl.CostEstimate(
+            flops=10_000_000_000 * count, bytes_accessed=2_500_000 * count, transcendentals=0
+        ),
         name="attend_back",
     )(flag, qkv, qkv, qkv, do, lse, id_col, id_row)
 
 
+def gelu_pair(inner):
+    size = jnp.abs(inner)
+    bell = jnp.exp(inner * (inner * -0.5))
+    t = 1.0 / (1.0 + (0.3275911 * 0.5**0.5) * size)
+    poly = (0.5 * 1.061405429) * t - 0.5 * 1.453152027
+    poly = poly * t + 0.5 * 1.421413741
+    poly = poly * t - 0.5 * 0.284496736
+    poly = poly * t + 0.5 * 0.254829592
+    tail = (poly * t) * bell
+    below = jnp.where(inner >= 0.0, 1.0 - tail, tail)
+    return (inner * below).astype(BF16), (below + inner * (bell * 0.3989422804014327)).astype(BF16)
+
+
 def ffn_in_kernel(x_ref, w_ref, b_ref, active_ref, slope_ref):
-    inner = matmul(x_ref[...], w_ref[...]) + b_ref[...]
-    size = jnp.abs(inner) * (0.5**0.5)
-    bell = jnp.exp(-0.5 * inner * inner)
-    t = 1.0 / (1.0 + 0.3275911 * size)
-    poly = 1.061405429 * t - 1.453152027
-    poly = poly * t + 1.421413741
-    poly = poly * t - 0.284496736
-    poly = poly * t + 0.254829592
-    tail = 0.5 * (poly * t) * bell
-    below = jnp.where(inner >= 0.0, 1.0 - tail, tail)
-    active_ref[...] = (inner * below).astype(BF16)
-    slope_ref[...] = (below + inner * bell * 0.3989422804014327).astype(BF16)
+    rows, cols = active_ref.shape
+    sub = 128
+    skew = 1
+
+    def open_unit(i):
+        return matmul(x_ref[i * sub : (i + 1) * sub, :], w_ref[...]) + b_ref[...]
+
+    count = rows // sub
+    pending = [open_unit(i) for i in range(skew)]
+    for i in range(count):
+        if i + skew < count:
+            pending.append(open_unit(i + skew))
+        active, slope = gelu_pair(pending.pop(0))
+        active_ref[i * sub : (i + 1) * sub, :] = active
+        slope_ref[i * sub : (i + 1) * sub, :] = slope
 
 
 def ffn_in(x, w, bias):
     tokens, depth = x.shape
     hidden = w.shape[1]
-    rows, cols = 256, 512
+    rows, cols = 1024, 512
     shape = jax.ShapeDtypeStruct((tokens, hidden), BF16)
     out = pl.BlockSpec((rows, cols), lambda n, m: (m, n))
     return pl.pallas_call(
@@ -1128,6 +1214,9 @@
         compiler_params=pltpu.CompilerParams(
             dimension_semantics=("arbitrary", "arbitrary"), vmem_limit_bytes=48 * 1024 * 1024
         ),
+        cost_estimate=pl.CostEstimate(
+            flops=14_000_000_000, bytes_accessed=14_000_000, transcendentals=0
+        ),
         name="ffn_in",
     )(x, w, bias)
 
@@ -1186,7 +1275,7 @@
     return output, kept
 
 
-def fast_backward(grad_output, kept, weights, vectors, ids):
+def fast_backward(grad_output, kept, weights, vectors, ids, later=None):
     (
         whole_in, qkv, lse, attended, normed_one, inverse_one,
         whole_mid, active, slope, normed_two, inverse_two,
@@ -1199,9 +1288,10 @@
     ffn_low = rounded(grad_second)
     whole_second = both(ffn_low)
     inner_low = rounded(against(whole_second, wouter) * slope.astype(F32))
-    outer_term = over_tokens(active, whole_second)
+    relative_second = by_place(whole_second)
+    outer_terms = outer_pieces(active, relative_second)
     grad_first = grad_second + share_sum(inner_low, winner, against)
-    inner_term = over_tokens(whole_mid, inner_low)
+    inner_terms = inner_pieces(by_place(whole_mid), inner_low)
     grad_attn, attn_gain_sum, attn_shift_sum = norm_rows_back(
         grad_first, normed_one, inverse_one, vectors["attn_gain"]
     )
@@ -1209,10 +1299,30 @@
     whole_attn = both(attn_low)
     mixed_grad = rounded(against(whole_attn, wproj))
     proj_term = over_tokens(attended, whole_attn)
-    grads = attend_back(flag, qkv, mixed_grad, lse, id_col, id_row)
+    if later is None:
+        grads = attend_back(flag, qkv, mixed_grad, lse, id_col, id_row)
+    else:
+        outer_terms = add_trees(outer_terms, later[0])
+        inner_terms = add_trees(inner_terms, later[1])
+        planes = [Plane(outer_terms, h, 1) for h in (0, 1)] + [
+            Plane(inner_terms, h, 0) for h in (0, 1)
+        ]
+        sent, mixed_grad = lax.optimization_barrier(([p.sent for p in planes], mixed_grad))
+        got = [p.step_one(s) for p, s in zip(planes, sent)]
+        early = attend_back(flag, qkv, mixed_grad, lse, id_col, id_row, 0, 2)
+        got, early = lax.optimization_barrier((got, early))
+        handed = [p.to_hand(g) for p, g in zip(planes, got)]
+        handed, mixed_grad = lax.optimization_barrier((handed, mixed_grad))
+        more = [p.step_two(v) for p, v in zip(planes, handed)]
+        late = attend_back(flag, qkv, mixed_grad, lse, id_col, id_row, 2, 2)
+        more, late = lax.optimization_barrier((more, late))
+        folded = [p.close(m) for p, m in zip(planes, more)]
+        outer_terms = fold_depth(folded[:2])
+        inner_terms = folded[2:]
+        grads = tuple(jnp.concatenate(pair, axis=1) for pair in zip(early, late))
     grad_qkv = jnp.concatenate(grads, axis=1)
     grad_input = grad_attn + share_sum(grad_qkv, wqkv, against)
-    terms = (outer_term, inner_term, proj_term) + tuple(
+    terms = (proj_term,) + tuple(
         over_tokens(whole_in, part) for part in grads
     )
     small = (
@@ -1220,7 +1330,100 @@
         attn_gain_sum, attn_shift_sum, token_sum(inner_low), token_sum(ffn_low),
         ffn_gain_sum, ffn_shift_sum,
     )
-    return grad_input, terms, small
+    return grad_input, terms, outer_terms, inner_terms, small
+
+
+def flip_row(bit):
+    return [(r, r + bit - 2 * bit * ((r // bit) % 2)) for r in range(8)]
+
+
+def by_place(values):
+    chip = lax.axis_index("row") // 2
+    x, y = chip % 2, chip // 2
+
+    def block(yy, xx):
+        return lax.dynamic_slice_in_dim(values, (yy * 2 + xx) * 256, 256, 1)
+
+    far = block(1 - y, 1 - x)
+    return jnp.concatenate(
+        [block(y, 1 - x), block(y, x), block(1 - y, x), far, block(y, 1 - x)], axis=1
+    )
+
+
+CUTS = (((512, 1024), (0, 256), (256, 512)), ((768, 1280), (512, 768), (256, 512)))
+
+
+def outer_pieces(active, relative):
+    return [
+        [over_tokens(active[:, h * 1024 : (h + 1) * 1024], relative[:, a:b]) for a, b in CUTS[h]]
+        for h in (0, 1)
+    ]
+
+
+def inner_pieces(relative, inner_low):
+    return [
+        [over_tokens(relative[:, a:b], inner_low[:, h * 1024 : (h + 1) * 1024]) for a, b in CUTS[h]]
+        for h in (0, 1)
+    ]
+
+
+def add_trees(left, right):
+    return jax.tree.map(lambda p, q: p + q, left, right)
+
+
+class Plane:
+    def __init__(self, pieces, half, axis):
+        sent, self.handed, self.own = pieces[half]
+        self.sent = rounded(sent)
+        self.half, self.axis = half, axis
+        self.first, self.second = (4, 2) if half == 0 else (2, 4)
+
+    def step_one(self, sent):
+        return lax.ppermute(sent, "row", flip_row(self.first))
+
+    def to_hand(self, got):
+        low, high = jnp.split(got, 2, axis=self.axis)
+        self.got, handed = (low, high) if self.half == 0 else (high, low)
+        return rounded(self.handed + handed.astype(F32))
+
+    def step_two(self, handed):
+        return lax.ppermute(handed, "row", flip_row(self.second))
+
+    def close(self, more):
+        return rounded(self.own + self.got.astype(F32) + more.astype(F32))
+
+
+def fold_depth(halves):
+    depth = lax.axis_index("col")
+    stacked = [half.reshape(4, 256, 256) for half in halves]
+
+    def unit(z):
+        picked = [lax.dynamic_index_in_dim(s, z, 0, keepdims=False) for s in stacked]
+        return jnp.concatenate(picked, axis=0)
+
+    total = unit(depth).astype(F32)
+    for k in (1, 2, 3):
+        pairs = [(z, (z + k) % 4) for z in range(4)]
+        total = total + lax.ppermute(unit((depth + k) % 4), "col", pairs).astype(F32)
+    return rounded(total)
+
+
+def spread_out(values, own_start):
+    core = lax.axis_index("row") % 2
+    depth = lax.axis_index("col")
+    j = (depth % 2) * 2 + core
+    parts = []
+    for k in range(4):
+        pairs = []
+        for r in range(8):
+            for z in range(4):
+                block = ((z % 2) * 2 + r % 2 + k) % 4
+                pairs.append((r * 4 + z, (r // 2 * 2 + z // 2) * 4 + block))
+        piece = lax.dynamic_slice_in_dim(values, ((j + k) % 4) * 256, 256, 1)
+        parts.append(lax.ppermute(piece, ("row", "col"), pairs))
+    cycle = jnp.concatenate(parts[::-1] * 2, axis=0)
+    start = ((3 - depth) * 512 - own_start + 2048) % 2048
+    return lax.dynamic_slice(cycle, (start, 0), (2048, 256)).astype(F32)
 
 
 VECTORS = (
@@ -1296,6 +1499,9 @@
         if name in SPLIT:
             part = jnp.where(core == 0, part[:, : size // 2], part[:, size // 2 :])
         vectors[name] = part.reshape(1, -1)
+    vectors["inner"] = (
+        vectors["inner"].reshape(4, 2, 256).transpose(1, 0, 2).reshape(1, 2048)
+    )
     vectors["qkv"] = jnp.concatenate(
         [vectors["q"], jnp.zeros_like(vectors["q"]), vectors["v"]], axis=1
     )
@@ -1303,14 +1509,21 @@
     middle, kept_one = fast_forward(start_low.astype(F32), weights, vectors, ids)
     final_out, kept_two = fast_forward(middle, weights, vectors, ids)
     grad_flow = grad_low.astype(F32)
-    grad_flow, terms_two, small_two = fast_backward(grad_flow, kept_two, weights, vectors, ids)
-    grad_flow, terms_one, small_one = fast_backward(grad_flow, kept_one, weights, vectors, ids)
+    grad_flow, terms_two, outer_two, inner_two, small_two = fast_backward(
+        grad_flow, kept_two, weights, vectors, ids
+    )
+    hidden_out = spread_out(rounded(final_out), own_start)
+    grad_flow, terms_one, outer_full, (inner_a, inner_b), small_one = fast_backward(
+        grad_flow, kept_one, weights, vectors, ids, (outer_two, inner_two)
+    )
     terms = [rounded(a + b) for a, b in zip(terms_two, terms_one)]
     pieces = []
     for (name, size), a, b in zip(VECTORS, small_two, small_one):
         total = a + b
         if name in SPLIT:
             half = total.reshape(4, 1, size // 2)
+            if name == "inner":
+                half = total.reshape(2, 4, 256).transpose(1, 0, 2).reshape(4, 1, 512)
             zero = jnp.zeros_like(half)
             total = jnp.where(
                 core == 0,
@@ -1319,15 +1532,15 @@
             )
         pieces.append(total.reshape(-1))
     small_sum = jnp.concatenate(pieces).reshape(96, 128)
-    results = scatter_all(*terms, small_sum, rounded(final_out), rounded(grad_flow))
-    outer_g, inner_g, proj_g, q_g, k_g, v_g, small_all, out_turned, grad_turned = results
+    results = scatter_all(*terms, inner_a, inner_b, outer_full, small_sum, rounded(grad_flow))
+    proj_g, q_g, k_g, v_g, inner_g, outer_g, small_all, grad_turned = results
     small_all = small_all.reshape(-1)
     sums, offset = {}, 0
     for name, size in VECTORS:
         sums[name] = lax.dynamic_slice(small_all, (offset + depth * size,), (size,))
         offset += 4 * size
     return (
-        turned_back(out_turned),
+        hidden_out,
         turned_back(grad_turned),
         q_g,
         k_g,

time: 691 us -> 622 us (0.900)
  Pallas kernels: 474 us -> 311 us
  waiting for transfers between devices: 26.1 us -> 70.8 us
  starting transfers between devices: 6.76 us -> 30.4 us
  matrix products: 123 us -> 141 us
    pallas_call x1, Pallas kernels: 168 us -> 77.8 us  [scatter_all(): pl.pallas_call(scatter_kernel, out_shape=tuple((sd(size, F32) for size in...]
    ppermute x0 -> x15, waiting for transfers between devices: none -> 53.5 us  [the longest x4 28.2 us: step_one(): return lax.ppermute(sent, 'row', flip_row(self.first))]
    pallas_call x1, Pallas kernels: 160 us -> 130 us  [gather_all(): pl.pallas_call(gather_kernel, out_shape=(sd((1024, 1536), BF16), sd((512,...]
    dot_general x12 -> x32, matrix products: 47.4 us -> 71.9 us  [over_tokens(): lax.dot_general(left, right, (((0,), (0,)), ((), ())), preferred_element_...]
    ppermute x0 -> x15, starting transfers between devices: none -> 21.9 us  [the longest x4 10.2 us: spread_out(): parts.append(lax.ppermute(piece, ('row', 'col'), pairs))]
    pallas_call x2 -> x3, Pallas kernels: 69.9 us -> 49.9 us  [attend_back(): pl.pallas_call(attend_back_kernel, out_shape=(shape, shape, shape), grid_...]
    pallas_call x2, Pallas kernels: 40.5 us -> 26.6 us  [attend(): pl.pallas_call(attend_kernel, out_shape=(jax.ShapeDtypeStruct((tokens, wi...]
    ppermute x17, waiting for transfers between devices: 26.1 us -> 17.2 us  [exchange(): return lax.ppermute(values, 'row', pairs)]
  transfers between devices with their start and end apart: 17 -> 32, of which waited for: 12 -> 18; matrix products, arithmetic and copies ran while one was open for 9% -> 11% of each run, Pallas kernels for 23% -> 4%
where the time goes in v2:
time: 622 us; the launch traced here: 616 us
  Pallas kernels  311 us (50%)
  matrix products  141 us (23%)
  waiting for transfers between devices  70.8 us (11%)
  starting transfers between devices  30.4 us (5%)
  other arithmetic  29.3 us (5%)
  local copies, waits for them, and re-layouts  24.3 us (4%)
  between operations  8.82 us (1%)
    pallas_call x1, Pallas kernels, gather_all(): pl.pallas_call(gather_kernel, out_shape=(sd((1024, 1536), BF16), sd((512,...  130 us
    pallas_call x1, Pallas kernels, scatter_all(): pl.pallas_call(scatter_kernel, out_shape=tuple((sd(size, F32) for size in...  77.8 us
    dot_general x32, matrix products, over_tokens(): lax.dot_general(left, right, (((0,), (0,)), ((), ())), preferred_element_...  71.9 us
    pallas_call x3, Pallas kernels, attend_back(): pl.pallas_call(attend_back_kernel, out_shape=(shape, shape, shape), grid_...  49.9 us
    dot_general x12, matrix products, against(): lax.dot_general(left, right, (((1,), (1,)), ((), ())), preferred_element_...  38.1 us
    dot_general x10, matrix products, matmul(): return jnp.dot(left, right, preferred_element_type=jnp.float32)  31.2 us
    ppermute x4, waiting for transfers between devices, step_one(): return lax.ppermute(sent, 'row', flip_row(self.first))  28.2 us
    pallas_call x2, Pallas kernels, ffn_in(): pl.pallas_call(ffn_in_kernel, out_shape=(shape, shape), grid=(hidden // c...  27.6 us
  transfers between devices with their start and end apart: 32, of which 18 were waited for; matrix products, arithmetic and copies ran while one was open for 11% of the time, Pallas kernels for 4%

profile of v2, /device:TPU:0, one launch (start us, length us, event | category | flops | bytes accessed | tf_op | source)
XLA Modules:
  0.0 616.3 jit_solution(5335067974867707327)
XLA Ops:
  4.6 5.3 fusion.203
  9.9 129.6 %shard_map.305 = (bf16[1024,1536]{1,0:T(8,128)(2,1)}, bf16[512,1024]{1,0:T(8,128)(2,1)}, bf16[1024,2048]{1,0:T(8,128)(2,1)}, bf16[2048,1024]{1,0:T(8,128)(2,1)},...) custom-call(bf16[128,256]{1,0:T(8,128)(2,1)} %q_ref.1, bf16[128,256]{1,0:T(8,128)(2,1)} %k_ref.1, ...), custom_call_target="tpu_custom_call" | custom-call | tf_op jit(solution)/shard_map/pallas_call | solution.py:693
  147.7 7.6 %add_convert_fusion.1.q_ref.k_ref.v_ref = bf16[1024,1536]{1,0:T(8,128)(2,1)} fusion(bf16[1024,1024]{1,0:T(8,128)(2,1)} %constant_dynamic-update-slice_fusion.1, bf16[1024,1536]{1,0:T(8,128)(2,1)} %get-tuple-element.74, f32[1536]{0:T(1024)S(1)} %fusion.261), kind=kOutput, calls=%fused_computation.5 | convolution fusion | flops 3224371200 | bytes 8394752 | tf_op jit(solution)/shard_map/dot_general | solution.py:26
  155.3 13.1 %attend.2 = (bf16[1024,512]{1,0:T(8,128)(2,1)S(1)}, f32[1024,512]{1,0:T(8,128)S(1)}) custom-call(s32[1]{0:T(128)} %bitcast.1.flag_ref, bf16[1024,1536]{1,0:T(8,128)(2,1)} %add_convert_fusion.1.q_ref.k_ref.v_ref, bf16[1024,1536]{1,0:T(8,128)(2,1)} %add_convert_fusion.1.q_ref.k_ref.v_ref, bf16[1024,1536]{1,0:T(8,128)(2,1)} %add_convert_fusion.1.q_ref.k_ref.v_ref, ...), custom_call_target="tpu_custom_call" | custom-call | flops 20000000000 | bytes 8000000 | tf_op jit(solution)/shard_map/attend/pallas_call | solution.py:1052
  169.3 2.6 collective-permute-done.2
  177.2 13.9 %ffn_in.2 = (bf16[1024,2048]{1,0:T(8,128)(2,1)}, bf16[1024,2048]{1,0:T(8,128)(2,1)}) custom-call(bf16[1024,1024]{1,0:T(8,128)(2,1)S(1)} %pad_maximum_fusion.x_ref, bf16[1024,2048]{1,0:T(8,128)(2,1)} %get-tuple-element.78.w_ref, f32[1,2048]{1,0:T(1,128)S(1)} %reshape.246.b_ref), custom_call_target="tpu_custom_call" | custom-call | flops 14000000000 | bytes 14000000 | tf_op jit(solution)/shard_map/ffn_in/pallas_call | solution.py:1204
  191.1 4.1 fusion.88
  198.0 2.9 fusion.289
  201.6 2.5 collective-permute-done.5
  205.1 5.7 add_convert_fusion.q_ref.k_ref.v_ref
  210.8 13.5 %attend.3 = (bf16[1024,512]{1,0:T(8,128)(2,1)S(1)}, f32[1024,512]{1,0:T(8,128)S(1)}) custom-call(s32[1]{0:T(128)} %bitcast.1.flag_ref, bf16[1024,1536]{1,0:T(8,128)(2,1)} %add_convert_fusion.q_ref.k_ref.v_ref, bf16[1024,1536]{1,0:T(8,128)(2,1)} %add_convert_fusion.q_ref.k_ref.v_ref, bf16[1024,1536]{1,0:T(8,128)(2,1)} %add_convert_fusion.q_ref.k_ref.v_ref, ...), custom_call_target="tpu_custom_call" | custom-call | flops 20000000000 | bytes 8000000 | tf_op jit(solution)/shard_map/attend/pallas_call | solution.py:1052
  225.2 2.5 collective-permute-done.6
  229.7 2.5 collective-permute-done.7
  233.2 13.7 %ffn_in.3 = (bf16[1024,2048]{1,0:T(8,128)(2,1)}, bf16[1024,2048]{1,0:T(8,128)(2,1)}) custom-call(bf16[1024,1024]{1,0:T(8,128)(2,1)S(1)} %pad_maximum_fusion.1.x_ref, bf16[1024,2048]{1,0:T(8,128)(2,1)} %get-tuple-element.78.w_ref, f32[1,2048]{1,0:T(1,128)S(1)} %reshape.246.b_ref), custom_call_target="tpu_custom_call" | custom-call | flops 14000000000 | bytes 14000000 | tf_op jit(solution)/shard_map/ffn_in/pallas_call | solution.py:1204
  247.0 4.1 fusion.91
  253.9 2.9 fusion.287
  266.0 7.3 %convert_reduce_fusion.1 = (f32[2048]{0:T(1024)S(1)}, bf16[1024,2048]{1,0:T(8,128)(2,1)S(1)}) fusion(bf16[1024,2048]{1,0:T(8,128)(2,1)} %get-tuple-element.84, bf16[2048,1024]{1,0:T(8,128)(2,1)S(1)} %copy-done.88, bf16[512,1024]{1,0:T(8,128)(2,1)} %collective-permute-done.13, bf16[512,1024]{1,0:T(8,128)(2,1)} %get-tuple-element.157), kind=kOutput, calls=%fused_computation.1 | convolution fusion | flops 4309645312 | bytes 14688256 | tf_op jit(solution)/shard_map/dot_general | solution.py:36
  282.9 2.7 fusion.50
  285.6 2.8 fusion.62
  288.4 2.7 fusion.42
  291.1 2.6 fusion.30
  294.2 4.2 multiply_reduce_fusion.2
  302.7 2.6 fusion.66
  305.4 2.6 fusion.54
  309.3 24.2 %attend_back.3 = (bf16[1024,512]{1,0:T(8,128)(2,1)S(1)}, bf16[1024,512]{1,0:T(8,128)(2,1)S(1)}, bf16[1024,512]{1,0:T(8,128)(2,1)S(1)}) custom-call(s32[1]{0:T(128)} %bitcast.1.flag_ref, bf16[1024,1536]{1,0:T(8,128)(2,1)} %add_convert_fusion.q_ref.k_ref.v_ref, bf16[1024,1536]{1,0:T(8,128)(2,1)} %add_convert_fusion.q_ref.k_ref.v_ref, ...), custom_call_target="tpu_custom_call" | custom-call | flops 40000000000 | bytes 10000000 | tf_op jit(solution)/shard_map/attend_back/pallas_call | solution.py:1137
  339.4 5.4 collective-permute-start.9
  345.2 3.6 collective-permute-start.11
  351.5 5.6 collective-permute-done.10
  357.1 5.2 collective-permute-done.11
  362.4 2.5 multiply_reduce_fusion
  367.0 5.1 collective-permute-start.17
  375.1 7.0 %convert_reduce_fusion = (f32[2048]{0:T(1024)S(1)}, bf16[1024,2048]{1,0:T(8,128)(2,1)S(1)}) fusion(bf16[1024,2048]{1,0:T(8,128)(2,1)} %get-tuple-element.89, bf16[2048,1024]{1,0:T(8,128)(2,1)S(1)} %copy-done.89, bf16[512,1024]{1,0:T(8,128)(2,1)S(1)} %collective-permute-done.17, bf16[512,1024]{1,0:T(8,128)(2,1)S(1)} %get-tuple-element.154), kind=kOutput, calls=%fused_computation | convolution fusion | flops 4309645312 | bytes 14688256 | tf_op jit(solution)/shard_map/dot_general | solution.py:36
  382.1 3.3 fusion.97
  385.8 5.0 add_convert_fusion.7
  413.1 12.7 %attend_back.4 = (bf16[1024,256]{1,0:T(8,128)(2,1)S(1)}, bf16[1024,256]{1,0:T(8,128)(2,1)S(1)}, bf16[1024,256]{1,0:T(8,128)(2,1)S(1)}) custom-call(s32[1]{0:T(128)} %bitcast.1.flag_ref, bf16[1024,1536]{1,0:T(8,128)(2,1)} %add_convert_fusion.1.q_ref.k_ref.v_ref, bf16[1024,1536]{1,0:T(8,128)(2,1)} %add_convert_fusion.1.q_ref.k_ref.v_ref, ...), custom_call_target="tpu_custom_call" | custom-call | flops 20000000000 | bytes 5000000 | tf_op jit(solution)/shard_map/attend_back/pallas_call | solution.py:1137
  425.8 3.0 fusion.170
  430.2 5.2 collective-permute-done.20
  436.9 20.2 %collective-permute-done.22 = bf16[512,1024]{1,0:T(8,128)(2,1)} collective-permute-done((bf16[512,1024]{1,0:T(8,128)(2,1)}, bf16[512,1024]{1,0:T(8,128)(2,1)}, u32[]{:S(2)}, u32[]{:S(2)}) %collective-permute-start.22) | collective-permute-done | bytes 1048608 | tf_op jit(solution)/shard_map/ppermute | solution.py:1382
  458.4 2.7 fusion.180
  461.1 2.8 fusion.177
  463.9 2.7 fusion.174
  466.6 2.6 fusion.171
  473.2 13.0 %attend_back.5 = (bf16[1024,256]{1,0:T(8,128)(2,1)S(1)}, bf16[1024,256]{1,0:T(8,128)(2,1)S(1)}, bf16[1024,256]{1,0:T(8,128)(2,1)S(1)}) custom-call(s32[1]{0:T(128)} %bitcast.1.flag_ref, bf16[1024,1536]{1,0:T(8,128)(2,1)} %add_convert_fusion.1.q_ref.k_ref.v_ref, bf16[1024,1536]{1,0:T(8,128)(2,1)} %add_convert_fusion.1.q_ref.k_ref.v_ref, ...), custom_call_target="tpu_custom_call" | custom-call | flops 20000000000 | bytes 5000000 | tf_op jit(solution)/shard_map/attend_back/pallas_call | solution.py:1137
  486.3 7.3 %collective-permute-done.26 = bf16[256,1024]{1,0:T(8,128)(2,1)} collective-permute-done((bf16[256,1024]{1,0:T(8,128)(2,1)}, bf16[256,1024]{1,0:T(8,128)(2,1)}, u32[]{:S(2)}, u32[]{:S(2)}) %collective-permute-start.26) | collective-permute-done | bytes 524320 | tf_op jit(solution)/shard_map/ppermute | solution.py:1390
  520.3 6.8 %collective-permute-done.29 = bf16[512,256]{1,0:T(8,128)(2,1)S(1)} collective-permute-done((bf16[512,256]{1,0:T(8,128)(2,1)S(1)}, bf16[512,256]{1,0:T(8,128)(2,1)S(1)}, u32[]{:S(2)}, u32[]{:S(2)}) %collective-permute-start.29) | collective-permute-done | bytes 262176 | tf_op jit(solution)/shard_map/ppermute | solution.py:1407
  527.3 2.8 add_convert_fusion.2.refs_8_
  530.1 77.8 %shard_map.306 = (f32[256,128]{1,0:T(8,128)S(1)}, f32[128,256]{1,0:T(8,128)S(1)}, f32[128,256]{1,0:T(8,128)S(1)}, f32[128,256]{1,0:T(8,128)S(1)}, f32[128,1024]{...) custom-call(bf16[512,1024]{1,0:T(8,128)(2,1)S(1)} %add_convert_fusion.10.refs_0_, ...), custom_call_target="tpu_custom_call" | custom-call | tf_op jit(solution)/shard_map/pallas_call | solution.py:985
  608.0 2.7 fusion.202
  (432 shorter events, 124.2 us)
Async XLA Ops:
  9.9 129.7 %copy-start.63 = (s32[1,2048]{1,0:T(1,128)S(1)}, s32[1,2048]{1,0:T(1,128)}, u32[]{:S(2)}) copy-start(s32[1,2048]{1,0:T(1,128)} %param.34) | copy-start | bytes 24580
  139.5 7.1 %collective-permute-start = (bf16[512,1024]{1,0:T(8,128)(2,1)}, bf16[512,1024]{1,0:T(8,128)(2,1)S(1)}, u32[]{:S(2)}, u32[]{:S(2)}) collective-permute-start(bf16[512,1024]{1,0:T(8,128)(2,1)} %get-tuple-element.73), channel_id=1, source_target_pairs={{0,4},{4,0},{8,12},{12,8},{16,20},{20,16},{24,28},{28,24},{1,5},{5... | collective-permute-start | bytes 3145736 | tf_op jit(solution)/shard_map/ppermute | solution.py:1226
  139.5 3.6 collective-permute-start.1
  146.5 64.2 %copy-start.2 = (s32[1,1024]{0,1:T(8,128)}, s32[1,1024]{0,1:T(8,128)S(1)}, u32[]{:S(2)}) copy-start(s32[1,1024]{0,1:T(8,128)S(1)} %copy.53) | copy-start | bytes 12292
  155.3 13.2 %copy-start.95 = (bf16[512,1024]{1,0:T(8,128)(2,1)S(1)}, bf16[512,1024]{1,0:T(8,128)(2,1)}, u32[]{:S(2)}) copy-start(bf16[512,1024]{1,0:T(8,128)(2,1)} %get-tuple-element.77) | copy-start | bytes 3145732
  169.2 2.7 collective-permute-start.2
  173.1 24.9 %copy-start.64 = (f32[512]{0:T(512)}, f32[512]{0:T(512)S(1)}, u32[]{:S(2)}) copy-start(f32[512]{0:T(512)S(1)} %get-tuple-element.221) | copy-start | bytes 6148
  173.1 24.9 %copy-start.66 = (f32[512]{0:T(512)}, f32[512]{0:T(512)S(1)}, u32[]{:S(2)}) copy-start(f32[512]{0:T(512)S(1)} %get-tuple-element.222) | copy-start | bytes 6148
  173.5 2.7 collective-permute-start.3
  177.2 13.9 %copy-start.87 = (bf16[2048,1024]{1,0:T(8,128)(2,1)S(1)}, bf16[2048,1024]{1,0:T(8,128)(2,1)}, u32[]{:S(2)}) copy-start(bf16[2048,1024]{1,0:T(8,128)(2,1)} %get-tuple-element.80) | copy-start | bytes 12582916
  195.3 2.7 collective-permute-start.4
  201.0 26.8 %copy-start.21 = (f32[512,1024]{1,0:T(8,128)}, f32[512,1024]{1,0:T(8,128)S(1)}, u32[]{:S(2)}) copy-start(f32[512,1024]{1,0:T(8,128)S(1)} %get-tuple-element.224) | copy-start | bytes 6291460
  201.4 9.4 %copy-start.47 = (bf16[512,1024]{1,0:T(8,128)(2,1)}, bf16[512,1024]{1,0:T(8,128)(2,1)S(1)}, u32[]{:S(2)}) copy-start(bf16[512,1024]{1,0:T(8,128)(2,1)S(1)} %fusion.24) | copy-start | bytes 3145732
  201.4 2.7 collective-permute-start.5
  210.8 13.5 %copy-start.96 = (bf16[512,1024]{1,0:T(8,128)(2,1)S(1)}, bf16[512,1024]{1,0:T(8,128)(2,1)}, u32[]{:S(2)}) copy-start(bf16[512,1024]{1,0:T(8,128)(2,1)} %get-tuple-element.77) | copy-start | bytes 3145732
  225.0 2.7 collective-permute-start.6
  229.0 24.8 %copy-start.23 = (f32[512,1024]{1,0:T(8,128)}, f32[512,1024]{1,0:T(8,128)S(1)}, u32[]{:S(2)}) copy-start(f32[512,1024]{1,0:T(8,128)S(1)} %get-tuple-element.225) | copy-start | bytes 6291460
  229.5 34.7 %copy-start.19 = (bf16[512,1024]{1,0:T(8,128)(2,1)}, bf16[512,1024]{1,0:T(8,128)(2,1)S(1)}, u32[]{:S(2)}) copy-start(bf16[512,1024]{1,0:T(8,128)(2,1)S(1)} %fusion.25) | copy-start | bytes 3145732
  229.5 2.7 collective-permute-start.7
  251.1 2.7 collective-permute-start.8
  260.7 4.2 collective-permute-start.13
  275.8 17.9 %collective-permute-start.14 = (bf16[512,1024]{1,0:T(8,128)(2,1)S(1)}, bf16[512,1024]{1,0:T(8,128)(2,1)S(1)}, u32[]{:S(2)}, u32[]{:S(2)}) collective-permute-start(bf16[512,1024]{1,0:T(8,128)(2,1)S(1)} %fusion.94), channel_id=1, source_target_pairs={{0,4},{4,0},{8,12},{12,8},{16,20},{20,16},{24,28},{28,24},{1,5},{5... | collective-permute-start | bytes 3145736 | tf_op jit(solution)/shard_map/ppermute | solution.py:1226
  299.7 8.2 %collective-permute-start.15 = (bf16[512,1024]{1,0:T(8,128)(2,1)S(1)}, bf16[512,1024]{1,0:T(8,128)(2,1)S(1)}, u32[]{:S(2)}, u32[]{:S(2)}) collective-permute-start(bf16[512,1024]{1,0:T(8,128)(2,1)S(1)} %get-tuple-element.162), channel_id=1, source_target_pairs={{0,4},{4,0},{8,12},{12,8},{16,20},{20,16},{24,28},{28,24},{1,5},{5... | collective-permute-start | bytes 3145736 | tf_op jit(solution)/shard_map/ppermute | solution.py:1226
  337.3 25.1 %collective-permute-start.16 = (bf16[512,1024]{1,0:T(8,128)(2,1)S(1)}, bf16[512,1024]{1,0:T(8,128)(2,1)S(1)}, u32[]{:S(2)}, u32[]{:S(2)}) collective-permute-start(bf16[512,1024]{1,0:T(8,128)(2,1)S(1)} %fusion.82), channel_id=1, source_target_pairs={{0,4},{4,0},{8,12},{12,8},{16,20},{20,16},{24,28},{28,24},{1,5},{5... | collective-permute-start | bytes 3145736 | tf_op jit(solution)/shard_map/ppermute | solution.py:1226
  339.4 12.1 %collective-permute-start.9 = (bf16[512,256]{1,0:T(8,128)(2,1)S(1)}, bf16[512,256]{1,0:T(8,128)(2,1)S(1)}, u32[]{:S(2)}, u32[]{:S(2)}) collective-permute-start(bf16[512,256]{1,0:T(8,128)(2,1)S(1)} %get-tuple-element.182), channel_id=1, source_target_pairs={{0,3},{1,1},{2,7},{3,5},{4,0},{5,2},{6,4},{7,6},{8,11},{9,9},{10,1... | collective-permute-start | bytes 786440 | tf_op jit(solution)/shard_map/ppermute | solution.py:1423
  344.8 12.3 %collective-permute-start.10 = (bf16[512,256]{1,0:T(8,128)(2,1)S(1)}, bf16[512,256]{1,0:T(8,128)(2,1)S(1)}, u32[]{:S(2)}, u32[]{:S(2)}) collective-permute-start(bf16[512,256]{1,0:T(8,128)(2,1)S(1)} %get-tuple-element.181), channel_id=1, source_target_pairs={{0,2},{1,0},{2,6},{3,4},{4,3},{5,1},{6,7},{7,5},{8,10},{9,8},{10,1... | collective-permute-start | bytes 786440 | tf_op jit(solution)/shard_map/ppermute | solution.py:1423
  345.2 17.1 %collective-permute-start.11 = (bf16[512,256]{1,0:T(8,128)(2,1)S(1)}, bf16[512,256]{1,0:T(8,128)(2,1)S(1)}, u32[]{:S(2)}, u32[]{:S(2)}) collective-permute-start(bf16[512,256]{1,0:T(8,128)(2,1)S(1)} %get-tuple-element.180), channel_id=1, source_target_pairs={{0,1},{1,3},{2,5},{3,7},{4,2},{5,0},{6,6},{7,4},{8,9},{9,11},{10,1... | collective-permute-start | bytes 786440 | tf_op jit(solution)/shard_map/ppermute | solution.py:1423
  350.5 11.8 %copy-start.22 = (f32[512,1024]{1,0:T(8,128)S(1)}, f32[512,1024]{1,0:T(8,128)}, u32[]{:S(2)}) copy-start(f32[512,1024]{1,0:T(8,128)} %copy-done.21) | copy-start | bytes 6291460
  350.6 11.8 %collective-permute-start.12 = (bf16[512,256]{1,0:T(8,128)(2,1)S(1)}, bf16[512,256]{1,0:T(8,128)(2,1)S(1)}, u32[]{:S(2)}, u32[]{:S(2)}) collective-permute-start(bf16[512,256]{1,0:T(8,128)(2,1)S(1)} %get-tuple-element.179), channel_id=1, source_target_pairs={{0,0},{1,2},{2,4},{3,6},{4,1},{5,3},{6,5},{7,7},{8,8},{9,10},{10,1... | collective-permute-start | bytes 786440 | tf_op jit(solution)/shard_map/ppermute | solution.py:1423
  367.0 7.4 %collective-permute-start.17 = (bf16[512,1024]{1,0:T(8,128)(2,1)S(1)}, bf16[512,1024]{1,0:T(8,128)(2,1)S(1)}, u32[]{:S(2)}, u32[]{:S(2)}) collective-permute-start(bf16[512,1024]{1,0:T(8,128)(2,1)S(1)} %get-tuple-element.154), channel_id=1, source_target_pairs={{0,4},{4,0},{8,12},{12,8},{16,20},{20,16},{24,28},{28,24},{1,5},{5... | collective-permute-start | bytes 3145736 | tf_op jit(solution)/shard_map/ppermute | solution.py:1226
  385.4 10.1 %collective-permute-start.18 = (bf16[512,1024]{1,0:T(8,128)(2,1)}, bf16[512,1024]{1,0:T(8,128)(2,1)}, u32[]{:S(2)}, u32[]{:S(2)}) collective-permute-start(bf16[512,1024]{1,0:T(8,128)(2,1)} %fusion.97), channel_id=1, source_target_pairs={{0,4},{4,0},{8,12},{12,8},{16,20},{20,16},{24,28},{28,24},{1,5},{5... | collective-permute-start | bytes 3145736 | tf_op jit(solution)/shard_map/ppermute | solution.py:1226
  400.1 7.5 %collective-permute-start.19 = (bf16[512,1024]{1,0:T(8,128)(2,1)S(1)}, bf16[512,1024]{1,0:T(8,128)(2,1)S(1)}, u32[]{:S(2)}, u32[]{:S(2)}) collective-permute-start(bf16[512,1024]{1,0:T(8,128)(2,1)S(1)} %get-tuple-element.159), channel_id=1, source_target_pairs={{0,4},{4,0},{8,12},{12,8},{16,20},{20,16},{24,28},{28,24},{1,5},{5... | collective-permute-start | bytes 3145736 | tf_op jit(solution)/shard_map/ppermute | solution.py:1226
  409.0 26.4 %collective-permute-start.20 = (bf16[1024,512]{1,0:T(8,128)(2,1)}, bf16[1024,512]{1,0:T(8,128)(2,1)}, u32[]{:S(2)}, u32[]{:S(2)}) collective-permute-start(bf16[1024,512]{1,0:T(8,128)(2,1)} %add_convert_fusion.9), channel_id=1, source_target_pairs={{0,16},{4,20},{8,24},{12,28},{16,0},{20,4},{24,8},{28,12},{1,17},{... | collective-permute-start | bytes 3145736 | tf_op jit(solution)/shard_map/ppermute | solution.py:1382
  410.5 26.3 %collective-permute-start.21 = (bf16[1024,512]{1,0:T(8,128)(2,1)}, bf16[1024,512]{1,0:T(8,128)(2,1)}, u32[]{:S(2)}, u32[]{:S(2)}) collective-permute-start(bf16[1024,512]{1,0:T(8,128)(2,1)} %add_convert_fusion.8), channel_id=1, source_target_pairs={{0,8},{4,12},{8,0},{12,4},{16,24},{20,28},{24,16},{28,20},{1,9},{5... | collective-permute-start | bytes 3145736 | tf_op jit(solution)/shard_map/ppermute | solution.py:1382
  411.1 46.0 %collective-permute-start.22 = (bf16[512,1024]{1,0:T(8,128)(2,1)}, bf16[512,1024]{1,0:T(8,128)(2,1)}, u32[]{:S(2)}, u32[]{:S(2)}) collective-permute-start(bf16[512,1024]{1,0:T(8,128)(2,1)} %add_convert_fusion.7), channel_id=1, source_target_pairs={{0,16},{4,20},{8,24},{12,28},{16,0},{20,4},{24,8},{28,12},{1,17},{... | collective-permute-start | bytes 3145736 | tf_op jit(solution)/shard_map/ppermute | solution.py:1382
  412.6 45.8 %collective-permute-start.23 = (bf16[512,1024]{1,0:T(8,128)(2,1)}, bf16[512,1024]{1,0:T(8,128)(2,1)}, u32[]{:S(2)}, u32[]{:S(2)}) collective-permute-start(bf16[512,1024]{1,0:T(8,128)(2,1)} %add_convert_fusion.6), channel_id=1, source_target_pairs={{0,8},{4,12},{8,0},{12,4},{16,24},{20,28},{24,16},{28,20},{1,9},{5... | collective-permute-start | bytes 3145736 | tf_op jit(solution)/shard_map/ppermute | solution.py:1382
  413.1 12.7 %copy-start.6 = (bf16[1024,512]{1,0:T(8,128)(2,1)S(1)}, bf16[1024,512]{1,0:T(8,128)(2,1)}, u32[]{:S(2)}) copy-start(bf16[1024,512]{1,0:T(8,128)(2,1)} %copy-done.5) | copy-start | bytes 3145732
  428.9 29.5 %copy-start.62 = (bf16[1024,256]{1,0:T(8,128)(2,1)S(1)}, bf16[1024,256]{1,0:T(8,128)(2,1)}, u32[]{:S(2)}) copy-start(bf16[1024,256]{1,0:T(8,128)(2,1)} %copy-done.61) | copy-start | bytes 1572868
  428.9 29.5 %copy-start.105 = (bf16[1024,2048]{1,0:T(8,128)(2,1)S(1)}, bf16[1024,2048]{1,0:T(8,128)(2,1)}, u32[]{:S(2)}) copy-start(bf16[1024,2048]{1,0:T(8,128)(2,1)} %get-tuple-element.79) | copy-start | bytes 12582916
  428.9 29.5 %copy-start.109 = (f32[1024,256]{1,0:T(8,128)S(1)}, f32[1024,256]{1,0:T(8,128)}, u32[]{:S(2)}) copy-start(f32[1024,256]{1,0:T(8,128)} %fusion.64) | copy-start | bytes 3145732
  469.2 17.1 %collective-permute-start.24 = (bf16[1024,256]{1,0:T(8,128)(2,1)}, bf16[1024,256]{1,0:T(8,128)(2,1)}, u32[]{:S(2)}, u32[]{:S(2)}) collective-permute-start(bf16[1024,256]{1,0:T(8,128)(2,1)} %fusion.180), channel_id=1, source_target_pairs={{0,8},{4,12},{8,0},{12,4},{16,24},{20,28},{24,16},{28,20},{1,9},{5... | collective-permute-start | bytes 1572872 | tf_op jit(solution)/shard_map/ppermute | solution.py:1390
  469.7 16.6 %collective-permute-start.25 = (bf16[1024,256]{1,0:T(8,128)(2,1)}, bf16[1024,256]{1,0:T(8,128)(2,1)}, u32[]{:S(2)}, u32[]{:S(2)}) collective-permute-start(bf16[1024,256]{1,0:T(8,128)(2,1)} %fusion.177), channel_id=1, source_target_pairs={{0,16},{4,20},{8,24},{12,28},{16,0},{20,4},{24,8},{28,12},{1,17},{... | collective-permute-start | bytes 1572872 | tf_op jit(solution)/shard_map/ppermute | solution.py:1390
  471.2 22.4 %collective-permute-start.26 = (bf16[256,1024]{1,0:T(8,128)(2,1)}, bf16[256,1024]{1,0:T(8,128)(2,1)}, u32[]{:S(2)}, u32[]{:S(2)}) collective-permute-start(bf16[256,1024]{1,0:T(8,128)(2,1)} %fusion.174), channel_id=1, source_target_pairs={{0,8},{4,12},{8,0},{12,4},{16,24},{20,28},{24,16},{28,20},{1,9},{5... | collective-permute-start | bytes 1572872 | tf_op jit(solution)/shard_map/ppermute | solution.py:1390
  471.7 22.2 %collective-permute-start.27 = (bf16[256,1024]{1,0:T(8,128)(2,1)}, bf16[256,1024]{1,0:T(8,128)(2,1)}, u32[]{:S(2)}, u32[]{:S(2)}) collective-permute-start(bf16[256,1024]{1,0:T(8,128)(2,1)} %fusion.171), channel_id=1, source_target_pairs={{0,16},{4,20},{8,24},{12,28},{16,0},{20,4},{24,8},{28,12},{1,17},{... | collective-permute-start | bytes 1572872 | tf_op jit(solution)/shard_map/ppermute | solution.py:1390
  504.3 16.0 %collective-permute-start.30 = (bf16[512,256]{1,0:T(8,128)(2,1)S(1)}, bf16[512,256]{1,0:T(8,128)(2,1)S(1)}, u32[]{:S(2)}, u32[]{:S(2)}) collective-permute-start(bf16[512,256]{1,0:T(8,128)(2,1)S(1)} %pad_maximum_fusion.15), channel_id=1, source_target_pairs={{0,3},{1,0},{2,1},{3,2},{4,7},{5,4},{6,5},{7,6},{8,11},{9,8},{10,9... | collective-permute-start | bytes 786440 | tf_op jit(solution)/shard_map/ppermute | solution.py:1407
  504.4 22.7 %collective-permute-start.29 = (bf16[512,256]{1,0:T(8,128)(2,1)S(1)}, bf16[512,256]{1,0:T(8,128)(2,1)S(1)}, u32[]{:S(2)}, u32[]{:S(2)}) collective-permute-start(bf16[512,256]{1,0:T(8,128)(2,1)S(1)} %pad_maximum_fusion.14), channel_id=1, source_target_pairs={{0,2},{1,3},{2,0},{3,1},{4,6},{5,7},{6,4},{7,5},{8,10},{9,11},{10,... | collective-permute-start | bytes 786440 | tf_op jit(solution)/shard_map/ppermute | solution.py:1407
  505.9 21.2 %collective-permute-start.28 = (bf16[512,256]{1,0:T(8,128)(2,1)S(1)}, bf16[512,256]{1,0:T(8,128)(2,1)S(1)}, u32[]{:S(2)}, u32[]{:S(2)}) collective-permute-start(bf16[512,256]{1,0:T(8,128)(2,1)S(1)} %pad_maximum_fusion.13), channel_id=1, source_target_pairs={{0,1},{1,2},{2,3},{3,0},{4,5},{5,6},{6,7},{7,4},{8,9},{9,10},{10,1... | collective-permute-start | bytes 786440 | tf_op jit(solution)/shard_map/ppermute | solution.py:1407
  509.9 17.4 %collective-permute-start.31 = (bf16[512,1024]{1,0:T(8,128)(2,1)S(1)}, bf16[512,1024]{1,0:T(8,128)(2,1)S(1)}, u32[]{:S(2)}, u32[]{:S(2)}) collective-permute-start(bf16[512,1024]{1,0:T(8,128)(2,1)S(1)} %fusion.85), channel_id=1, source_target_pairs={{0,4},{4,0},{8,12},{12,8},{16,20},{20,16},{24,28},{28,24},{1,5},{5... | collective-permute-start | bytes 3145736 | tf_op jit(solution)/shard_map/ppermute | solution.py:1226
  (99 other events, 351.4 us)

commit v3 on v2

--- a/solution.py
+++ b/solution.py
@@ -715,12 +715,12 @@
 
 
 SHAPES = ((256, 256), (128, 512), (128, 512), (128, 512))
-UNITS = ((128, 256), (256, 128), (256, 128), (256, 128), (256, 256), (256, 256))
+UNITS = ((128, 256), (256, 128), (256, 128), (256, 128))
 FULLS = ((512, 256), (256, 512), (256, 512), (256, 512))
 OUTS = ((256, 128), (128, 256), (128, 256), (128, 256), (128, 1024), (1024, 128))
-HALVES = ((128, 128), (128, 128), (128, 128), (128, 128), (128, 256), (128, 256), (512, 128))
-BY_COLS = (True, False, False, False, False, False)
-OUTER = 6
+HALVES = ((128, 128), (128, 128), (128, 128), (128, 128), (128, 512), (512, 128))
+BY_COLS = (True, False, False, False)
+INNER, OUTER = 4, 5
 
 
 def add_rows(dst, terms):
@@ -740,18 +740,17 @@
 
 def scatter_kernel(*refs):
     grads = refs[0:4]
-    inner_ref = refs[4:6]
-    outer_ref, small_ref, gi_ref = refs[6:9]
-    outs = refs[9:15]
-    small_out, gi_out = refs[15:17]
-    rest = list(refs[17:])
+    inner_ref, outer_ref, small_ref, gi_ref = refs[4:8]
+    outs = refs[8:14]
+    small_out, gi_out = refs[14:16]
+    rest = list(refs[16:])
     own = [[rest.pop(0) for _ in range(2)] for _ in range(4)]
     got1 = [[rest.pop(0) for _ in range(2)] for _ in range(4)]
     got2 = [[rest.pop(0) for _ in range(2)] for _ in range(4)]
     full = [rest.pop(0) for _ in range(4)]
-    zgot = [rest.pop(0) for _ in range(6)]
-    fin = [rest.pop(0) for _ in range(6)]
-    cgot = [rest.pop(0) for _ in range(7)]
+    zgot = [rest.pop(0) for _ in range(4)]
+    fin = [rest.pop(0) for _ in range(4)]
+    cgot = [rest.pop(0) for _ in range(6)]
     sb = rest.pop(0)
     sg = rest.pop(0)
     (o_s, p1_s, p1_r, p2_s, p2_r, z_s, z_r, c_s, c_r, sm_s, sm_r, t_s, t_r, t_l) = rest
@@ -769,8 +768,6 @@
         return grads[group].at[span(block * 256 + part * 128, 128), :]
 
     def unit(group, z):
-        if group >= 4:
-            return inner_ref[group - 4].at[:, span(z * 256, 256)]
         if BY_COLS[group]:
             return full[group].at[span(z * UNITS[group][0], UNITS[group][0]), :]
         return full[group].at[:, span(z * UNITS[group][1], UNITS[group][1])]
@@ -778,6 +775,8 @@
     def side(group, half):
         if group == OUTER:
             return outer_ref.at[:, span(half * 128, 128)]
+        if group == INNER:
+            return inner_ref.at[span(half * 128, 128), :]
         if BY_COLS[group]:
             return fin[group].at[:, span(half * 128, 128)]
         return fin[group].at[span(half * 128, 128), :]
@@ -785,8 +784,8 @@
     def out_side(group, half):
         if group == OUTER:
             return outs[5].at[span(half * 512, 512), :]
-        if group >= 4:
-            return outs[4].at[:, span(half * 512 + (group - 4) * 256, 256)]
+        if group == INNER:
+            return outs[4].at[:, span(half * 512, 512)]
         size = HALVES[group]
         if BY_COLS[group]:
             return outs[group].at[span(half * size[0], size[0]), :]
@@ -929,12 +928,12 @@
         start_first(group)
     small_send(0, 0, mate, depth)
     send_core(OUTER)
-    send_depth(4)
-    send_depth(5)
+    send_core(INNER)
     token_copies(0, gi_ref, gi_out)
     small_add(0, 0)
     small_send(1, 1, x_row, depth)
     finish(OUTER)
+    finish(INNER)
     for group in range(4):
         start_second(group)
         if group == 0:
@@ -946,14 +945,12 @@
     for k in (1, 2, 3):
         small_send(3, 2 + k, row, (depth + k) % 4)
     start_depth(3)
-    for group in (4, 5):
-        start_core(group)
     for group in (0, 1, 2):
         start_core(group)
     for k in (1, 2, 3):
         copies["s", 2 + k].wait_recv()
     small_out[...] = ((sb[3] + sg[3]) + sg[4]) + sg[5]
-    for group in (4, 5, 0, 1, 2):
+    for group in (0, 1, 2):
         finish(group)
     start_core(3)
     token_waits(0, gi_ref, gi_out)
@@ -963,7 +960,7 @@
             cp.wait_send()
 
 
-def scatter_all(proj, q, k, v, inner_a, inner_b, outer, small, gi):
+def scatter_all(proj, q, k, v, inner, outer, small, gi):
     sd = jax.ShapeDtypeStruct
     scratch = []
     for size in SHAPES:
@@ -979,20 +976,20 @@
     scratch += [pltpu.VMEM((4,) + small.shape, F32), pltpu.VMEM((6,) + small.shape, F32)]
     scratch += [
         DMA((4, 2, 2)), DMA((4, 2, 2)), DMA((4, 2, 2)), DMA((4, 2)), DMA((4, 2)),
-        DMA((6, 3)), DMA((6, 3)), DMA((7,)), DMA((7,)), DMA((6,)), DMA((6,)),
+        DMA((4, 3)), DMA((4, 3)), DMA((6,)), DMA((6,)), DMA((6,)), DMA((6,)),
         DMA((1, 4)), DMA((1, 4)), DMA((1,)),
     ]
     return pl.pallas_call(
         scatter_kernel,
         out_shape=tuple(sd(size, F32) for size in OUTS)
         + (sd(small.shape, F32), sd((2048, 256), BF16)),
-        in_specs=[ANY] * 4 + [VMEM] * 4 + [ANY],
+        in_specs=[ANY] * 4 + [VMEM] * 3 + [ANY],
         out_specs=[VMEM] * 7 + [ANY],
         scratch_shapes=scratch,
         compiler_params=pltpu.CompilerParams(
             collective_id=2, has_side_effects=True, vmem_limit_bytes=48 * 1024 * 1024
         ),
-    )(proj, q, k, v, inner_a, inner_b, outer, small, gi)
+    )(proj, q, k, v, inner, outer, small, gi)
 
 
 def attend_kernel(flag_ref, q_ref, k_ref, v_ref, idq_ref, idk_ref, o_ref, lse_ref):
@@ -1231,9 +1228,11 @@
 
 
 def share_sum(left, weight, product):
-    mate_part = rounded(product(left[512:], weight))
+    mate_part, left_own = lax.optimization_barrier(
+        (rounded(product(left[512:], weight)), left[:512])
+    )
     other = exchange(mate_part)
-    return product(left[:512], weight) + other.astype(F32)
+    return product(left_own, weight) + other.astype(F32)
 
 
 def norm_rows(summed, gain, shift):
@@ -1275,7 +1274,7 @@
     return output, kept
 
 
-def fast_backward(grad_output, kept, weights, vectors, ids, later=None):
+def fast_backward(grad_output, kept, weights, vectors, ids, later=None, beside=None):
     (
         whole_in, qkv, lse, attended, normed_one, inverse_one,
         whole_mid, active, slope, normed_two, inverse_two,
@@ -1288,10 +1287,15 @@
     ffn_low = rounded(grad_second)
     whole_second = both(ffn_low)
     inner_low = rounded(against(whole_second, wouter) * slope.astype(F32))
-    relative_second = by_place(whole_second)
-    outer_terms = outer_pieces(active, relative_second)
+    outer_terms = outer_pieces(active, by_place(whole_second))
+    if later is not None:
+        outer_planes = [Plane(add_trees(outer_terms, later[0]), h, 1) for h in (0, 1)]
+        outer_got = [p.step_one() for p in outer_planes]
     grad_first = grad_second + share_sum(inner_low, winner, against)
     inner_terms = inner_pieces(by_place(whole_mid), inner_low)
+    if later is not None:
+        inner_planes = [Plane(add_trees(inner_terms, later[1]), h, 0) for h in (0, 1)]
+        inner_got = [p.step_one() for p in inner_planes]
     grad_attn, attn_gain_sum, attn_shift_sum = norm_rows_back(
         grad_first, normed_one, inverse_one, vectors["attn_gain"]
     )
@@ -1301,24 +1305,22 @@
     proj_term = over_tokens(attended, whole_attn)
     if later is None:
         grads = attend_back(flag, qkv, mixed_grad, lse, id_col, id_row)
+        if beside is not None:
+            beside, grads = lax.optimization_barrier((beside, grads))
+        outer_terms, inner_terms = (outer_terms, inner_terms), beside
     else:
-        outer_terms = add_trees(outer_terms, later[0])
-        inner_terms = add_trees(inner_terms, later[1])
-        planes = [Plane(outer_terms, h, 1) for h in (0, 1)] + [
-            Plane(inner_terms, h, 0) for h in (0, 1)
-        ]
-        sent, mixed_grad = lax.optimization_barrier(([p.sent for p in planes], mixed_grad))
-        got = [p.step_one(s) for p, s in zip(planes, sent)]
         early = attend_back(flag, qkv, mixed_grad, lse, id_col, id_row, 0, 2)
-        got, early = lax.optimization_barrier((got, early))
-        handed = [p.to_hand(g) for p, g in zip(planes, got)]
-        handed, mixed_grad = lax.optimization_barrier((handed, mixed_grad))
-        more = [p.step_two(v) for p, v in zip(planes, handed)]
+        outer_got, early = lax.optimization_barrier((outer_got, early))
+        outer_hand = [p.to_hand(g) for p, g in zip(outer_planes, outer_got)]
+        outer_hand, mixed_grad = lax.optimization_barrier((outer_hand, mixed_grad))
+        outer_more = [p.step_two(v) for p, v in zip(outer_planes, outer_hand)]
         late = attend_back(flag, qkv, mixed_grad, lse, id_col, id_row, 2, 2)
-        more, late = lax.optimization_barrier((more, late))
-        folded = [p.close(m) for p, m in zip(planes, more)]
-        outer_terms = fold_depth(folded[:2])
-        inner_terms = folded[2:]
+        inner_got, late = lax.optimization_barrier((inner_got, late))
+        inner_hand = [p.to_hand(g) for p, g in zip(inner_planes, inner_got)]
+        inner_hand, outer_more, late = lax.optimization_barrier((inner_hand, outer_more, late))
+        inner_more = [p.step_two(v) for p, v in zip(inner_planes, inner_hand)]
+        outer_terms = fold_depth([p.close(m) for p, m in zip(outer_planes, outer_more)], 0)
+        inner_terms = fold_depth([p.close(m) for p, m in zip(inner_planes, inner_more)], 1)
         grads = tuple(jnp.concatenate(pair, axis=1) for pair in zip(early, late))
     grad_qkv = jnp.concatenate(grads, axis=1)
     grad_input = grad_attn + share_sum(grad_qkv, wqkv, against)
@@ -1378,8 +1380,8 @@
         self.half, self.axis = half, axis
         self.first, self.second = (4, 2) if half == 0 else (2, 4)
 
-    def step_one(self, sent):
-        return lax.ppermute(sent, "row", flip_row(self.first))
+    def step_one(self):
+        return lax.ppermute(self.sent, "row", flip_row(self.first))
 
     def to_hand(self, got):
         low, high = jnp.split(got, 2, axis=self.axis)
@@ -1393,13 +1395,12 @@
         return rounded(self.own + self.got.astype(F32) + more.astype(F32))
 
 
-def fold_depth(halves):
+def fold_depth(halves, axis):
     depth = lax.axis_index("col")
-    stacked = [half.reshape(4, 256, 256) for half in halves]
 
     def unit(z):
-        picked = [lax.dynamic_index_in_dim(s, z, 0, keepdims=False) for s in stacked]
-        return jnp.concatenate(picked, axis=0)
+        picked = [lax.dynamic_slice_in_dim(half, z * 256, 256, axis) for half in halves]
+        return jnp.concatenate(picked, axis=axis)
 
     total = unit(depth).astype(F32)
     for k in (1, 2, 3):
@@ -1408,7 +1409,7 @@
     return rounded(total)
 
 
-def spread_out(values, own_start):
+def spread_out(values):
     core = lax.axis_index("row") % 2
     depth = lax.axis_index("col")
     j = (depth % 2) * 2 + core
@@ -1421,6 +1422,11 @@
                 pairs.append((r * 4 + z, (r // 2 * 2 + z // 2) * 4 + block))
         piece = lax.dynamic_slice_in_dim(values, ((j + k) % 4) * 256, 256, 1)
         parts.append(lax.ppermute(piece, ("row", "col"), pairs))
+    return parts
+
+
+def join_parts(parts, own_start):
+    depth = lax.axis_index("col")
     cycle = jnp.concatenate(parts[::-1] * 2, axis=0)
     start = ((3 - depth) * 512 - own_start + 2048) % 2048
     return lax.dynamic_slice(cycle, (start, 0), (2048, 256)).astype(F32)
@@ -1509,12 +1515,13 @@
     middle, kept_one = fast_forward(start_low.astype(F32), weights, vectors, ids)
     final_out, kept_two = fast_forward(middle, weights, vectors, ids)
     grad_flow = grad_low.astype(F32)
-    grad_flow, terms_two, outer_two, inner_two, small_two = fast_backward(
-        grad_flow, kept_two, weights, vectors, ids
-    )
-    hidden_out = spread_out(rounded(final_out), own_start)
-    grad_flow, terms_one, outer_full, (inner_a, inner_b), small_one = fast_backward(
-        grad_flow, kept_one, weights, vectors, ids, (outer_two, inner_two)
+    parts = spread_out(rounded(final_out))
+    grad_flow, terms_two, ffn_two, parts, small_two = fast_backward(
+        grad_flow, kept_two, weights, vectors, ids, None, parts
+    )
+    hidden_out = join_parts(parts, own_start)
+    grad_flow, terms_one, outer_full, inner_full, small_one = fast_backward(
+        grad_flow, kept_one, weights, vectors, ids, ffn_two
     )
     terms = [rounded(a + b) for a, b in zip(terms_two, terms_one)]
     pieces = []
@@ -1532,7 +1539,7 @@
             )
         pieces.append(total.reshape(-1))
     small_sum = jnp.concatenate(pieces).reshape(96, 128)
-    results = scatter_all(*terms, inner_a, inner_b, outer_full, small_sum, rounded(grad_flow))
+    results = scatter_all(*terms, inner_full, outer_full, small_sum, rounded(grad_flow))
     proj_g, q_g, k_g, v_g, inner_g, outer_g, small_all, grad_turned = results
     small_all = small_all.reshape(-1)
     sums, offset = {}, 0

time: 622 us -> 589 us (0.947)
  waiting for transfers between devices: 70.8 us -> 52.8 us
  Pallas kernels: 311 us -> 295 us
    ppermute x4, waiting for transfers between devices: 28.2 us -> 6.06 us  [step_one(): return lax.ppermute(self.sent, 'row', flip_row(self.first))]
    ppermute x3 -> x6, waiting for transfers between devices: 6.82 us -> 25.6 us  [fold_depth(): lax.ppermute(unit((depth + k) % 4), 'col', pairs).astype(F32)]
    pallas_call x1, Pallas kernels: 77.8 us -> 60.5 us  [scatter_all(): pl.pallas_call(scatter_kernel, out_shape=tuple((sd(size, F32) for size in...]
    ppermute x4, waiting for transfers between devices: 10.9 us -> 0.01 us  [spread_out(): parts.append(lax.ppermute(piece, ('row', 'col'), pairs))]
    unnamed x269 -> x267, local copies, waits for them, and re-layouts: 21.1 us -> 20.9 us
  transfers between devices with their start and end apart: 32 -> 35, of which waited for: 18 -> 15; matrix products, arithmetic and copies ran while one was open for 11% -> 15% of each run, Pallas kernels for 4% -> 9%
where the time goes in v3:
time: 589 us; the launch traced here: 584 us
  Pallas kernels  295 us (50%)
  matrix products  138 us (23%)
  waiting for transfers between devices  52.8 us (9%)
  starting transfers between devices  31.7 us (5%)
  other arithmetic  30.4 us (5%)
  local copies, waits for them, and re-layouts  27.1 us (5%)
  between operations  9.05 us (2%)
    pallas_call x1, Pallas kernels, gather_all(): pl.pallas_call(gather_kernel, out_shape=(sd((1024, 1536), BF16), sd((512,...  130 us
    dot_general x32, matrix products, over_tokens(): lax.dot_general(left, right, (((0,), (0,)), ((), ())), preferred_element_...  66.3 us
    pallas_call x1, Pallas kernels, scatter_all(): pl.pallas_call(scatter_kernel, out_shape=tuple((sd(size, F32) for size in...  60.5 us
    pallas_call x3, Pallas kernels, attend_back(): pl.pallas_call(attend_back_kernel, out_shape=(shape, shape, shape), grid_...  50.2 us
    dot_general x12, matrix products, against(): lax.dot_general(left, right, (((1,), (1,)), ((), ())), preferred_element_...  40 us
    dot_general x10, matrix products, matmul(): return jnp.dot(left, right, preferred_element_type=jnp.float32)  31.9 us
    pallas_call x2, Pallas kernels, ffn_in(): pl.pallas_call(ffn_in_kernel, out_shape=(shape, shape), grid=(hidden // c...  27.6 us
    pallas_call x2, Pallas kernels, attend(): pl.pallas_call(attend_kernel, out_shape=(jax.ShapeDtypeStruct((tokens, wi...  26.6 us
  transfers between devices with their start and end apart: 35, of which 15 were waited for; matrix products, arithmetic and copies ran while one was open for 15% of the time, Pallas kernels for 9%

profile of v3, /device:TPU:0, one launch (start us, length us, event | category | flops | bytes accessed | tf_op | source)
XLA Modules:
  0.0 583.7 jit_solution(14186036575650486917)
XLA Ops:
  4.6 5.2 fusion.183
  9.8 129.7 %shard_map.305 = (bf16[1024,1536]{1,0:T(8,128)(2,1)}, bf16[512,1024]{1,0:T(8,128)(2,1)}, bf16[1024,2048]{1,0:T(8,128)(2,1)}, bf16[2048,1024]{1,0:T(8,128)(2,1)},...) custom-call(bf16[128,256]{1,0:T(8,128)(2,1)} %q_ref.1, bf16[128,256]{1,0:T(8,128)(2,1)} %k_ref.1, ...), custom_call_target="tpu_custom_call" | custom-call | tf_op jit(solution)/shard_map/pallas_call | solution.py:693
  147.7 7.6 %add_convert_fusion.1.q_ref.k_ref.v_ref = bf16[1024,1536]{1,0:T(8,128)(2,1)} fusion(bf16[1024,1024]{1,0:T(8,128)(2,1)} %constant_dynamic-update-slice_fusion.1, bf16[1024,1536]{1,0:T(8,128)(2,1)} %get-tuple-element.93, f32[1536]{0:T(1024)S(1)} %fusion.233), kind=kOutput, calls=%fused_computation.5 | convolution fusion | flops 3224371200 | bytes 8394752 | tf_op jit(solution)/shard_map/dot_general | solution.py:26
  155.3 13.1 %attend.2 = (bf16[1024,512]{1,0:T(8,128)(2,1)S(1)}, f32[1024,512]{1,0:T(8,128)S(1)}) custom-call(s32[1]{0:T(128)} %bitcast.1.flag_ref, bf16[1024,1536]{1,0:T(8,128)(2,1)} %add_convert_fusion.1.q_ref.k_ref.v_ref, bf16[1024,1536]{1,0:T(8,128)(2,1)} %add_convert_fusion.1.q_ref.k_ref.v_ref, bf16[1024,1536]{1,0:T(8,128)(2,1)} %add_convert_fusion.1.q_ref.k_ref.v_ref, ...), custom_call_target="tpu_custom_call" | custom-call | flops 20000000000 | bytes 8000000 | tf_op jit(solution)/shard_map/attend/pallas_call | solution.py:1049
  169.4 2.5 collective-permute-done.2
  177.3 13.7 %ffn_in.2 = (bf16[1024,2048]{1,0:T(8,128)(2,1)}, bf16[1024,2048]{1,0:T(8,128)(2,1)}) custom-call(bf16[1024,1024]{1,0:T(8,128)(2,1)S(1)} %pad_maximum_fusion.x_ref, bf16[1024,2048]{1,0:T(8,128)(2,1)} %get-tuple-element.99.w_ref, f32[1,2048]{1,0:T(1,128)S(1)} %reshape.240.b_ref), custom_call_target="tpu_custom_call" | custom-call | flops 14000000000 | bytes 14000000 | tf_op jit(solution)/shard_map/ffn_in/pallas_call | solution.py:1201
  193.9 4.7 fusion.76
  198.8 2.5 collective-permute-done.4
  201.3 3.0 fusion.261
  205.0 2.5 collective-permute-done.5
  208.5 5.6 add_convert_fusion.q_ref.k_ref.v_ref
  214.1 13.4 %attend.3 = (bf16[1024,512]{1,0:T(8,128)(2,1)S(1)}, f32[1024,512]{1,0:T(8,128)S(1)}) custom-call(s32[1]{0:T(128)} %bitcast.1.flag_ref, bf16[1024,1536]{1,0:T(8,128)(2,1)} %add_convert_fusion.q_ref.k_ref.v_ref, bf16[1024,1536]{1,0:T(8,128)(2,1)} %add_convert_fusion.q_ref.k_ref.v_ref, bf16[1024,1536]{1,0:T(8,128)(2,1)} %add_convert_fusion.q_ref.k_ref.v_ref, ...), custom_call_target="tpu_custom_call" | custom-call | flops 20000000000 | bytes 8000000 | tf_op jit(solution)/shard_map/attend/pallas_call | solution.py:1049
  228.6 2.5 collective-permute-done.6
  233.0 2.5 collective-permute-done.7
  236.6 13.9 %ffn_in.3 = (bf16[1024,2048]{1,0:T(8,128)(2,1)}, bf16[1024,2048]{1,0:T(8,128)(2,1)}) custom-call(bf16[1024,1024]{1,0:T(8,128)(2,1)S(1)} %pad_maximum_fusion.1.x_ref, bf16[1024,2048]{1,0:T(8,128)(2,1)} %get-tuple-element.99.w_ref, f32[1,2048]{1,0:T(1,128)S(1)} %reshape.240.b_ref), custom_call_target="tpu_custom_call" | custom-call | flops 14000000000 | bytes 14000000 | tf_op jit(solution)/shard_map/ffn_in/pallas_call | solution.py:1201
  250.6 4.1 fusion.79
  255.1 2.5 collective-permute-done.8
  257.6 3.0 fusion.259
  269.8 7.5 %convert_reduce_fusion.1 = (f32[2048]{0:T(1024)S(1)}, bf16[1024,2048]{1,0:T(8,128)(2,1)S(1)}) fusion(bf16[1024,2048]{1,0:T(8,128)(2,1)} %get-tuple-element.111, bf16[2048,1024]{1,0:T(8,128)(2,1)S(1)} %copy-done.96, bf16[512,1024]{1,0:T(8,128)(2,1)} %collective-permute-done.13, bf16[512,1024]{1,0:T(8,128)(2,1)} %get-tuple-element.195), kind=kOutput, calls=%fused_computation.1 | convolution fusion | flops 4309645312 | bytes 14688256 | tf_op jit(solution)/shard_map/dot_general | solution.py:36
  277.3 2.4 fusion.82
  288.9 2.8 fusion.42
  291.7 2.8 fusion.54
  294.5 2.6 fusion.32
  297.1 2.6 fusion.22
  300.3 6.4 %multiply_reduce_fusion.2 = (f32[1024]{0:T(1024)}, f32[512]{0:T(512)S(1)}, f32[512]{0:T(512)S(1)}, f32[1024]{0:T(1024)}, f32[512,1024]{1,0:T(8,128)S(1)}, /*index=5*/bf16[512,1024]{1,0:T(8,128)(2,1)S(1)}) fusion(f32[512,1024]{1,0:T(8,128)S(1)} %copy-done.27, f32[512]{0:T(512)S(1)} %get-tuple-element.269, f32[512]{0:T(512)S(1)} %get-tuple-element.268, ...), kind=kOutput, calls=%fused_computation.64 | convolution fusion | flops 2159539200 | bytes 15765504 | tf_op jit(solution)/shard_map/dot_general | solution.py:36
  310.1 2.7 fusion.58
  312.7 2.7 fusion.46
  316.3 2.8 collective-permute-start.10
  319.2 4.4 collective-permute-start.11
  323.6 4.4 collective-permute-start.12
  329.4 24.2 %attend_back.3 = (bf16[1024,512]{1,0:T(8,128)(2,1)S(1)}, bf16[1024,512]{1,0:T(8,128)(2,1)S(1)}, bf16[1024,512]{1,0:T(8,128)(2,1)S(1)}) custom-call(s32[1]{0:T(128)} %bitcast.1.flag_ref, bf16[1024,1536]{1,0:T(8,128)(2,1)} %add_convert_fusion.q_ref.k_ref.v_ref, bf16[1024,1536]{1,0:T(8,128)(2,1)} %add_convert_fusion.q_ref.k_ref.v_ref, ...), custom_call_target="tpu_custom_call" | custom-call | flops 40000000000 | bytes 10000000 | tf_op jit(solution)/shard_map/attend_back/pallas_call | solution.py:1134
  367.9 7.0 %convert_reduce_fusion = (f32[2048]{0:T(1024)S(1)}, bf16[1024,2048]{1,0:T(8,128)(2,1)S(1)}) fusion(bf16[1024,2048]{1,0:T(8,128)(2,1)} %get-tuple-element.127, bf16[2048,1024]{1,0:T(8,128)(2,1)S(1)} %copy-done.97, bf16[512,1024]{1,0:T(8,128)(2,1)S(1)} %collective-permute-done.17, bf16[512,1024]{1,0:T(8,128)(2,1)S(1)} %get-tuple-element.192), kind=kOutput, calls=%fused_computation | convolution fusion | flops 4309645312 | bytes 14688256 | tf_op jit(solution)/shard_map/dot_general | solution.py:36
  375.0 2.4 fusion.85
  384.5 2.4 fusion.266
  400.5 3.3 convolution_convert_fusion.do_ref
  403.8 12.8 %attend_back.4 = (bf16[1024,256]{1,0:T(8,128)(2,1)S(1)}, bf16[1024,256]{1,0:T(8,128)(2,1)S(1)}, bf16[1024,256]{1,0:T(8,128)(2,1)S(1)}) custom-call(s32[1]{0:T(128)} %bitcast.1.flag_ref, bf16[1024,1536]{1,0:T(8,128)(2,1)} %add_convert_fusion.1.q_ref.k_ref.v_ref, bf16[1024,1536]{1,0:T(8,128)(2,1)} %add_convert_fusion.1.q_ref.k_ref.v_ref, ...), custom_call_target="tpu_custom_call" | custom-call | flops 20000000000 | bytes 5000000 | tf_op jit(solution)/shard_map/attend_back/pallas_call | solution.py:1134
  416.6 2.9 collective-permute-done.21
  419.5 2.8 fusion.166
  422.3 2.6 fusion.163
  424.9 13.2 %attend_back.5 = (bf16[1024,256]{1,0:T(8,128)(2,1)S(1)}, bf16[1024,256]{1,0:T(8,128)(2,1)S(1)}, bf16[1024,256]{1,0:T(8,128)(2,1)S(1)}) custom-call(s32[1]{0:T(128)} %bitcast.1.flag_ref, bf16[1024,1536]{1,0:T(8,128)(2,1)} %add_convert_fusion.1.q_ref.k_ref.v_ref, bf16[1024,1536]{1,0:T(8,128)(2,1)} %add_convert_fusion.1.q_ref.k_ref.v_ref, ...), custom_call_target="tpu_custom_call" | custom-call | flops 20000000000 | bytes 5000000 | tf_op jit(solution)/shard_map/attend_back/pallas_call | solution.py:1134
  438.1 3.1 collective-permute-done.23
  447.1 3.0 fusion.156
  451.5 3.3 collective-permute-done.24
  482.5 3.2 collective-permute-start.30
  487.4 6.5 %collective-permute-done.32 = bf16[512,256]{1,0:T(8,128)(2,1)S(1)} collective-permute-done((bf16[512,256]{1,0:T(8,128)(2,1)S(1)}, bf16[512,256]{1,0:T(8,128)(2,1)S(1)}, u32[]{:S(2)}, u32[]{:S(2)}) %collective-permute-start.32) | collective-permute-done | bytes 262176 | tf_op jit(solution)/shard_map/ppermute | solution.py:1408
  495.7 17.5 %collective-permute-done.29 = bf16[256,512]{1,0:T(8,128)(2,1)S(1)} collective-permute-done((bf16[256,512]{1,0:T(8,128)(2,1)S(1)}, bf16[256,512]{1,0:T(8,128)(2,1)S(1)}, u32[]{:S(2)}, u32[]{:S(2)}) %collective-permute-start.29) | collective-permute-done | bytes 262176 | tf_op jit(solution)/shard_map/ppermute | solution.py:1408
  514.9 60.5 %shard_map.306 = (f32[256,128]{1,0:T(8,128)S(1)}, f32[128,256]{1,0:T(8,128)S(1)}, f32[128,256]{1,0:T(8,128)S(1)}, f32[128,256]{1,0:T(8,128)S(1)}, f32[128,1024]{...) custom-call(bf16[512,1024]{1,0:T(8,128)(2,1)S(1)} %add_convert_fusion.10.refs_0_, ...), custom_call_target="tpu_custom_call" | custom-call | tf_op jit(solution)/shard_map/pallas_call | solution.py:982
  575.4 2.6 fusion.182
  (452 shorter events, 125.1 us)
Async XLA Ops:
  9.8 129.8 %copy-start.70 = (s32[1,2048]{1,0:T(1,128)S(1)}, s32[1,2048]{1,0:T(1,128)}, u32[]{:S(2)}) copy-start(s32[1,2048]{1,0:T(1,128)} %param.34) | copy-start | bytes 24580
  139.5 7.1 %collective-permute-start = (bf16[512,1024]{1,0:T(8,128)(2,1)}, bf16[512,1024]{1,0:T(8,128)(2,1)S(1)}, u32[]{:S(2)}, u32[]{:S(2)}) collective-permute-start(bf16[512,1024]{1,0:T(8,128)(2,1)} %get-tuple-element.92), channel_id=1, source_target_pairs={{0,4},{4,0},{8,12},{12,8},{16,20},{20,16},{24,28},{28,24},{1,5},{5... | collective-permute-start | bytes 3145736 | tf_op jit(solution)/shard_map/ppermute | solution.py:1223
  139.6 3.6 collective-permute-start.1
  146.6 67.5 %copy-start.2 = (s32[1,1024]{0,1:T(8,128)}, s32[1,1024]{0,1:T(8,128)S(1)}, u32[]{:S(2)}) copy-start(s32[1,1024]{0,1:T(8,128)S(1)} %copy.53) | copy-start | bytes 12292
  169.3 2.7 collective-permute-start.2
  173.2 28.1 %copy-start.71 = (f32[512]{0:T(512)}, f32[512]{0:T(512)S(1)}, u32[]{:S(2)}) copy-start(f32[512]{0:T(512)S(1)} %get-tuple-element.272) | copy-start | bytes 6148
  173.2 28.1 %copy-start.73 = (f32[512]{0:T(512)}, f32[512]{0:T(512)S(1)}, u32[]{:S(2)}) copy-start(f32[512]{0:T(512)S(1)} %get-tuple-element.273) | copy-start | bytes 6148
  173.6 2.7 collective-permute-start.3
  198.6 2.7 collective-permute-start.4
  204.3 26.8 %copy-start.16 = (f32[512,1024]{1,0:T(8,128)}, f32[512,1024]{1,0:T(8,128)S(1)}, u32[]{:S(2)}) copy-start(f32[512,1024]{1,0:T(8,128)S(1)} %get-tuple-element.207) | copy-start | bytes 6291460
  204.8 2.7 collective-permute-start.5
  228.4 2.7 collective-permute-start.6
  232.4 25.2 %copy-start.26 = (f32[512,1024]{1,0:T(8,128)}, f32[512,1024]{1,0:T(8,128)S(1)}, u32[]{:S(2)}) copy-start(f32[512,1024]{1,0:T(8,128)S(1)} %get-tuple-element.206) | copy-start | bytes 6291460
  232.8 75.5 %copy-start.23 = (bf16[512,1024]{1,0:T(8,128)(2,1)}, bf16[512,1024]{1,0:T(8,128)(2,1)S(1)}, u32[]{:S(2)}) copy-start(bf16[512,1024]{1,0:T(8,128)(2,1)S(1)} %fusion.17) | copy-start | bytes 3145732
  232.8 2.7 collective-permute-start.7
  254.9 2.7 collective-permute-start.8
  264.4 4.2 collective-permute-start.13
  280.0 19.8 %collective-permute-start.14 = (bf16[512,1024]{1,0:T(8,128)(2,1)S(1)}, bf16[512,1024]{1,0:T(8,128)(2,1)S(1)}, u32[]{:S(2)}, u32[]{:S(2)}) collective-permute-start(bf16[512,1024]{1,0:T(8,128)(2,1)S(1)} %fusion.82), channel_id=1, source_target_pairs={{0,4},{4,0},{8,12},{12,8},{16,20},{20,16},{24,28},{28,24},{1,5},{5... | collective-permute-start | bytes 3145736 | tf_op jit(solution)/shard_map/ppermute | solution.py:1223
  308.2 19.8 %copy-start.34 = (bf16[512,1024]{1,0:T(8,128)(2,1)}, bf16[512,1024]{1,0:T(8,128)(2,1)S(1)}, u32[]{:S(2)}) copy-start(bf16[512,1024]{1,0:T(8,128)(2,1)S(1)} %get-tuple-element.200) | copy-start | bytes 3145732
  308.2 19.8 %collective-permute-start.15 = (bf16[512,1024]{1,0:T(8,128)(2,1)S(1)}, bf16[512,1024]{1,0:T(8,128)(2,1)S(1)}, u32[]{:S(2)}, u32[]{:S(2)}) collective-permute-start(bf16[512,1024]{1,0:T(8,128)(2,1)S(1)} %get-tuple-element.200), channel_id=1, source_target_pairs={{0,4},{4,0},{8,12},{12,8},{16,20},{20,16},{24,28},{28,24},{1,5},{5... | collective-permute-start | bytes 3145736 | tf_op jit(solution)/shard_map/ppermute | solution.py:1223
  315.5 38.1 %collective-permute-start.9 = (bf16[512,256]{1,0:T(8,128)(2,1)S(1)}, bf16[512,256]{1,0:T(8,128)(2,1)S(1)}, u32[]{:S(2)}, u32[]{:S(2)}) collective-permute-start(bf16[512,256]{1,0:T(8,128)(2,1)S(1)} %get-tuple-element.225), channel_id=1, source_target_pairs={{0,0},{1,2},{2,4},{3,6},{4,1},{5,3},{6,5},{7,7},{8,8},{9,10},{10,1... | collective-permute-start | bytes 786440 | tf_op jit(solution)/shard_map/ppermute | solution.py:1424
  316.3 37.3 %collective-permute-start.10 = (bf16[512,256]{1,0:T(8,128)(2,1)S(1)}, bf16[512,256]{1,0:T(8,128)(2,1)S(1)}, u32[]{:S(2)}, u32[]{:S(2)}) collective-permute-start(bf16[512,256]{1,0:T(8,128)(2,1)S(1)} %get-tuple-element.224), channel_id=1, source_target_pairs={{0,1},{1,3},{2,5},{3,7},{4,2},{5,0},{6,6},{7,4},{8,9},{9,11},{10,1... | collective-permute-start | bytes 786440 | tf_op jit(solution)/shard_map/ppermute | solution.py:1424
  319.2 34.5 %collective-permute-start.11 = (bf16[512,256]{1,0:T(8,128)(2,1)S(1)}, bf16[512,256]{1,0:T(8,128)(2,1)S(1)}, u32[]{:S(2)}, u32[]{:S(2)}) collective-permute-start(bf16[512,256]{1,0:T(8,128)(2,1)S(1)} %get-tuple-element.223), channel_id=1, source_target_pairs={{0,2},{1,0},{2,6},{3,4},{4,3},{5,1},{6,7},{7,5},{8,10},{9,8},{10,1... | collective-permute-start | bytes 786440 | tf_op jit(solution)/shard_map/ppermute | solution.py:1424
  323.6 30.1 %collective-permute-start.12 = (bf16[512,256]{1,0:T(8,128)(2,1)S(1)}, bf16[512,256]{1,0:T(8,128)(2,1)S(1)}, u32[]{:S(2)}, u32[]{:S(2)}) collective-permute-start(bf16[512,256]{1,0:T(8,128)(2,1)S(1)} %get-tuple-element.222), channel_id=1, source_target_pairs={{0,3},{1,1},{2,7},{3,5},{4,0},{5,2},{6,4},{7,6},{8,11},{9,9},{10,1... | collective-permute-start | bytes 786440 | tf_op jit(solution)/shard_map/ppermute | solution.py:1424
  357.6 4.8 collective-permute-start.16
  364.6 2.7 collective-permute-start.17
  375.0 22.6 %copy-start.21 = (bf16[1024,2048]{1,0:T(8,128)(2,1)}, bf16[1024,2048]{1,0:T(8,128)(2,1)S(1)}, u32[]{:S(2)}) copy-start(bf16[1024,2048]{1,0:T(8,128)(2,1)S(1)} %get-tuple-element.277) | copy-start | bytes 12582916
  377.6 9.3 %collective-permute-start.18 = (bf16[512,1024]{1,0:T(8,128)(2,1)S(1)}, bf16[512,1024]{1,0:T(8,128)(2,1)S(1)}, u32[]{:S(2)}, u32[]{:S(2)}) collective-permute-start(bf16[512,1024]{1,0:T(8,128)(2,1)S(1)} %fusion.85), channel_id=1, source_target_pairs={{0,4},{4,0},{8,12},{12,8},{16,20},{20,16},{24,28},{28,24},{1,5},{5... | collective-permute-start | bytes 3145736 | tf_op jit(solution)/shard_map/ppermute | solution.py:1223
  383.0 33.6 %collective-permute-start.20 = (bf16[1024,512]{1,0:T(8,128)(2,1)}, bf16[1024,512]{1,0:T(8,128)(2,1)}, u32[]{:S(2)}, u32[]{:S(2)}) collective-permute-start(bf16[1024,512]{1,0:T(8,128)(2,1)} %add_convert_fusion.9), channel_id=1, source_target_pairs={{0,16},{4,20},{8,24},{12,28},{16,0},{20,4},{24,8},{28,12},{1,17},{... | collective-permute-start | bytes 3145736 | tf_op jit(solution)/shard_map/ppermute | solution.py:1384
  390.6 9.9 %collective-permute-start.19 = (bf16[512,1024]{1,0:T(8,128)(2,1)}, bf16[512,1024]{1,0:T(8,128)(2,1)}, u32[]{:S(2)}, u32[]{:S(2)}) collective-permute-start(bf16[512,1024]{1,0:T(8,128)(2,1)} %get-tuple-element.197), channel_id=1, source_target_pairs={{0,4},{4,0},{8,12},{12,8},{16,20},{20,16},{24,28},{28,24},{1,5},{5... | collective-permute-start | bytes 3145736 | tf_op jit(solution)/shard_map/ppermute | solution.py:1223
  393.2 26.3 %collective-permute-start.21 = (bf16[1024,512]{1,0:T(8,128)(2,1)}, bf16[1024,512]{1,0:T(8,128)(2,1)}, u32[]{:S(2)}, u32[]{:S(2)}) collective-permute-start(bf16[1024,512]{1,0:T(8,128)(2,1)} %add_convert_fusion.8), channel_id=1, source_target_pairs={{0,8},{4,12},{8,0},{12,4},{16,24},{20,28},{24,16},{28,20},{1,9},{5... | collective-permute-start | bytes 3145736 | tf_op jit(solution)/shard_map/ppermute | solution.py:1384
  396.0 42.1 %collective-permute-start.22 = (bf16[512,1024]{1,0:T(8,128)(2,1)}, bf16[512,1024]{1,0:T(8,128)(2,1)}, u32[]{:S(2)}, u32[]{:S(2)}) collective-permute-start(bf16[512,1024]{1,0:T(8,128)(2,1)} %add_convert_fusion.7), channel_id=1, source_target_pairs={{0,16},{4,20},{8,24},{12,28},{16,0},{20,4},{24,8},{28,12},{1,17},{... | collective-permute-start | bytes 3145736 | tf_op jit(solution)/shard_map/ppermute | solution.py:1384
  399.9 41.4 %collective-permute-start.23 = (bf16[512,1024]{1,0:T(8,128)(2,1)}, bf16[512,1024]{1,0:T(8,128)(2,1)}, u32[]{:S(2)}, u32[]{:S(2)}) collective-permute-start(bf16[512,1024]{1,0:T(8,128)(2,1)} %add_convert_fusion.6), channel_id=1, source_target_pairs={{0,8},{4,12},{8,0},{12,4},{16,24},{20,28},{24,16},{28,20},{1,9},{5... | collective-permute-start | bytes 3145736 | tf_op jit(solution)/shard_map/ppermute | solution.py:1384
  424.9 18.4 %copy-start.22 = (bf16[1024,2048]{1,0:T(8,128)(2,1)S(1)}, bf16[1024,2048]{1,0:T(8,128)(2,1)}, u32[]{:S(2)}) copy-start(bf16[1024,2048]{1,0:T(8,128)(2,1)} %copy-done.21) | copy-start | bytes 12582916
  424.9 18.4 %copy-start.41 = (f32[256,1024]{1,0:T(8,128)S(1)}, f32[256,1024]{1,0:T(8,128)}, u32[]{:S(2)}) copy-start(f32[256,1024]{1,0:T(8,128)} %fusion.34) | copy-start | bytes 3145732
  424.9 18.4 %copy-start.64 = (bf16[1024,256]{1,0:T(8,128)(2,1)S(1)}, bf16[1024,256]{1,0:T(8,128)(2,1)}, u32[]{:S(2)}) copy-start(bf16[1024,256]{1,0:T(8,128)(2,1)} %get-tuple-element.211) | copy-start | bytes 1572868
  441.3 13.4 %collective-permute-start.24 = (bf16[1024,256]{1,0:T(8,128)(2,1)}, bf16[1024,256]{1,0:T(8,128)(2,1)S(1)}, u32[]{:S(2)}, u32[]{:S(2)}) collective-permute-start(bf16[1024,256]{1,0:T(8,128)(2,1)} %fusion.166), channel_id=1, source_target_pairs={{0,8},{4,12},{8,0},{12,4},{16,24},{20,28},{24,16},{28,20},{1,9},{5... | collective-permute-start | bytes 1572872 | tf_op jit(solution)/shard_map/ppermute | solution.py:1392
  441.8 13.2 %collective-permute-start.25 = (bf16[1024,256]{1,0:T(8,128)(2,1)}, bf16[1024,256]{1,0:T(8,128)(2,1)S(1)}, u32[]{:S(2)}, u32[]{:S(2)}) collective-permute-start(bf16[1024,256]{1,0:T(8,128)(2,1)} %fusion.163), channel_id=1, source_target_pairs={{0,16},{4,20},{8,24},{12,28},{16,0},{20,4},{24,8},{28,12},{1,17},{... | collective-permute-start | bytes 1572872 | tf_op jit(solution)/shard_map/ppermute | solution.py:1392
  462.0 16.3 %collective-permute-start.27 = (bf16[256,1024]{1,0:T(8,128)(2,1)S(1)}, bf16[256,1024]{1,0:T(8,128)(2,1)S(1)}, u32[]{:S(2)}, u32[]{:S(2)}) collective-permute-start(bf16[256,1024]{1,0:T(8,128)(2,1)S(1)} %fusion.157), channel_id=1, source_target_pairs={{0,16},{4,20},{8,24},{12,28},{16,0},{20,4},{24,8},{28,12},{1,17},{... | collective-permute-start | bytes 1572872 | tf_op jit(solution)/shard_map/ppermute | solution.py:1392
  463.6 16.9 %collective-permute-start.26 = (bf16[256,1024]{1,0:T(8,128)(2,1)S(1)}, bf16[256,1024]{1,0:T(8,128)(2,1)S(1)}, u32[]{:S(2)}, u32[]{:S(2)}) collective-permute-start(bf16[256,1024]{1,0:T(8,128)(2,1)S(1)} %fusion.160), channel_id=1, source_target_pairs={{0,8},{4,12},{8,0},{12,4},{16,24},{20,28},{24,16},{28,20},{1,9},{5... | collective-permute-start | bytes 1572872 | tf_op jit(solution)/shard_map/ppermute | solution.py:1392
  468.0 17.7 %collective-permute-start.33 = (bf16[512,256]{1,0:T(8,128)(2,1)S(1)}, bf16[512,256]{1,0:T(8,128)(2,1)S(1)}, u32[]{:S(2)}, u32[]{:S(2)}) collective-permute-start(bf16[512,256]{1,0:T(8,128)(2,1)S(1)} %pad_maximum_fusion.18), channel_id=1, source_target_pairs={{0,3},{1,0},{2,1},{3,2},{4,7},{5,4},{6,5},{7,6},{8,11},{9,8},{10,9... | collective-permute-start | bytes 786440 | tf_op jit(solution)/shard_map/ppermute | solution.py:1408
  469.3 24.6 %collective-permute-start.32 = (bf16[512,256]{1,0:T(8,128)(2,1)S(1)}, bf16[512,256]{1,0:T(8,128)(2,1)S(1)}, u32[]{:S(2)}, u32[]{:S(2)}) collective-permute-start(bf16[512,256]{1,0:T(8,128)(2,1)S(1)} %pad_maximum_fusion.17), channel_id=1, source_target_pairs={{0,2},{1,3},{2,0},{3,1},{4,6},{5,7},{6,4},{7,5},{8,10},{9,11},{10,... | collective-permute-start | bytes 786440 | tf_op jit(solution)/shard_map/ppermute | solution.py:1408
  469.5 24.4 %collective-permute-start.31 = (bf16[512,256]{1,0:T(8,128)(2,1)S(1)}, bf16[512,256]{1,0:T(8,128)(2,1)S(1)}, u32[]{:S(2)}, u32[]{:S(2)}) collective-permute-start(bf16[512,256]{1,0:T(8,128)(2,1)S(1)} %pad_maximum_fusion.16), channel_id=1, source_target_pairs={{0,1},{1,2},{2,3},{3,0},{4,5},{5,6},{6,7},{7,4},{8,9},{9,10},{10,1... | collective-permute-start | bytes 786440 | tf_op jit(solution)/shard_map/ppermute | solution.py:1408
  478.3 34.9 %collective-permute-start.34 = (bf16[512,1024]{1,0:T(8,128)(2,1)S(1)}, bf16[512,1024]{1,0:T(8,128)(2,1)S(1)}, u32[]{:S(2)}, u32[]{:S(2)}) collective-permute-start(bf16[512,1024]{1,0:T(8,128)(2,1)S(1)} %fusion.73), channel_id=1, source_target_pairs={{0,4},{4,0},{8,12},{12,8},{16,20},{20,16},{24,28},{28,24},{1,5},{5... | collective-permute-start | bytes 3145736 | tf_op jit(solution)/shard_map/ppermute | solution.py:1223
  482.5 30.8 %copy-start.25 = (f32[512,1024]{1,0:T(8,128)S(1)}, f32[512,1024]{1,0:T(8,128)}, u32[]{:S(2)}) copy-start(f32[512,1024]{1,0:T(8,128)} %get-tuple-element.198) | copy-start | bytes 6291460
  482.5 13.2 %collective-permute-start.30 = (bf16[256,512]{1,0:T(8,128)(2,1)S(1)}, bf16[256,512]{1,0:T(8,128)(2,1)S(1)}, u32[]{:S(2)}, u32[]{:S(2)}) collective-permute-start(bf16[256,512]{1,0:T(8,128)(2,1)S(1)} %pad_maximum_fusion.15), channel_id=1, source_target_pairs={{0,3},{1,0},{2,1},{3,2},{4,7},{5,4},{6,5},{7,6},{8,11},{9,8},{10,9... | collective-permute-start | bytes 786440 | tf_op jit(solution)/shard_map/ppermute | solution.py:1408
  485.7 27.4 %collective-permute-start.29 = (bf16[256,512]{1,0:T(8,128)(2,1)S(1)}, bf16[256,512]{1,0:T(8,128)(2,1)S(1)}, u32[]{:S(2)}, u32[]{:S(2)}) collective-permute-start(bf16[256,512]{1,0:T(8,128)(2,1)S(1)} %pad_maximum_fusion.14), channel_id=1, source_target_pairs={{0,2},{1,3},{2,0},{3,1},{4,6},{5,7},{6,4},{7,5},{8,10},{9,11},{10,... | collective-permute-start | bytes 786440 | tf_op jit(solution)/shard_map/ppermute | solution.py:1408
  493.8 19.3 %collective-permute-start.28 = (bf16[256,512]{1,0:T(8,128)(2,1)S(1)}, bf16[256,512]{1,0:T(8,128)(2,1)S(1)}, u32[]{:S(2)}, u32[]{:S(2)}) collective-permute-start(bf16[256,512]{1,0:T(8,128)(2,1)S(1)} %pad_maximum_fusion.13), channel_id=1, source_target_pairs={{0,1},{1,2},{2,3},{3,0},{4,5},{5,6},{6,7},{7,4},{8,9},{9,10},{10,1... | collective-permute-start | bytes 786440 | tf_op jit(solution)/shard_map/ppermute | solution.py:1408
  (101 other events, 440.6 us)

commit v4 on v3

--- a/solution.py
+++ b/solution.py
@@ -450,7 +450,15 @@
     )
 
 
+def slot_of(block, x, y):
+    dx = (block % 2 - x) * (block % 2 - x)
+    dy = (block // 2 - y) * (block // 2 - y)
+    return 3 * dy + dx - 2 * dx * dy
+
+
 def span(start, size):
+    if isinstance(start, int):
+        return pl.ds(start, size)
     return pl.ds(pl.multiple_of(start, 128), size)
 
 
@@ -478,14 +486,12 @@
     q_ref, k_ref, v_ref, proj_ref, inner_ref, outer_ref, small_ref, x_ref, g_ref,
     wqkv, wproj, winner, wouter, smalls, u_out, g_out,
     swap_s, swap_r, local_s, up_s, up_r, down_s, down_r, sm_s, sm_r,
-    p1_s, p1_r, p2_s, p2_r, t_s, t_r, t_l,
+    p1_s, p1_r, p2_s, p2_r, t_s, t_r, t_l, pair_s, pair_r,
 ):
     row, depth, core, chip, x, y = place()
     mate = chip * 2 + (1 - core)
-    x_chip = y * 2 + 1 - x
-    y_chip = (1 - y) * 2 + x
-    x_row = x_chip * 2 + core
-    y_row = y_chip * 2 + core
+    x_row = (y * 2 + 1 - x) * 2 + core
+    y_row = ((1 - y) * 2 + x) * 2 + core
     greet(row, depth, core, chip, x, y)
 
     def swap_src(piece, half):
@@ -524,7 +530,7 @@
 
     swaps, locals_ = [], []
     for piece in range(PIECES):
-        target = cell(piece, row * 128, 128, depth)
+        target = cell(piece, core * 128, 128, depth)
         cp = remote(
             swap_src(piece, 1 - core), target, swap_s.at[piece], swap_r.at[piece], mate, depth
         )
@@ -538,7 +544,7 @@
 
     def travel(piece, step, up):
         origin = depth - step if up else depth + step
-        ref = cell(piece, chip * 256, 256, origin)
+        ref = cell(piece, 0, 256, origin)
         send, recv = (up_s, up_r) if up else (down_s, down_r)
         return remote(
             ref, ref, send.at[piece, step], recv.at[piece, step], row,
@@ -558,7 +564,7 @@
                     @pl.when(inside)
                     def _():
                         origin = depth - step if up else depth + step
-                        ref = cell(piece, chip * 256, 256, origin)
+                        ref = cell(piece, 0, 256, origin)
                         recv = up_r if up else down_r
                         remote(
                             ref, ref, up_s.at[piece, step - 1], recv.at[piece, step - 1],
@@ -586,7 +592,7 @@
             to_core, to_depth = j % 2, core * 2 + j // 2
             mine = (to_core == core) & (to_depth == depth)
             source = src.at[pl.ds(j * 512, 512), :]
-            target = dst.at[:, span(depth * 256, 256)]
+            target = dst.at[pl.ds(0, 512), span(slot_of(depth, x, y) * 256, 256)]
 
             @pl.when(mine)
             def _():
@@ -603,7 +609,7 @@
         from_core = depth // 2
         for s in range(4):
             mine = (from_core == core) & (s == depth)
-            target = dst.at[:, pl.ds(s * 256, 256)]
+            target = dst.at[pl.ds(0, 512), span(slot_of(s, x, y) * 256, 256)]
             source = src.at[pl.ds(0, 512), :]
 
             @pl.when(mine)
@@ -622,27 +628,29 @@
             @pl.when(jnp.logical_not(mine))
             def _():
                 remote(
-                    src.at[pl.ds(j * 512, 512), :], dst.at[:, pl.ds(0, 256)],
+                    src.at[pl.ds(j * 512, 512), :], dst.at[pl.ds(0, 512), pl.ds(0, 256)],
                     t_s.at[index, j], t_r.at[index, 0], mate, depth,
                 ).wait_send()
 
     first, second = {}, {}
 
     def start_first(group):
-        for part, target in ((0, x_row), (1, y_row)):
+        for part, target, to in ((0, x_row, 1), (1, y_row, 3)):
             cp = remote(
-                region(group, part, chip), region(group, part, chip),
+                region(group, part, 0), region(group, part, to),
                 p1_s.at[group, part], p1_r.at[group, part], target, depth,
             )
             cp.start()
             first[group, part] = cp
 
     def start_second(group):
-        for part, target, other in ((0, y_row, x_chip), (1, x_row, y_chip)):
+        for part, target, moves in (
+            (0, y_row, ((0, 3), (1, 2))), (1, x_row, ((0, 1), (3, 2))),
+        ):
             first[group, part].wait_recv()
-            for i, block in enumerate((chip, other)):
+            for i, (origin, to) in enumerate(moves):
                 cp = remote(
-                    region(group, part, block), region(group, part, block),
+                    region(group, part, origin), region(group, part, to),
                     p2_s.at[group, part, i], p2_r.at[group, part, i], target, depth,
                 )
                 cp.start()
@@ -671,7 +679,12 @@
                 small_copies.append(cp)
             token_copies(1, g_ref, g_out)
     token_waits(0, x_ref, u_out)
+    pair = remote(
+        u_out.at[pl.ds(0, 512), :], u_out.at[pl.ds(512, 512), :], pair_s, pair_r, mate, depth
+    )
+    pair.start()
     token_waits(1, g_ref, g_out)
+    pair.wait()
     for cp in small_copies:
         cp.wait()
     small_local.wait()
@@ -698,7 +711,7 @@
             sd((1024, 2048), BF16),
             sd((2048, 1024), BF16),
             sd((4,) + small.shape, F32),
-            sd((512, 1024), BF16),
+            sd((1024, 1024), BF16),
             sd((512, 1024), BF16),
         ),
         in_specs=[VMEM] * 7 + [ANY] * 2,
@@ -708,7 +721,7 @@
             DMA((PIECES, 3)), DMA((PIECES, 3)), DMA((PIECES, 3)), DMA((PIECES, 3)),
             DMA((3,)), DMA((3,)),
             DMA((n, 2)), DMA((n, 2)), DMA((n, 2, 2)), DMA((n, 2, 2)),
-            DMA((2, 4)), DMA((2, 4)), DMA((2,)),
+            DMA((2, 4)), DMA((2, 4)), DMA((2,)), DMA, DMA,
         ],
         compiler_params=pltpu.CompilerParams(collective_id=1, has_side_effects=True),
     )(q, k, v, proj, inner, outer, small, x_rolled, g_rolled)
@@ -797,8 +810,8 @@
         for part in (0, 1):
             target = y_row if part == 0 else x_row
             for i in (0, 1):
-                kept = y * 2 + i if part == 0 else i * 2 + x
-                sent = (1 - y) * 2 + i if part == 0 else i * 2 + (1 - x)
+                kept = ((0, 1), (0, 3))[part][i]
+                sent = ((3, 2), (1, 2))[part][i]
                 lc = pltpu.make_async_copy(
                     region(group, part, kept), own[group][part].at[i], o_s.at[group, part, i]
                 )
@@ -814,12 +827,11 @@
     def start_second(group):
         for part in (0, 1):
             target = x_row if part == 0 else y_row
-            mine = x if part == 0 else y
             for i in (0, 1):
                 copies["o", group, part, i].wait()
                 copies["p1", group, part, i].wait_recv()
-            other = own[group][part].at[1 - mine]
-            add_rows(other, (other, got1[group][part].at[1 - mine]))
+            other = own[group][part].at[1]
+            add_rows(other, (other, got1[group][part].at[1]))
             cp = remote(
                 other, got2[group][part], p2_s.at[group, part], p2_r.at[group, part], target, depth
             )
@@ -838,11 +850,10 @@
     def start_depth(group):
         rows = SHAPES[group][0]
         for part in (0, 1):
-            mine = x if part == 0 else y
             copies["p2", group, part].wait_recv()
             add_rows(
                 full[group].at[pl.ds(part * rows, rows), :],
-                (own[group][part].at[mine], got1[group][part].at[mine], got2[group][part]),
+                (own[group][part].at[0], got1[group][part].at[0], got2[group][part]),
             )
         send_depth(group)
 
@@ -872,7 +883,7 @@
         to_core = depth // 2
         for z in range(4):
             mine = (to_core == core) & (z == depth)
-            source = src.at[:, pl.ds(z * 256, 256)]
+            source = src.at[:, span(slot_of(z, x, y) * 256, 256)]
             target = dst.at[span(j * 512, 512), :]
 
             @pl.when(mine)
@@ -1227,12 +1238,14 @@
     return jnp.concatenate([own, exchange(own)], axis=0)
 
 
-def share_sum(left, weight, product):
+def share_sum(left, weight, product, apart=False):
     mate_part, left_own = lax.optimization_barrier(
         (rounded(product(left[512:], weight)), left[:512])
     )
-    other = exchange(mate_part)
-    return product(left_own, weight) + other.astype(F32)
+    own_part, other = product(left_own, weight), exchange(mate_part)
+    if apart:
+        own_part, other = lax.optimization_barrier((own_part, other))
+    return own_part + other.astype(F32)
 
 
 def norm_rows(summed, gain, shift):
@@ -1251,19 +1264,20 @@
     return grad_input, token_sum(grad_output * normed), token_sum(grad_output)
 
 
-def fast_forward(hidden, weights, vectors, ids):
+def fast_forward(hidden, weights, vectors, ids, whole_in=None):
     wqkv, wproj, winner, wouter = weights
     flag, id_col, id_row = ids
-    whole_in = both(rounded(hidden))
+    if whole_in is None:
+        whole_in = both(rounded(hidden))
     qkv = rounded(matmul(whole_in, wqkv) + vectors["qkv"])
     attended, lse = attend(flag, qkv, id_col, id_row)
-    branch = share_sum(attended, wproj, matmul) + vectors["proj"]
+    branch = share_sum(attended, wproj, matmul, True) + vectors["proj"]
     first, normed_one, inverse_one = norm_rows(
         hidden + branch, vectors["attn_gain"], vectors["attn_shift"]
     )
     whole_mid = both(rounded(first))
     active, slope = ffn_in(whole_mid, winner, vectors["inner"])
-    ffn = share_sum(active, wouter, matmul) + vectors["outer"]
+    ffn = share_sum(active, wouter, matmul, True) + vectors["outer"]
     output, normed_two, inverse_two = norm_rows(
         first + ffn, vectors["ffn_gain"], vectors["ffn_shift"]
     )
@@ -1287,14 +1301,16 @@
     ffn_low = rounded(grad_second)
     whole_second = both(ffn_low)
     inner_low = rounded(against(whole_second, wouter) * slope.astype(F32))
-    outer_terms = outer_pieces(active, by_place(whole_second))
-    if later is not None:
-        outer_planes = [Plane(add_trees(outer_terms, later[0]), h, 1) for h in (0, 1)]
+    if later is None:
+        outer_terms = rounded(over_tokens(active, whole_second))
+    else:
+        outer_terms = add_trees(outer_pieces(active, whole_second), outer_cuts(later[0]))
+        outer_planes = [Plane(outer_terms, h, 1) for h in (0, 1)]
         outer_got = [p.step_one() for p in outer_planes]
     grad_first = grad_second + share_sum(inner_low, winner, against)
-    inner_terms = inner_pieces(by_place(whole_mid), inner_low)
+    inner_terms = rounded(add_later(over_tokens(whole_mid, inner_low), later, 1))
     if later is not None:
-        inner_planes = [Plane(add_trees(inner_terms, later[1]), h, 0) for h in (0, 1)]
+        inner_planes = [Plane(inner_cuts(inner_terms), h, 0) for h in (0, 1)]
         inner_got = [p.step_one() for p in inner_planes]
     grad_attn, attn_gain_sum, attn_shift_sum = norm_rows_back(
         grad_first, normed_one, inverse_one, vectors["attn_gain"]
@@ -1339,20 +1355,7 @@
     return [(r, r + bit - 2 * bit * ((r // bit) % 2)) for r in range(8)]
 
 
-def by_place(values):
-    chip = lax.axis_index("row") // 2
-    x, y = chip % 2, chip // 2
-
-    def block(yy, xx):
-        return lax.dynamic_slice_in_dim(values, (yy * 2 + xx) * 256, 256, 1)
-
-    far = block(1 - y, 1 - x)
-    return jnp.concatenate(
-        [block(y, 1 - x), block(y, x), block(1 - y, x), far, block(y, 1 - x)], axis=1
-    )
-
-
-CUTS = (((512, 1024), (0, 256), (256, 512)), ((768, 1280), (512, 768), (256, 512)))
+CUTS = (((512, 1024), (256, 512), (0, 256)), ((256, 768), (768, 1024), (0, 256)))
 
 
 def outer_pieces(active, relative):
@@ -1362,21 +1365,31 @@
     ]
 
 
-def inner_pieces(relative, inner_low):
+def add_trees(left, right):
+    return jax.tree.map(lambda p, q: p + q.astype(F32), left, right)
+
+
+def outer_cuts(whole):
     return [
-        [over_tokens(relative[:, a:b], inner_low[:, h * 1024 : (h + 1) * 1024]) for a, b in CUTS[h]]
-        for h in (0, 1)
+        [whole[h * 1024 : (h + 1) * 1024, a:b] for a, b in CUTS[h]] for h in (0, 1)
     ]
 
 
-def add_trees(left, right):
-    return jax.tree.map(lambda p, q: p + q, left, right)
+def inner_cuts(whole):
+    return [
+        [whole[a:b, h * 1024 : (h + 1) * 1024] for a, b in CUTS[h]] for h in (0, 1)
+    ]
+
+
+def add_later(term, later, index):
+    return term if later is None else term + later[index].astype(F32)
 
 
 class Plane:
     def __init__(self, pieces, half, axis):
-        sent, self.handed, self.own = pieces[half]
+        sent, handed, own = pieces[half]
         self.sent = rounded(sent)
+        self.handed, self.own = handed.astype(F32), own.astype(F32)
         self.half, self.axis = half, axis
         self.first, self.second = (4, 2) if half == 0 else (2, 4)
 
@@ -1385,7 +1398,7 @@
 
     def to_hand(self, got):
         low, high = jnp.split(got, 2, axis=self.axis)
-        self.got, handed = (low, high) if self.half == 0 else (high, low)
+        self.got, handed = (high, low) if self.half == 0 else (low, high)
         return rounded(self.handed + handed.astype(F32))
 
     def step_two(self, handed):
@@ -1413,6 +1426,7 @@
     core = lax.axis_index("row") % 2
     depth = lax.axis_index("col")
     j = (depth % 2) * 2 + core
+    x, y = place()[4:]
     parts = []
     for k in range(4):
         pairs = []
@@ -1420,7 +1434,7 @@
             for z in range(4):
                 block = ((z % 2) * 2 + r % 2 + k) % 4
                 pairs.append((r * 4 + z, (r // 2 * 2 + z // 2) * 4 + block))
-        piece = lax.dynamic_slice_in_dim(values, ((j + k) % 4) * 256, 256, 1)
+        piece = lax.dynamic_slice_in_dim(values, slot_of((j + k) % 4, x, y) * 256, 256, 1)
         parts.append(lax.ppermute(piece, ("row", "col"), pairs))
     return parts
 
@@ -1496,11 +1510,14 @@
         query_weight, key_weight, value_weight, proj_weight, inner_weight, outer_weight,
         small, turned(hidden_in), turned(grad_out),
     )
+    smalls = smalls.reshape(4, 3072)
+    x, y = place()[4:]
+    order = (y * 2 + x, y * 2 + 1 - x, (1 - y) * 2 + 1 - x, (1 - y) * 2 + x)
+    placed = jnp.stack([lax.dynamic_index_in_dim(smalls, b, 0, keepdims=False) for b in order])
     weights = (wqkv, wproj, winner, wouter)
-    smalls = smalls.reshape(4, 3072)
     vectors, offset = {}, 0
     for name, size in VECTORS:
-        part = smalls[:, offset : offset + size]
+        part = (smalls if name in SPLIT else placed)[:, offset : offset + size]
         offset += size
         if name in SPLIT:
             part = jnp.where(core == 0, part[:, : size // 2], part[:, size // 2 :])
@@ -1512,7 +1529,9 @@
         [vectors["q"], jnp.zeros_like(vectors["q"]), vectors["v"]], axis=1
     )
 
-    middle, kept_one = fast_forward(start_low.astype(F32), weights, vectors, ids)
+    middle, kept_one = fast_forward(
+        start_low[:512].astype(F32), weights, vectors, ids, start_low
+    )
     final_out, kept_two = fast_forward(middle, weights, vectors, ids)
     grad_flow = grad_low.astype(F32)
     parts = spread_out(rounded(final_out))
@@ -1527,6 +1546,14 @@
     pieces = []
     for (name, size), a, b in zip(VECTORS, small_two, small_one):
         total = a + b
+        if name not in SPLIT:
+            blocks = total.reshape(4, 256)
+            total = jnp.stack(
+                [
+                    lax.dynamic_index_in_dim(blocks, slot_of(n, x, y), 0, keepdims=False)
+                    for n in range(4)
+                ]
+            )
         if name in SPLIT:
             half = total.reshape(4, 1, size // 2)
             if name == "inner":

time: 589 us -> 572 us (0.971)
  waiting for transfers between devices: 52.8 us -> 28.7 us
  matrix products: 138 us -> 127 us
  other arithmetic: 30.4 us -> 38.1 us
    ppermute x6, waiting for transfers between devices: 25.6 us -> 13.8 us  [fold_depth(): lax.ppermute(unit((depth + k) % 4), 'col', pairs).astype(F32)]
    dot_general x32 -> x17, matrix products: 66.3 us -> 55.2 us  [over_tokens(): lax.dot_general(left, right, (((0,), (0,)), ((), ())), preferred_element_...]
    ppermute x6, starting transfers between devices: 7.19 us -> 13.4 us  [fold_depth(): lax.ppermute(unit((depth + k) % 4), 'col', pairs).astype(F32)]
    ppermute x4, waiting for transfers between devices: 6.06 us -> 0.01 us  [step_one(): return lax.ppermute(self.sent, 'row', flip_row(self.first))]
    ppermute x17 -> x16, waiting for transfers between devices: 17.6 us -> 13.6 us  [exchange(): return lax.ppermute(values, 'row', pairs)]
    unnamed x267 -> x210, local copies, waits for them, and re-layouts: 20.9 us -> 18 us
  transfers between devices with their start and end apart: 35 -> 34, of which waited for: 15 -> 12; matrix products, arithmetic and copies ran while one was open for 15% -> 16% of each run, Pallas kernels for 9% -> 32%
where the time goes in v4:
time: 572 us; the launch traced here: 565 us
  Pallas kernels  299 us (52%)
  matrix products  127 us (22%)
  other arithmetic  38.1 us (7%)
  starting transfers between devices  35.9 us (6%)
  waiting for transfers between devices  28.7 us (5%)
  local copies, waits for them, and re-layouts  27.3 us (5%)
  between operations  8.99 us (2%)
    pallas_call x1, Pallas kernels, gather_all(): pl.pallas_call(gather_kernel, out_shape=(sd((1024, 1536), BF16), sd((512,...  130 us
    pallas_call x1, Pallas kernels, scatter_all(): pl.pallas_call(scatter_kernel, out_shape=tuple((sd(size, F32) for size in...  64.9 us
    dot_general x17, matrix products, over_tokens(): lax.dot_general(left, right, (((0,), (0,)), ((), ())), preferred_element_...  55.2 us
    pallas_call x3, Pallas kernels, attend_back(): pl.pallas_call(attend_back_kernel, out_shape=(shape, shape, shape), grid_...  50.2 us
    dot_general x12, matrix products, against(): lax.dot_general(left, right, (((1,), (1,)), ((), ())), preferred_element_...  40 us
    dot_general x10, matrix products, matmul(): return jnp.dot(left, right, preferred_element_type=jnp.float32)  31.8 us
    pallas_call x2, Pallas kernels, ffn_in(): pl.pallas_call(ffn_in_kernel, out_shape=(shape, shape), grid=(hidden // c...  27.5 us
    pallas_call x2, Pallas kernels, attend(): pl.pallas_call(attend_kernel, out_shape=(jax.ShapeDtypeStruct((tokens, wi...  26.6 us
  transfers between devices with their start and end apart: 34, of which 12 were waited for; matrix products, arithmetic and copies ran while one was open for 16% of the time, Pallas kernels for 32%

profile of v4, /device:TPU:0, one launch (start us, length us, event | category | flops | bytes accessed | tf_op | source)
XLA Modules:
  0.0 564.8 jit_solution(7542751288811115903)
XLA Ops:
  5.0 5.2 fusion.101
  10.2 129.6 %shard_map.305 = (bf16[1024,1536]{1,0:T(8,128)(2,1)}, bf16[512,1024]{1,0:T(8,128)(2,1)}, bf16[1024,2048]{1,0:T(8,128)(2,1)}, bf16[2048,1024]{1,0:T(8,128)(2,1)},...) custom-call(bf16[128,256]{1,0:T(8,128)(2,1)} %q_ref.1, bf16[128,256]{1,0:T(8,128)(2,1)} %k_ref.1, ...), custom_call_target="tpu_custom_call" | custom-call | tf_op jit(solution)/shard_map/pallas_call | solution.py:706
  140.8 7.6 %add_convert_fusion.2.q_ref.k_ref.v_ref = bf16[1024,1536]{1,0:T(8,128)(2,1)} fusion(bf16[1024,1024]{1,0:T(8,128)(2,1)} %get-tuple-element.100, bf16[1024,1536]{1,0:T(8,128)(2,1)} %get-tuple-element.101, f32[1536]{0:T(1024)S(1)} %fusion.120), kind=kOutput, calls=%fused_computation.6 | convolution fusion | flops 3224371200 | bytes 8394752 | tf_op jit(solution)/shard_map/dot_general | solution.py:26
  151.8 13.3 %attend.2 = (bf16[1024,512]{1,0:T(8,128)(2,1)S(1)}, f32[1024,512]{1,0:T(8,128)S(1)}) custom-call(s32[1]{0:T(128)} %bitcast.1.flag_ref, bf16[1024,1536]{1,0:T(8,128)(2,1)} %add_convert_fusion.2.q_ref.k_ref.v_ref, bf16[1024,1536]{1,0:T(8,128)(2,1)} %add_convert_fusion.2.q_ref.k_ref.v_ref, bf16[1024,1536]{1,0:T(8,128)(2,1)} %add_convert_fusion.2.q_ref.k_ref.v_ref, ...), custom_call_target="tpu_custom_call" | custom-call | flops 20000000000 | bytes 8000000 | tf_op jit(solution)/shard_map/attend/pallas_call | solution.py:1060
  174.4 2.8 collective-permute-done.2
  179.0 13.8 %ffn_in.2 = (bf16[1024,2048]{1,0:T(8,128)(2,1)}, bf16[1024,2048]{1,0:T(8,128)(2,1)}) custom-call(bf16[1024,1024]{1,0:T(8,128)(2,1)S(1)} %pad_maximum_fusion.2.x_ref, bf16[1024,2048]{1,0:T(8,128)(2,1)} %get-tuple-element.109.w_ref, f32[1,2048]{1,0:T(1,128)S(1)} %reshape.282.b_ref), custom_call_target="tpu_custom_call" | custom-call | flops 14000000000 | bytes 14000000 | tf_op jit(solution)/shard_map/ffn_in/pallas_call | solution.py:1212
  195.6 4.7 fusion.40
  200.5 2.3 fusion.147
  204.8 2.4 collective-permute-done.4
  208.2 5.6 add_convert_fusion.1.q_ref.k_ref.v_ref
  213.8 13.3 %attend.3 = (bf16[1024,512]{1,0:T(8,128)(2,1)S(1)}, f32[1024,512]{1,0:T(8,128)S(1)}) custom-call(s32[1]{0:T(128)} %bitcast.1.flag_ref, bf16[1024,1536]{1,0:T(8,128)(2,1)} %add_convert_fusion.1.q_ref.k_ref.v_ref, bf16[1024,1536]{1,0:T(8,128)(2,1)} %add_convert_fusion.1.q_ref.k_ref.v_ref, bf16[1024,1536]{1,0:T(8,128)(2,1)} %add_convert_fusion.1.q_ref.k_ref.v_ref, ...), custom_call_target="tpu_custom_call" | custom-call | flops 20000000000 | bytes 8000000 | tf_op jit(solution)/shard_map/attend/pallas_call | solution.py:1060
  232.4 2.4 collective-permute-done.6
  235.8 13.7 %ffn_in.3 = (bf16[1024,2048]{1,0:T(8,128)(2,1)}, bf16[1024,2048]{1,0:T(8,128)(2,1)}) custom-call(bf16[1024,1024]{1,0:T(8,128)(2,1)S(1)} %pad_maximum_fusion.4.x_ref, bf16[1024,2048]{1,0:T(8,128)(2,1)} %get-tuple-element.109.w_ref, f32[1,2048]{1,0:T(1,128)S(1)} %reshape.282.b_ref), custom_call_target="tpu_custom_call" | custom-call | flops 14000000000 | bytes 14000000 | tf_op jit(solution)/shard_map/ffn_in/pallas_call | solution.py:1212
  249.6 4.1 fusion.43
  254.3 2.3 fusion.149
  259.9 2.4 collective-permute-done.12
  262.3 5.3 convert_reduce_fusion.1
  267.7 3.4 fusion.46
  274.8 9.6 %convolution_convert_fusion = bf16[2048,1024]{1,0:T(8,128)(2,1)} fusion(bf16[1024,2048]{1,0:T(8,128)(2,1)} %get-tuple-element.121, bf16[512,1024]{1,0:T(8,128)(2,1)} %copy-done.75, bf16[512,1024]{1,0:T(8,128)(2,1)} %copy-done.44), kind=kOutput, calls=%fused_computation.7 | convolution fusion | flops 4301258752 | bytes 10485760 | tf_op jit(solution)/shard_map/dot_general | solution.py:30
  284.5 4.9 multiply_reduce_fusion.2
  292.6 6.5 %fusion.137 = bf16[1024,2048]{1,0:T(8,128)(2,1)} fusion(bf16[1024,2048]{1,0:T(8,128)(2,1)S(1)} %copy-done.37, bf16[512,1024]{1,0:T(8,128)(2,1)S(1)} %copy-done.43, bf16[512,1024]{1,0:T(8,128)(2,1)S(1)} %copy-done.27), kind=kOutput, calls=%fused_computation.319 | convolution fusion | flops 4299161600 | bytes 10485760 | tf_op jit(solution)/shard_map/dot_general | solution.py:30
  299.3 3.7 collective-permute-start.11
  303.4 3.5 collective-permute-start.9
  309.1 24.4 %attend_back.3 = (bf16[1024,512]{1,0:T(8,128)(2,1)S(1)}, bf16[1024,512]{1,0:T(8,128)(2,1)S(1)}, bf16[1024,512]{1,0:T(8,128)(2,1)S(1)}) custom-call(s32[1]{0:T(128)} %bitcast.1.flag_ref, bf16[1024,1536]{1,0:T(8,128)(2,1)} %add_convert_fusion.1.q_ref.k_ref.v_ref, bf16[1024,1536]{1,0:T(8,128)(2,1)} %add_convert_fusion.1.q_ref.k_ref.v_ref, ...), custom_call_target="tpu_custom_call" | custom-call | flops 40000000000 | bytes 10000000 | tf_op jit(solution)/shard_map/attend_back/pallas_call | solution.py:1145
  343.6 2.3 convert_reduce_fusion.3
  349.0 8.7 %convert_reduce_fusion = (f32[2048]{0:T(1024)S(1)}, bf16[1024,2048]{1,0:T(8,128)(2,1)S(1)}) fusion(bf16[1024,2048]{1,0:T(8,128)(2,1)} %get-tuple-element.143, bf16[2048,1024]{1,0:T(8,128)(2,1)} %get-tuple-element.111, bf16[512,1024]{1,0:T(8,128)(2,1)} %collective-permute-done.16, bf16[512,1024]{1,0:T(8,128)(2,1)} %get-tuple-element.208), kind=kOutput, calls=%fused_computation | convolution fusion | flops 4309645312 | bytes 14688256 | tf_op jit(solution)/shard_map/dot_general | solution.py:36
  357.8 3.4 fusion.49
  362.7 4.8 add_convert_fusion.7
  368.8 4.3 add_convert_fusion.8
  373.9 2.4 fusion.151
  377.8 2.3 convert_reduce_fusion.5
  381.3 6.5 %add_convert_fusion = bf16[1024,2048]{1,0:T(8,128)(2,1)S(1)} fusion(bf16[1024,2048]{1,0:T(8,128)(2,1)S(1)} %copy-done.77, bf16[1024,2048]{1,0:T(8,128)(2,1)S(1)} %copy-done.39, bf16[512,1024]{1,0:T(8,128)(2,1)} %collective-permute-done.2, bf16[512,1024]{1,0:T(8,128)(2,1)} %fusion.15), kind=kOutput, calls=%fused_computation.2 | convolution fusion | flops 4305453056 | bytes 14680064 | tf_op jit(solution)/shard_map/dot_general | solution.py:30
  393.6 3.3 convolution_convert_fusion.1.do_ref
  396.9 12.8 %attend_back.4 = (bf16[1024,256]{1,0:T(8,128)(2,1)S(1)}, bf16[1024,256]{1,0:T(8,128)(2,1)S(1)}, bf16[1024,256]{1,0:T(8,128)(2,1)S(1)}) custom-call(s32[1]{0:T(128)} %bitcast.1.flag_ref, bf16[1024,1536]{1,0:T(8,128)(2,1)} %add_convert_fusion.2.q_ref.k_ref.v_ref, bf16[1024,1536]{1,0:T(8,128)(2,1)} %add_convert_fusion.2.q_ref.k_ref.v_ref, ...), custom_call_target="tpu_custom_call" | custom-call | flops 20000000000 | bytes 5000000 | tf_op jit(solution)/shard_map/attend_back/pallas_call | solution.py:1145
  409.7 3.0 fusion.90
  416.9 13.0 %attend_back.5 = (bf16[1024,256]{1,0:T(8,128)(2,1)S(1)}, bf16[1024,256]{1,0:T(8,128)(2,1)S(1)}, bf16[1024,256]{1,0:T(8,128)(2,1)S(1)}) custom-call(s32[1]{0:T(128)} %bitcast.1.flag_ref, bf16[1024,1536]{1,0:T(8,128)(2,1)} %add_convert_fusion.2.q_ref.k_ref.v_ref, bf16[1024,1536]{1,0:T(8,128)(2,1)} %add_convert_fusion.2.q_ref.k_ref.v_ref, ...), custom_call_target="tpu_custom_call" | custom-call | flops 20000000000 | bytes 5000000 | tf_op jit(solution)/shard_map/attend_back/pallas_call | solution.py:1145
  432.0 3.0 fusion.86
  444.4 2.3 fusion.93
  446.8 2.6 collective-permute-start.30
  449.6 2.6 collective-permute-start.32
  456.3 2.3 add_convert_fusion.5.refs_2_
  458.6 2.3 add_convert_fusion.4.refs_3_
  467.9 2.3 collective-permute-start.28
  470.2 5.7 %collective-permute-start.29 = (bf16[256,512]{1,0:T(8,128)(2,1)S(1)}, bf16[256,512]{1,0:T(8,128)(2,1)S(1)}, u32[]{:S(2)}, u32[]{:S(2)}) collective-permute-start(bf16[256,512]{1,0:T(8,128)(2,1)S(1)} %pad_maximum_fusion.16), channel_id=1, source_target_pairs={{0,3},{1,0},{2,1},{3,2},{4,7},{5,4},{6,5},{7,6},{8,11},{9,8},{10,9... | collective-permute-start | bytes 786440 | tf_op jit(solution)/shard_map/ppermute | solution.py:1421
  476.0 2.9 collective-permute-done.27
  478.9 10.9 %collective-permute-done.28 = bf16[256,512]{1,0:T(8,128)(2,1)S(1)} collective-permute-done((bf16[256,512]{1,0:T(8,128)(2,1)S(1)}, bf16[256,512]{1,0:T(8,128)(2,1)S(1)}, u32[]{:S(2)}, u32[]{:S(2)}) %collective-permute-start.28) | collective-permute-done | bytes 262176 | tf_op jit(solution)/shard_map/ppermute | solution.py:1421
  491.6 64.9 %shard_map.306 = (f32[256,128]{1,0:T(8,128)S(1)}, f32[128,256]{1,0:T(8,128)S(1)}, f32[128,256]{1,0:T(8,128)S(1)}, f32[128,256]{1,0:T(8,128)S(1)}, f32[128,1024]{...) custom-call(bf16[512,1024]{1,0:T(8,128)(2,1)S(1)} %add_convert_fusion.9.refs_0_, ...), custom_call_target="tpu_custom_call" | custom-call | tf_op jit(solution)/shard_map/pallas_call | solution.py:993
  557.1 2.6 fusion.100
  (402 shorter events, 97.7 us)
Async XLA Ops:
  0.8 147.6 %collective-permute-start = (s32[2048]{0:T(1024)}, s32[2048]{0:T(1024)S(1)}, u32[]{:S(2)}, u32[]{:S(2)}) collective-permute-start(s32[2048]{0:T(1024)} %bitcast.156), channel_id=1, source_target_pairs={{0,4},{4,0},{8,12},{12,8},{16,20},{20,16},{24,28},{28,24},{1,5},{5... | collective-permute-start | bytes 24584 | tf_op jit(solution)/shard_map/ppermute | solution.py:1234
  151.7 62.1 %copy-start.2 = (s32[1,1024]{0,1:T(8,128)}, s32[1,1024]{0,1:T(8,128)S(1)}, u32[]{:S(2)}) copy-start(s32[1,1024]{0,1:T(8,128)S(1)} %copy.53) | copy-start | bytes 12292
  151.7 14.3 %copy-start.18 = (bf16[512,1024]{1,0:T(8,128)(2,1)S(1)}, bf16[512,1024]{1,0:T(8,128)(2,1)}, u32[]{:S(2)}) copy-start(bf16[512,1024]{1,0:T(8,128)(2,1)} %get-tuple-element.104) | copy-start | bytes 3145732
  167.7 3.0 collective-permute-start.1
  172.6 30.4 %copy-start.10 = (f32[512,1024]{1,0:T(8,128)}, f32[512,1024]{1,0:T(8,128)S(1)}, u32[]{:S(2)}) copy-start(f32[512,1024]{1,0:T(8,128)S(1)} %get-tuple-element.224) | copy-start | bytes 6291460
  172.6 30.4 %copy-start.49 = (f32[512]{0:T(512)}, f32[512]{0:T(512)S(1)}, u32[]{:S(2)}) copy-start(f32[512]{0:T(512)S(1)} %get-tuple-element.310) | copy-start | bytes 6148
  172.6 30.4 %copy-start.51 = (f32[512]{0:T(512)}, f32[512]{0:T(512)S(1)}, u32[]{:S(2)}) copy-start(f32[512]{0:T(512)S(1)} %get-tuple-element.311) | copy-start | bytes 6148
  174.2 3.0 collective-permute-start.2
  200.3 2.7 collective-permute-start.3
  204.0 26.6 %copy-start.12 = (f32[512,1024]{1,0:T(8,128)}, f32[512,1024]{1,0:T(8,128)S(1)}, u32[]{:S(2)}) copy-start(f32[512,1024]{1,0:T(8,128)S(1)} %get-tuple-element.223) | copy-start | bytes 6291460
  204.5 2.7 collective-permute-start.4
  213.8 13.4 %copy-start.19 = (bf16[512,1024]{1,0:T(8,128)(2,1)S(1)}, bf16[512,1024]{1,0:T(8,128)(2,1)}, u32[]{:S(2)}) copy-start(bf16[512,1024]{1,0:T(8,128)(2,1)} %get-tuple-element.104) | copy-start | bytes 3145732
  227.9 2.7 collective-permute-start.5
  232.1 2.7 collective-permute-start.6
  235.8 13.7 %copy-start.69 = (bf16[2048,1024]{1,0:T(8,128)(2,1)S(1)}, bf16[2048,1024]{1,0:T(8,128)(2,1)}, u32[]{:S(2)}) copy-start(bf16[2048,1024]{1,0:T(8,128)(2,1)} %get-tuple-element.111) | copy-start | bytes 12582916
  253.9 2.7 collective-permute-start.7
  259.6 2.7 collective-permute-start.12
  272.5 11.9 %collective-permute-start.13 = (bf16[512,1024]{1,0:T(8,128)(2,1)}, bf16[512,1024]{1,0:T(8,128)(2,1)}, u32[]{:S(2)}, u32[]{:S(2)}) collective-permute-start(bf16[512,1024]{1,0:T(8,128)(2,1)} %fusion.46), channel_id=1, source_target_pairs={{0,4},{4,0},{8,12},{12,8},{16,20},{20,16},{24,28},{28,24},{1,5},{5... | collective-permute-start | bytes 3145736 | tf_op jit(solution)/shard_map/ppermute | solution.py:1234
  274.8 9.6 %copy-start.15 = (f32[512,1024]{1,0:T(8,128)S(1)}, f32[512,1024]{1,0:T(8,128)}, u32[]{:S(2)}) copy-start(f32[512,1024]{1,0:T(8,128)} %copy-done.14) | copy-start | bytes 6291460
  274.8 9.6 %copy-start.25 = (bf16[512,1024]{1,0:T(8,128)(2,1)S(1)}, bf16[512,1024]{1,0:T(8,128)(2,1)}, u32[]{:S(2)}) copy-start(bf16[512,1024]{1,0:T(8,128)(2,1)} %get-tuple-element.126) | copy-start | bytes 3145732
  290.2 17.6 %copy-start.22 = (bf16[512,1024]{1,0:T(8,128)(2,1)}, bf16[512,1024]{1,0:T(8,128)(2,1)S(1)}, u32[]{:S(2)}) copy-start(bf16[512,1024]{1,0:T(8,128)(2,1)S(1)} %get-tuple-element.216) | copy-start | bytes 3145732
  290.2 17.6 %collective-permute-start.14 = (bf16[512,1024]{1,0:T(8,128)(2,1)S(1)}, bf16[512,1024]{1,0:T(8,128)(2,1)S(1)}, u32[]{:S(2)}, u32[]{:S(2)}) collective-permute-start(bf16[512,1024]{1,0:T(8,128)(2,1)S(1)} %get-tuple-element.216), channel_id=1, source_target_pairs={{0,4},{4,0},{8,12},{12,8},{16,20},{20,16},{24,28},{28,24},{1,5},{5... | collective-permute-start | bytes 3145736 | tf_op jit(solution)/shard_map/ppermute | solution.py:1234
  299.3 34.3 %collective-permute-start.11 = (bf16[512,256]{1,0:T(8,128)(2,1)S(1)}, bf16[512,256]{1,0:T(8,128)(2,1)S(1)}, u32[]{:S(2)}, u32[]{:S(2)}) collective-permute-start(bf16[512,256]{1,0:T(8,128)(2,1)S(1)} %get-tuple-element.232), channel_id=1, source_target_pairs={{0,3},{1,1},{2,7},{3,5},{4,0},{5,2},{6,4},{7,6},{8,11},{9,9},{10,1... | collective-permute-start | bytes 786440 | tf_op jit(solution)/shard_map/ppermute | solution.py:1438
  303.0 30.6 %collective-permute-start.10 = (bf16[512,256]{1,0:T(8,128)(2,1)S(1)}, bf16[512,256]{1,0:T(8,128)(2,1)S(1)}, u32[]{:S(2)}, u32[]{:S(2)}) collective-permute-start(bf16[512,256]{1,0:T(8,128)(2,1)S(1)} %get-tuple-element.233), channel_id=1, source_target_pairs={{0,2},{1,0},{2,6},{3,4},{4,3},{5,1},{6,7},{7,5},{8,10},{9,8},{10,1... | collective-permute-start | bytes 786440 | tf_op jit(solution)/shard_map/ppermute | solution.py:1438
  303.4 30.2 %collective-permute-start.9 = (bf16[512,256]{1,0:T(8,128)(2,1)S(1)}, bf16[512,256]{1,0:T(8,128)(2,1)S(1)}, u32[]{:S(2)}, u32[]{:S(2)}) collective-permute-start(bf16[512,256]{1,0:T(8,128)(2,1)S(1)} %get-tuple-element.234), channel_id=1, source_target_pairs={{0,1},{1,3},{2,5},{3,7},{4,2},{5,0},{6,6},{7,4},{8,9},{9,11},{10,1... | collective-permute-start | bytes 786440 | tf_op jit(solution)/shard_map/ppermute | solution.py:1438
  307.0 26.6 %collective-permute-start.8 = (bf16[512,256]{1,0:T(8,128)(2,1)S(1)}, bf16[512,256]{1,0:T(8,128)(2,1)S(1)}, u32[]{:S(2)}, u32[]{:S(2)}) collective-permute-start(bf16[512,256]{1,0:T(8,128)(2,1)S(1)} %get-tuple-element.235), channel_id=1, source_target_pairs={{0,0},{1,2},{2,4},{3,6},{4,1},{5,3},{6,5},{7,7},{8,8},{9,10},{10,1... | collective-permute-start | bytes 786440 | tf_op jit(solution)/shard_map/ppermute | solution.py:1438
  337.7 4.5 collective-permute-start.15
  346.0 3.0 collective-permute-start.16
  367.5 42.2 %collective-permute-start.20 = (bf16[1024,512]{1,0:T(8,128)(2,1)}, bf16[1024,512]{1,0:T(8,128)(2,1)}, u32[]{:S(2)}, u32[]{:S(2)}) collective-permute-start(bf16[1024,512]{1,0:T(8,128)(2,1)} %add_convert_fusion.7), channel_id=1, source_target_pairs={{0,8},{4,12},{8,0},{12,4},{16,24},{20,28},{24,16},{28,20},{1,9},{5... | collective-permute-start | bytes 3145736 | tf_op jit(solution)/shard_map/ppermute | solution.py:1397
  368.7 7.6 %collective-permute-start.17 = (bf16[512,1024]{1,0:T(8,128)(2,1)S(1)}, bf16[512,1024]{1,0:T(8,128)(2,1)S(1)}, u32[]{:S(2)}, u32[]{:S(2)}) collective-permute-start(bf16[512,1024]{1,0:T(8,128)(2,1)S(1)} %copy-done.76), channel_id=1, source_target_pairs={{0,4},{4,0},{8,12},{12,8},{16,20},{20,16},{24,28},{28,24},{1,5},{5... | collective-permute-start | bytes 3145736 | tf_op jit(solution)/shard_map/ppermute | solution.py:1234
  373.2 36.6 %collective-permute-start.19 = (bf16[1024,512]{1,0:T(8,128)(2,1)}, bf16[1024,512]{1,0:T(8,128)(2,1)}, u32[]{:S(2)}, u32[]{:S(2)}) collective-permute-start(bf16[1024,512]{1,0:T(8,128)(2,1)} %add_convert_fusion.8), channel_id=1, source_target_pairs={{0,16},{4,20},{8,24},{12,28},{16,0},{20,4},{24,8},{28,12},{1,17},{... | collective-permute-start | bytes 3145736 | tf_op jit(solution)/shard_map/ppermute | solution.py:1397
  380.1 13.4 %collective-permute-start.18 = (bf16[512,1024]{1,0:T(8,128)(2,1)}, bf16[512,1024]{1,0:T(8,128)(2,1)}, u32[]{:S(2)}, u32[]{:S(2)}) collective-permute-start(bf16[512,1024]{1,0:T(8,128)(2,1)} %get-tuple-element.213), channel_id=1, source_target_pairs={{0,4},{4,0},{8,12},{12,8},{16,20},{20,16},{24,28},{28,24},{1,5},{5... | collective-permute-start | bytes 3145736 | tf_op jit(solution)/shard_map/ppermute | solution.py:1234
  391.3 38.6 %collective-permute-start.22 = (bf16[512,1024]{1,0:T(8,128)(2,1)}, bf16[512,1024]{1,0:T(8,128)(2,1)}, u32[]{:S(2)}, u32[]{:S(2)}) collective-permute-start(bf16[512,1024]{1,0:T(8,128)(2,1)} %get-tuple-element.229), channel_id=1, source_target_pairs={{0,8},{4,12},{8,0},{12,4},{16,24},{20,28},{24,16},{28,20},{1,9},{5... | collective-permute-start | bytes 3145736 | tf_op jit(solution)/shard_map/ppermute | solution.py:1397
  392.7 37.3 %collective-permute-start.21 = (bf16[512,1024]{1,0:T(8,128)(2,1)}, bf16[512,1024]{1,0:T(8,128)(2,1)}, u32[]{:S(2)}, u32[]{:S(2)}) collective-permute-start(bf16[512,1024]{1,0:T(8,128)(2,1)} %get-tuple-element.230), channel_id=1, source_target_pairs={{0,16},{4,20},{8,24},{12,28},{16,0},{20,4},{24,8},{28,12},{1,17},{... | collective-permute-start | bytes 3145736 | tf_op jit(solution)/shard_map/ppermute | solution.py:1397
  396.9 12.8 %copy-start.33 = (bf16[1024,2048]{1,0:T(8,128)(2,1)S(1)}, bf16[1024,2048]{1,0:T(8,128)(2,1)}, u32[]{:S(2)}) copy-start(bf16[1024,2048]{1,0:T(8,128)(2,1)} %get-tuple-element.110) | copy-start | bytes 12582916
  414.9 21.5 %collective-permute-start.23 = (bf16[1024,256]{1,0:T(8,128)(2,1)}, bf16[1024,256]{1,0:T(8,128)(2,1)S(1)}, u32[]{:S(2)}, u32[]{:S(2)}) collective-permute-start(bf16[1024,256]{1,0:T(8,128)(2,1)} %fusion.90), channel_id=1, source_target_pairs={{0,8},{4,12},{8,0},{12,4},{16,24},{20,28},{24,16},{28,20},{1,9},{5... | collective-permute-start | bytes 1572872 | tf_op jit(solution)/shard_map/ppermute | solution.py:1405
  416.3 20.0 %collective-permute-start.24 = (bf16[1024,256]{1,0:T(8,128)(2,1)S(1)}, bf16[1024,256]{1,0:T(8,128)(2,1)S(1)}, u32[]{:S(2)}, u32[]{:S(2)}) collective-permute-start(bf16[1024,256]{1,0:T(8,128)(2,1)S(1)} %fusion.87), channel_id=1, source_target_pairs={{0,16},{4,20},{8,24},{12,28},{16,0},{20,4},{24,8},{28,12},{1,17},{... | collective-permute-start | bytes 1572872 | tf_op jit(solution)/shard_map/ppermute | solution.py:1405
  444.4 9.9 %copy-start.72 = (bf16[1024,1536]{1,0:T(8,128)(2,1)S(1)}, bf16[1024,1536]{1,0:T(8,128)(2,1)}, u32[]{:S(2)}) copy-start(bf16[1024,1536]{1,0:T(8,128)(2,1)} %get-tuple-element.101) | copy-start | bytes 9437188
  446.8 21.0 %collective-permute-start.30 = (bf16[512,256]{1,0:T(8,128)(2,1)S(1)}, bf16[512,256]{1,0:T(8,128)(2,1)S(1)}, u32[]{:S(2)}, u32[]{:S(2)}) collective-permute-start(bf16[512,256]{1,0:T(8,128)(2,1)S(1)} %pad_maximum_fusion.17), channel_id=1, source_target_pairs={{0,1},{1,2},{2,3},{3,0},{4,5},{5,6},{6,7},{7,4},{8,9},{9,10},{10,1... | collective-permute-start | bytes 786440 | tf_op jit(solution)/shard_map/ppermute | solution.py:1421
  449.5 20.8 %collective-permute-start.31 = (bf16[512,256]{1,0:T(8,128)(2,1)S(1)}, bf16[512,256]{1,0:T(8,128)(2,1)S(1)}, u32[]{:S(2)}, u32[]{:S(2)}) collective-permute-start(bf16[512,256]{1,0:T(8,128)(2,1)S(1)} %pad_maximum_fusion.18), channel_id=1, source_target_pairs={{0,2},{1,3},{2,0},{3,1},{4,6},{5,7},{6,4},{7,5},{8,10},{9,11},{10,... | collective-permute-start | bytes 786440 | tf_op jit(solution)/shard_map/ppermute | solution.py:1421
  449.6 26.3 %collective-permute-start.32 = (bf16[512,256]{1,0:T(8,128)(2,1)S(1)}, bf16[512,256]{1,0:T(8,128)(2,1)S(1)}, u32[]{:S(2)}, u32[]{:S(2)}) collective-permute-start(bf16[512,256]{1,0:T(8,128)(2,1)S(1)} %pad_maximum_fusion.19), channel_id=1, source_target_pairs={{0,3},{1,0},{2,1},{3,2},{4,7},{5,4},{6,5},{7,6},{8,11},{9,8},{10,9... | collective-permute-start | bytes 786440 | tf_op jit(solution)/shard_map/ppermute | solution.py:1421
  452.2 12.5 %collective-permute-start.25 = (bf16[256,1024]{1,0:T(8,128)(2,1)S(1)}, bf16[256,1024]{1,0:T(8,128)(2,1)S(1)}, u32[]{:S(2)}, u32[]{:S(2)}) collective-permute-start(bf16[256,1024]{1,0:T(8,128)(2,1)S(1)} %get-tuple-element.169), channel_id=1, source_target_pairs={{0,8},{4,12},{8,0},{12,4},{16,24},{20,28},{24,16},{28,20},{1,9},{5... | collective-permute-start | bytes 1572872 | tf_op jit(solution)/shard_map/ppermute | solution.py:1405
  453.6 11.7 %collective-permute-start.26 = (bf16[256,1024]{1,0:T(8,128)(2,1)S(1)}, bf16[256,1024]{1,0:T(8,128)(2,1)S(1)}, u32[]{:S(2)}, u32[]{:S(2)}) collective-permute-start(bf16[256,1024]{1,0:T(8,128)(2,1)S(1)} %get-tuple-element.170), channel_id=1, source_target_pairs={{0,16},{4,20},{8,24},{12,28},{16,0},{20,4},{24,8},{28,12},{1,17},{... | collective-permute-start | bytes 1572872 | tf_op jit(solution)/shard_map/ppermute | solution.py:1405
  464.7 25.2 %collective-permute-start.33 = (bf16[512,1024]{1,0:T(8,128)(2,1)S(1)}, bf16[512,1024]{1,0:T(8,128)(2,1)S(1)}, u32[]{:S(2)}, u32[]{:S(2)}) collective-permute-start(bf16[512,1024]{1,0:T(8,128)(2,1)S(1)} %fusion.37), channel_id=1, source_target_pairs={{0,4},{4,0},{8,12},{12,8},{16,20},{20,16},{24,28},{28,24},{1,5},{5... | collective-permute-start | bytes 3145736 | tf_op jit(solution)/shard_map/ppermute | solution.py:1234
  467.7 22.2 %copy-start.16 = (f32[512,1024]{1,0:T(8,128)S(1)}, f32[512,1024]{1,0:T(8,128)}, u32[]{:S(2)}) copy-start(f32[512,1024]{1,0:T(8,128)} %get-tuple-element.214) | copy-start | bytes 6291460
  467.7 11.1 %collective-permute-start.27 = (bf16[256,512]{1,0:T(8,128)(2,1)S(1)}, bf16[256,512]{1,0:T(8,128)(2,1)S(1)}, u32[]{:S(2)}, u32[]{:S(2)}) collective-permute-start(bf16[256,512]{1,0:T(8,128)(2,1)S(1)} %pad_maximum_fusion.14), channel_id=1, source_target_pairs={{0,1},{1,2},{2,3},{3,0},{4,5},{5,6},{6,7},{7,4},{8,9},{9,10},{10,1... | collective-permute-start | bytes 786440 | tf_op jit(solution)/shard_map/ppermute | solution.py:1421
  467.9 21.9 %collective-permute-start.28 = (bf16[256,512]{1,0:T(8,128)(2,1)S(1)}, bf16[256,512]{1,0:T(8,128)(2,1)S(1)}, u32[]{:S(2)}, u32[]{:S(2)}) collective-permute-start(bf16[256,512]{1,0:T(8,128)(2,1)S(1)} %pad_maximum_fusion.15), channel_id=1, source_target_pairs={{0,2},{1,3},{2,0},{3,1},{4,6},{5,7},{6,4},{7,5},{8,10},{9,11},{10,... | collective-permute-start | bytes 786440 | tf_op jit(solution)/shard_map/ppermute | solution.py:1421
  470.2 19.6 %collective-permute-start.29 = (bf16[256,512]{1,0:T(8,128)(2,1)S(1)}, bf16[256,512]{1,0:T(8,128)(2,1)S(1)}, u32[]{:S(2)}, u32[]{:S(2)}) collective-permute-start(bf16[256,512]{1,0:T(8,128)(2,1)S(1)} %pad_maximum_fusion.16), channel_id=1, source_target_pairs={{0,3},{1,0},{2,1},{3,2},{4,7},{5,4},{6,5},{7,6},{8,11},{9,8},{10,9... | collective-permute-start | bytes 786440 | tf_op jit(solution)/shard_map/ppermute | solution.py:1421
  (67 other events, 253.1 us)

commit v5 on v4

--- a/solution.py
+++ b/solution.py
@@ -697,7 +697,7 @@
         cp.wait_send()
 
 
-TOKEN_TICK = 7
+TOKEN_TICK = 9
 
 
 def gather_all(q, k, v, proj, inner, outer, small, x_rolled, g_rolled):
@@ -935,7 +935,7 @@
         sb[step + 1] = sb[step] + sg[slot]
 
     sb[0] = small_ref[...]
-    for group in range(4):
+    for group in range(2):
         start_first(group)
     small_send(0, 0, mate, depth)
     send_core(OUTER)
@@ -947,6 +947,8 @@
     finish(INNER)
     for group in range(4):
         start_second(group)
+        if group + 2 < 4:
+            start_first(group + 2)
         if group == 0:
             small_add(1, 1)
             small_send(2, 2, y_row, depth)

time: 572 us -> 566 us (0.990)
  Pallas kernels: 299 us -> 292 us
where the time goes in v5:
time: 566 us; the launch traced here: 559 us
  Pallas kernels  292 us (52%)
  matrix products  127 us (22%)
  other arithmetic  38.1 us (7%)
  starting transfers between devices  37.6 us (7%)
  waiting for transfers between devices  28.7 us (5%)
  local copies, waits for them, and re-layouts  27.3 us (5%)
  between operations  8.98 us (2%)
    pallas_call x1, Pallas kernels, gather_all(): pl.pallas_call(gather_kernel, out_shape=(sd((1024, 1536), BF16), sd((512,...  127 us
    pallas_call x1, Pallas kernels, scatter_all(): pl.pallas_call(scatter_kernel, out_shape=tuple((sd(size, F32) for size in...  60 us
    dot_general x17, matrix products, over_tokens(): lax.dot_general(left, right, (((0,), (0,)), ((), ())), preferred_element_...  55 us
    pallas_call x3, Pallas kernels, attend_back(): pl.pallas_call(attend_back_kernel, out_shape=(shape, shape, shape), grid_...  50.2 us
    dot_general x12, matrix products, against(): lax.dot_general(left, right, (((1,), (1,)), ((), ())), preferred_element_...  40 us
    dot_general x10, matrix products, matmul(): return jnp.dot(left, right, preferred_element_type=jnp.float32)  31.8 us
    pallas_call x2, Pallas kernels, ffn_in(): pl.pallas_call(ffn_in_kernel, out_shape=(shape, shape), grid=(hidden // c...  27.5 us
    pallas_call x2, Pallas kernels, attend(): pl.pallas_call(attend_kernel, out_shape=(jax.ShapeDtypeStruct((tokens, wi...  26.5 us
  transfers between devices with their start and end apart: 34, of which 12 were waited for; matrix products, arithmetic and copies ran while one was open for 16% of the time, Pallas kernels for 32%

profile of v5, /device:TPU:0, one launch (start us, length us, event | category | flops | bytes accessed | tf_op | source)
XLA Modules:
  0.0 559.1 jit_solution(16254548066724908662)
XLA Ops:
  5.0 5.2 fusion.101
  10.3 127.2 %shard_map.305 = (bf16[1024,1536]{1,0:T(8,128)(2,1)}, bf16[512,1024]{1,0:T(8,128)(2,1)}, bf16[1024,2048]{1,0:T(8,128)(2,1)}, bf16[2048,1024]{1,0:T(8,128)(2,1)},...) custom-call(bf16[128,256]{1,0:T(8,128)(2,1)} %q_ref.1, bf16[128,256]{1,0:T(8,128)(2,1)} %k_ref.1, ...), custom_call_target="tpu_custom_call" | custom-call | tf_op jit(solution)/shard_map/pallas_call | solution.py:706
  138.4 7.6 %add_convert_fusion.2.q_ref.k_ref.v_ref = bf16[1024,1536]{1,0:T(8,128)(2,1)} fusion(bf16[1024,1024]{1,0:T(8,128)(2,1)} %get-tuple-element.100, bf16[1024,1536]{1,0:T(8,128)(2,1)} %get-tuple-element.101, f32[1536]{0:T(1024)S(1)} %fusion.120), kind=kOutput, calls=%fused_computation.6 | convolution fusion | flops 3224371200 | bytes 8394752 | tf_op jit(solution)/shard_map/dot_general | solution.py:26
  149.4 13.3 %attend.2 = (bf16[1024,512]{1,0:T(8,128)(2,1)S(1)}, f32[1024,512]{1,0:T(8,128)S(1)}) custom-call(s32[1]{0:T(128)} %bitcast.1.flag_ref, bf16[1024,1536]{1,0:T(8,128)(2,1)} %add_convert_fusion.2.q_ref.k_ref.v_ref, bf16[1024,1536]{1,0:T(8,128)(2,1)} %add_convert_fusion.2.q_ref.k_ref.v_ref, bf16[1024,1536]{1,0:T(8,128)(2,1)} %add_convert_fusion.2.q_ref.k_ref.v_ref, ...), custom_call_target="tpu_custom_call" | custom-call | flops 20000000000 | bytes 8000000 | tf_op jit(solution)/shard_map/attend/pallas_call | solution.py:1062
  172.1 2.8 collective-permute-done.2
  176.6 13.8 %ffn_in.2 = (bf16[1024,2048]{1,0:T(8,128)(2,1)}, bf16[1024,2048]{1,0:T(8,128)(2,1)}) custom-call(bf16[1024,1024]{1,0:T(8,128)(2,1)S(1)} %pad_maximum_fusion.2.x_ref, bf16[1024,2048]{1,0:T(8,128)(2,1)} %get-tuple-element.109.w_ref, f32[1,2048]{1,0:T(1,128)S(1)} %reshape.282.b_ref), custom_call_target="tpu_custom_call" | custom-call | flops 14000000000 | bytes 14000000 | tf_op jit(solution)/shard_map/ffn_in/pallas_call | solution.py:1214
  193.2 4.7 fusion.40
  198.1 2.3 fusion.147
  202.4 2.4 collective-permute-done.4
  205.8 5.6 %add_convert_fusion.1.q_ref.k_ref.v_ref = bf16[1024,1536]{1,0:T(8,128)(2,1)} fusion(bf16[1024,1536]{1,0:T(8,128)(2,1)S(1)} %copy-done.70, f32[1536]{0:T(1024)S(1)} %fusion.120, bf16[512,1024]{1,0:T(8,128)(2,1)S(1)} %collective-permute-done.4, bf16[512,1024]{1,0:T(8,128)(2,1)S(1)} %fusion.16), kind=kOutput, calls=%fused_computation.5 | convolution fusion | flops 3228565504 | bytes 8394752 | tf_op jit(solution)/shard_map/dot_general | solution.py:26
  211.4 13.3 %attend.3 = (bf16[1024,512]{1,0:T(8,128)(2,1)S(1)}, f32[1024,512]{1,0:T(8,128)S(1)}) custom-call(s32[1]{0:T(128)} %bitcast.1.flag_ref, bf16[1024,1536]{1,0:T(8,128)(2,1)} %add_convert_fusion.1.q_ref.k_ref.v_ref, bf16[1024,1536]{1,0:T(8,128)(2,1)} %add_convert_fusion.1.q_ref.k_ref.v_ref, bf16[1024,1536]{1,0:T(8,128)(2,1)} %add_convert_fusion.1.q_ref.k_ref.v_ref, ...), custom_call_target="tpu_custom_call" | custom-call | flops 20000000000 | bytes 8000000 | tf_op jit(solution)/shard_map/attend/pallas_call | solution.py:1062
  230.0 2.4 collective-permute-done.6
  233.4 13.7 %ffn_in.3 = (bf16[1024,2048]{1,0:T(8,128)(2,1)}, bf16[1024,2048]{1,0:T(8,128)(2,1)}) custom-call(bf16[1024,1024]{1,0:T(8,128)(2,1)S(1)} %pad_maximum_fusion.4.x_ref, bf16[1024,2048]{1,0:T(8,128)(2,1)} %get-tuple-element.109.w_ref, f32[1,2048]{1,0:T(1,128)S(1)} %reshape.282.b_ref), custom_call_target="tpu_custom_call" | custom-call | flops 14000000000 | bytes 14000000 | tf_op jit(solution)/shard_map/ffn_in/pallas_call | solution.py:1214
  247.2 4.1 fusion.43
  251.9 2.3 fusion.149
  257.6 2.4 collective-permute-done.12
  260.0 5.3 convert_reduce_fusion.1
  265.3 3.4 fusion.46
  272.5 9.6 %convolution_convert_fusion = bf16[2048,1024]{1,0:T(8,128)(2,1)} fusion(bf16[1024,2048]{1,0:T(8,128)(2,1)} %get-tuple-element.121, bf16[512,1024]{1,0:T(8,128)(2,1)} %copy-done.75, bf16[512,1024]{1,0:T(8,128)(2,1)} %copy-done.44), kind=kOutput, calls=%fused_computation.7 | convolution fusion | flops 4301258752 | bytes 10485760 | tf_op jit(solution)/shard_map/dot_general | solution.py:30
  282.1 4.9 multiply_reduce_fusion.2
  290.2 6.5 %fusion.137 = bf16[1024,2048]{1,0:T(8,128)(2,1)} fusion(bf16[1024,2048]{1,0:T(8,128)(2,1)S(1)} %copy-done.37, bf16[512,1024]{1,0:T(8,128)(2,1)S(1)} %copy-done.43, bf16[512,1024]{1,0:T(8,128)(2,1)S(1)} %copy-done.27), kind=kOutput, calls=%fused_computation.319 | convolution fusion | flops 4299161600 | bytes 10485760 | tf_op jit(solution)/shard_map/dot_general | solution.py:30
  296.9 6.1 %collective-permute-start.11 = (bf16[512,256]{1,0:T(8,128)(2,1)S(1)}, bf16[512,256]{1,0:T(8,128)(2,1)S(1)}, u32[]{:S(2)}, u32[]{:S(2)}) collective-permute-start(bf16[512,256]{1,0:T(8,128)(2,1)S(1)} %get-tuple-element.232), channel_id=1, source_target_pairs={{0,3},{1,1},{2,7},{3,5},{4,0},{5,2},{6,4},{7,6},{8,11},{9,9},{10,1... | collective-permute-start | bytes 786440 | tf_op jit(solution)/shard_map/ppermute | solution.py:1440
  303.5 3.5 collective-permute-start.9
  309.2 24.4 %attend_back.3 = (bf16[1024,512]{1,0:T(8,128)(2,1)S(1)}, bf16[1024,512]{1,0:T(8,128)(2,1)S(1)}, bf16[1024,512]{1,0:T(8,128)(2,1)S(1)}) custom-call(s32[1]{0:T(128)} %bitcast.1.flag_ref, bf16[1024,1536]{1,0:T(8,128)(2,1)} %add_convert_fusion.1.q_ref.k_ref.v_ref, bf16[1024,1536]{1,0:T(8,128)(2,1)} %add_convert_fusion.1.q_ref.k_ref.v_ref, ...), custom_call_target="tpu_custom_call" | custom-call | flops 40000000000 | bytes 10000000 | tf_op jit(solution)/shard_map/attend_back/pallas_call | solution.py:1147
  342.9 2.3 convert_reduce_fusion.3
  348.2 8.7 %convert_reduce_fusion = (f32[2048]{0:T(1024)S(1)}, bf16[1024,2048]{1,0:T(8,128)(2,1)S(1)}) fusion(bf16[1024,2048]{1,0:T(8,128)(2,1)} %get-tuple-element.143, bf16[2048,1024]{1,0:T(8,128)(2,1)} %get-tuple-element.111, bf16[512,1024]{1,0:T(8,128)(2,1)} %collective-permute-done.16, bf16[512,1024]{1,0:T(8,128)(2,1)} %get-tuple-element.208), kind=kOutput, calls=%fused_computation | convolution fusion | flops 4309645312 | bytes 14688256 | tf_op jit(solution)/shard_map/dot_general | solution.py:36
  357.0 3.4 fusion.49
  361.9 4.8 add_convert_fusion.7
  368.2 4.1 add_convert_fusion.8
  373.0 2.4 fusion.151
  376.9 2.3 convert_reduce_fusion.5
  380.4 6.5 %add_convert_fusion = bf16[1024,2048]{1,0:T(8,128)(2,1)S(1)} fusion(bf16[1024,2048]{1,0:T(8,128)(2,1)S(1)} %copy-done.77, bf16[1024,2048]{1,0:T(8,128)(2,1)S(1)} %copy-done.39, bf16[512,1024]{1,0:T(8,128)(2,1)} %collective-permute-done.2, bf16[512,1024]{1,0:T(8,128)(2,1)} %fusion.15), kind=kOutput, calls=%fused_computation.2 | convolution fusion | flops 4305453056 | bytes 14680064 | tf_op jit(solution)/shard_map/dot_general | solution.py:30
  392.7 3.3 convolution_convert_fusion.1.do_ref
  396.0 12.8 %attend_back.4 = (bf16[1024,256]{1,0:T(8,128)(2,1)S(1)}, bf16[1024,256]{1,0:T(8,128)(2,1)S(1)}, bf16[1024,256]{1,0:T(8,128)(2,1)S(1)}) custom-call(s32[1]{0:T(128)} %bitcast.1.flag_ref, bf16[1024,1536]{1,0:T(8,128)(2,1)} %add_convert_fusion.2.q_ref.k_ref.v_ref, bf16[1024,1536]{1,0:T(8,128)(2,1)} %add_convert_fusion.2.q_ref.k_ref.v_ref, ...), custom_call_target="tpu_custom_call" | custom-call | flops 20000000000 | bytes 5000000 | tf_op jit(solution)/shard_map/attend_back/pallas_call | solution.py:1147
  408.9 3.0 fusion.90
  416.1 13.0 %attend_back.5 = (bf16[1024,256]{1,0:T(8,128)(2,1)S(1)}, bf16[1024,256]{1,0:T(8,128)(2,1)S(1)}, bf16[1024,256]{1,0:T(8,128)(2,1)S(1)}) custom-call(s32[1]{0:T(128)} %bitcast.1.flag_ref, bf16[1024,1536]{1,0:T(8,128)(2,1)} %add_convert_fusion.2.q_ref.k_ref.v_ref, bf16[1024,1536]{1,0:T(8,128)(2,1)} %add_convert_fusion.2.q_ref.k_ref.v_ref, ...), custom_call_target="tpu_custom_call" | custom-call | flops 20000000000 | bytes 5000000 | tf_op jit(solution)/shard_map/attend_back/pallas_call | solution.py:1147
  431.1 3.0 fusion.86
  443.6 2.3 fusion.93
  446.0 2.9 collective-permute-start.30
  449.4 2.2 collective-permute-start.32
  455.6 2.3 add_convert_fusion.5.refs_2_
  457.9 2.3 add_convert_fusion.4.refs_3_
  467.5 2.3 collective-permute-start.28
  469.8 5.5 collective-permute-start.29
  475.4 3.1 collective-permute-done.27
  478.5 10.4 %collective-permute-done.28 = bf16[256,512]{1,0:T(8,128)(2,1)S(1)} collective-permute-done((bf16[256,512]{1,0:T(8,128)(2,1)S(1)}, bf16[256,512]{1,0:T(8,128)(2,1)S(1)}, u32[]{:S(2)}, u32[]{:S(2)}) %collective-permute-start.28) | collective-permute-done | bytes 262176 | tf_op jit(solution)/shard_map/ppermute | solution.py:1423
  490.7 60.0 %shard_map.306 = (f32[256,128]{1,0:T(8,128)S(1)}, f32[128,256]{1,0:T(8,128)S(1)}, f32[128,256]{1,0:T(8,128)S(1)}, f32[128,256]{1,0:T(8,128)S(1)}, f32[128,1024]{...) custom-call(bf16[512,1024]{1,0:T(8,128)(2,1)S(1)} %add_convert_fusion.9.refs_0_, ...), custom_call_target="tpu_custom_call" | custom-call | tf_op jit(solution)/shard_map/pallas_call | solution.py:995
  551.4 2.6 fusion.100
  (402 shorter events, 97.7 us)
Async XLA Ops:
  0.8 145.2 %collective-permute-start = (s32[2048]{0:T(1024)}, s32[2048]{0:T(1024)S(1)}, u32[]{:S(2)}, u32[]{:S(2)}) collective-permute-start(s32[2048]{0:T(1024)} %bitcast.156), channel_id=1, source_target_pairs={{0,4},{4,0},{8,12},{12,8},{16,20},{20,16},{24,28},{28,24},{1,5},{5... | collective-permute-start | bytes 24584 | tf_op jit(solution)/shard_map/ppermute | solution.py:1236
  149.4 62.0 %copy-start.2 = (s32[1,1024]{0,1:T(8,128)}, s32[1,1024]{0,1:T(8,128)S(1)}, u32[]{:S(2)}) copy-start(s32[1,1024]{0,1:T(8,128)S(1)} %copy.53) | copy-start | bytes 12292
  149.4 14.3 %copy-start.18 = (bf16[512,1024]{1,0:T(8,128)(2,1)S(1)}, bf16[512,1024]{1,0:T(8,128)(2,1)}, u32[]{:S(2)}) copy-start(bf16[512,1024]{1,0:T(8,128)(2,1)} %get-tuple-element.104) | copy-start | bytes 3145732
  165.3 3.0 collective-permute-start.1
  170.2 30.4 %copy-start.10 = (f32[512,1024]{1,0:T(8,128)}, f32[512,1024]{1,0:T(8,128)S(1)}, u32[]{:S(2)}) copy-start(f32[512,1024]{1,0:T(8,128)S(1)} %get-tuple-element.224) | copy-start | bytes 6291460
  170.3 30.4 %copy-start.49 = (f32[512]{0:T(512)}, f32[512]{0:T(512)S(1)}, u32[]{:S(2)}) copy-start(f32[512]{0:T(512)S(1)} %get-tuple-element.310) | copy-start | bytes 6148
  170.3 30.4 %copy-start.51 = (f32[512]{0:T(512)}, f32[512]{0:T(512)S(1)}, u32[]{:S(2)}) copy-start(f32[512]{0:T(512)S(1)} %get-tuple-element.311) | copy-start | bytes 6148
  171.9 3.0 collective-permute-start.2
  197.9 2.7 collective-permute-start.3
  201.6 26.6 %copy-start.12 = (f32[512,1024]{1,0:T(8,128)}, f32[512,1024]{1,0:T(8,128)S(1)}, u32[]{:S(2)}) copy-start(f32[512,1024]{1,0:T(8,128)S(1)} %get-tuple-element.223) | copy-start | bytes 6291460
  202.1 2.7 collective-permute-start.4
  211.4 13.4 %copy-start.19 = (bf16[512,1024]{1,0:T(8,128)(2,1)S(1)}, bf16[512,1024]{1,0:T(8,128)(2,1)}, u32[]{:S(2)}) copy-start(bf16[512,1024]{1,0:T(8,128)(2,1)} %get-tuple-element.104) | copy-start | bytes 3145732
  225.5 2.7 collective-permute-start.5
  229.7 2.7 collective-permute-start.6
  233.4 13.7 %copy-start.69 = (bf16[2048,1024]{1,0:T(8,128)(2,1)S(1)}, bf16[2048,1024]{1,0:T(8,128)(2,1)}, u32[]{:S(2)}) copy-start(bf16[2048,1024]{1,0:T(8,128)(2,1)} %get-tuple-element.111) | copy-start | bytes 12582916
  251.6 2.7 collective-permute-start.7
  257.2 2.7 collective-permute-start.12
  270.2 11.9 %collective-permute-start.13 = (bf16[512,1024]{1,0:T(8,128)(2,1)}, bf16[512,1024]{1,0:T(8,128)(2,1)}, u32[]{:S(2)}, u32[]{:S(2)}) collective-permute-start(bf16[512,1024]{1,0:T(8,128)(2,1)} %fusion.46), channel_id=1, source_target_pairs={{0,4},{4,0},{8,12},{12,8},{16,20},{20,16},{24,28},{28,24},{1,5},{5... | collective-permute-start | bytes 3145736 | tf_op jit(solution)/shard_map/ppermute | solution.py:1236
  272.4 9.6 %copy-start.15 = (f32[512,1024]{1,0:T(8,128)S(1)}, f32[512,1024]{1,0:T(8,128)}, u32[]{:S(2)}) copy-start(f32[512,1024]{1,0:T(8,128)} %copy-done.14) | copy-start | bytes 6291460
  287.8 20.0 %copy-start.22 = (bf16[512,1024]{1,0:T(8,128)(2,1)}, bf16[512,1024]{1,0:T(8,128)(2,1)S(1)}, u32[]{:S(2)}) copy-start(bf16[512,1024]{1,0:T(8,128)(2,1)S(1)} %get-tuple-element.216) | copy-start | bytes 3145732
  287.8 20.0 %collective-permute-start.14 = (bf16[512,1024]{1,0:T(8,128)(2,1)S(1)}, bf16[512,1024]{1,0:T(8,128)(2,1)S(1)}, u32[]{:S(2)}, u32[]{:S(2)}) collective-permute-start(bf16[512,1024]{1,0:T(8,128)(2,1)S(1)} %get-tuple-element.216), channel_id=1, source_target_pairs={{0,4},{4,0},{8,12},{12,8},{16,20},{20,16},{24,28},{28,24},{1,5},{5... | collective-permute-start | bytes 3145736 | tf_op jit(solution)/shard_map/ppermute | solution.py:1236
  296.8 11.1 %copy-start.20 = (bf16[512,1024]{1,0:T(8,128)(2,1)S(1)}, bf16[512,1024]{1,0:T(8,128)(2,1)}, u32[]{:S(2)}) copy-start(bf16[512,1024]{1,0:T(8,128)(2,1)} %get-tuple-element.104) | copy-start | bytes 3145732
  296.9 36.7 %collective-permute-start.11 = (bf16[512,256]{1,0:T(8,128)(2,1)S(1)}, bf16[512,256]{1,0:T(8,128)(2,1)S(1)}, u32[]{:S(2)}, u32[]{:S(2)}) collective-permute-start(bf16[512,256]{1,0:T(8,128)(2,1)S(1)} %get-tuple-element.232), channel_id=1, source_target_pairs={{0,3},{1,1},{2,7},{3,5},{4,0},{5,2},{6,4},{7,6},{8,11},{9,9},{10,1... | collective-permute-start | bytes 786440 | tf_op jit(solution)/shard_map/ppermute | solution.py:1440
  303.0 30.6 %collective-permute-start.10 = (bf16[512,256]{1,0:T(8,128)(2,1)S(1)}, bf16[512,256]{1,0:T(8,128)(2,1)S(1)}, u32[]{:S(2)}, u32[]{:S(2)}) collective-permute-start(bf16[512,256]{1,0:T(8,128)(2,1)S(1)} %get-tuple-element.233), channel_id=1, source_target_pairs={{0,2},{1,0},{2,6},{3,4},{4,3},{5,1},{6,7},{7,5},{8,10},{9,8},{10,1... | collective-permute-start | bytes 786440 | tf_op jit(solution)/shard_map/ppermute | solution.py:1440
  303.5 30.2 %collective-permute-start.9 = (bf16[512,256]{1,0:T(8,128)(2,1)S(1)}, bf16[512,256]{1,0:T(8,128)(2,1)S(1)}, u32[]{:S(2)}, u32[]{:S(2)}) collective-permute-start(bf16[512,256]{1,0:T(8,128)(2,1)S(1)} %get-tuple-element.234), channel_id=1, source_target_pairs={{0,1},{1,3},{2,5},{3,7},{4,2},{5,0},{6,6},{7,4},{8,9},{9,11},{10,1... | collective-permute-start | bytes 786440 | tf_op jit(solution)/shard_map/ppermute | solution.py:1440
  307.0 26.6 %collective-permute-start.8 = (bf16[512,256]{1,0:T(8,128)(2,1)S(1)}, bf16[512,256]{1,0:T(8,128)(2,1)S(1)}, u32[]{:S(2)}, u32[]{:S(2)}) collective-permute-start(bf16[512,256]{1,0:T(8,128)(2,1)S(1)} %get-tuple-element.235), channel_id=1, source_target_pairs={{0,0},{1,2},{2,4},{3,6},{4,1},{5,3},{6,5},{7,7},{8,8},{9,10},{10,1... | collective-permute-start | bytes 786440 | tf_op jit(solution)/shard_map/ppermute | solution.py:1440
  337.7 3.7 collective-permute-start.15
  345.2 3.0 collective-permute-start.16
  366.7 42.1 %collective-permute-start.20 = (bf16[1024,512]{1,0:T(8,128)(2,1)}, bf16[1024,512]{1,0:T(8,128)(2,1)}, u32[]{:S(2)}, u32[]{:S(2)}) collective-permute-start(bf16[1024,512]{1,0:T(8,128)(2,1)} %add_convert_fusion.7), channel_id=1, source_target_pairs={{0,8},{4,12},{8,0},{12,4},{16,24},{20,28},{24,16},{28,20},{1,9},{5... | collective-permute-start | bytes 3145736 | tf_op jit(solution)/shard_map/ppermute | solution.py:1399
  368.1 7.3 %collective-permute-start.17 = (bf16[512,1024]{1,0:T(8,128)(2,1)S(1)}, bf16[512,1024]{1,0:T(8,128)(2,1)S(1)}, u32[]{:S(2)}, u32[]{:S(2)}) collective-permute-start(bf16[512,1024]{1,0:T(8,128)(2,1)S(1)} %copy-done.76), channel_id=1, source_target_pairs={{0,4},{4,0},{8,12},{12,8},{16,20},{20,16},{24,28},{28,24},{1,5},{5... | collective-permute-start | bytes 3145736 | tf_op jit(solution)/shard_map/ppermute | solution.py:1236
  372.4 36.5 %collective-permute-start.19 = (bf16[1024,512]{1,0:T(8,128)(2,1)}, bf16[1024,512]{1,0:T(8,128)(2,1)}, u32[]{:S(2)}, u32[]{:S(2)}) collective-permute-start(bf16[1024,512]{1,0:T(8,128)(2,1)} %add_convert_fusion.8), channel_id=1, source_target_pairs={{0,16},{4,20},{8,24},{12,28},{16,0},{20,4},{24,8},{28,12},{1,17},{... | collective-permute-start | bytes 3145736 | tf_op jit(solution)/shard_map/ppermute | solution.py:1399
  379.3 13.4 %collective-permute-start.18 = (bf16[512,1024]{1,0:T(8,128)(2,1)}, bf16[512,1024]{1,0:T(8,128)(2,1)}, u32[]{:S(2)}, u32[]{:S(2)}) collective-permute-start(bf16[512,1024]{1,0:T(8,128)(2,1)} %get-tuple-element.213), channel_id=1, source_target_pairs={{0,4},{4,0},{8,12},{12,8},{16,20},{20,16},{24,28},{28,24},{1,5},{5... | collective-permute-start | bytes 3145736 | tf_op jit(solution)/shard_map/ppermute | solution.py:1236
  390.4 38.6 %collective-permute-start.22 = (bf16[512,1024]{1,0:T(8,128)(2,1)}, bf16[512,1024]{1,0:T(8,128)(2,1)}, u32[]{:S(2)}, u32[]{:S(2)}) collective-permute-start(bf16[512,1024]{1,0:T(8,128)(2,1)} %get-tuple-element.229), channel_id=1, source_target_pairs={{0,8},{4,12},{8,0},{12,4},{16,24},{20,28},{24,16},{28,20},{1,9},{5... | collective-permute-start | bytes 3145736 | tf_op jit(solution)/shard_map/ppermute | solution.py:1399
  391.9 37.2 %collective-permute-start.21 = (bf16[512,1024]{1,0:T(8,128)(2,1)}, bf16[512,1024]{1,0:T(8,128)(2,1)}, u32[]{:S(2)}, u32[]{:S(2)}) collective-permute-start(bf16[512,1024]{1,0:T(8,128)(2,1)} %get-tuple-element.230), channel_id=1, source_target_pairs={{0,16},{4,20},{8,24},{12,28},{16,0},{20,4},{24,8},{28,12},{1,17},{... | collective-permute-start | bytes 3145736 | tf_op jit(solution)/shard_map/ppermute | solution.py:1399
  396.0 12.8 %copy-start.33 = (bf16[1024,2048]{1,0:T(8,128)(2,1)S(1)}, bf16[1024,2048]{1,0:T(8,128)(2,1)}, u32[]{:S(2)}) copy-start(bf16[1024,2048]{1,0:T(8,128)(2,1)} %get-tuple-element.110) | copy-start | bytes 12582916
  414.0 21.5 %collective-permute-start.23 = (bf16[1024,256]{1,0:T(8,128)(2,1)}, bf16[1024,256]{1,0:T(8,128)(2,1)S(1)}, u32[]{:S(2)}, u32[]{:S(2)}) collective-permute-start(bf16[1024,256]{1,0:T(8,128)(2,1)} %fusion.90), channel_id=1, source_target_pairs={{0,8},{4,12},{8,0},{12,4},{16,24},{20,28},{24,16},{28,20},{1,9},{5... | collective-permute-start | bytes 1572872 | tf_op jit(solution)/shard_map/ppermute | solution.py:1407
  415.5 20.0 %collective-permute-start.24 = (bf16[1024,256]{1,0:T(8,128)(2,1)S(1)}, bf16[1024,256]{1,0:T(8,128)(2,1)S(1)}, u32[]{:S(2)}, u32[]{:S(2)}) collective-permute-start(bf16[1024,256]{1,0:T(8,128)(2,1)S(1)} %fusion.87), channel_id=1, source_target_pairs={{0,16},{4,20},{8,24},{12,28},{16,0},{20,4},{24,8},{28,12},{1,17},{... | collective-permute-start | bytes 1572872 | tf_op jit(solution)/shard_map/ppermute | solution.py:1407
  443.5 10.1 %copy-start.72 = (bf16[1024,1536]{1,0:T(8,128)(2,1)S(1)}, bf16[1024,1536]{1,0:T(8,128)(2,1)}, u32[]{:S(2)}) copy-start(bf16[1024,1536]{1,0:T(8,128)(2,1)} %get-tuple-element.101) | copy-start | bytes 9437188
  446.0 21.5 %collective-permute-start.30 = (bf16[512,256]{1,0:T(8,128)(2,1)S(1)}, bf16[512,256]{1,0:T(8,128)(2,1)S(1)}, u32[]{:S(2)}, u32[]{:S(2)}) collective-permute-start(bf16[512,256]{1,0:T(8,128)(2,1)S(1)} %pad_maximum_fusion.17), channel_id=1, source_target_pairs={{0,1},{1,2},{2,3},{3,0},{4,5},{5,6},{6,7},{7,4},{8,9},{9,10},{10,1... | collective-permute-start | bytes 786440 | tf_op jit(solution)/shard_map/ppermute | solution.py:1423
  448.9 21.0 %collective-permute-start.31 = (bf16[512,256]{1,0:T(8,128)(2,1)S(1)}, bf16[512,256]{1,0:T(8,128)(2,1)S(1)}, u32[]{:S(2)}, u32[]{:S(2)}) collective-permute-start(bf16[512,256]{1,0:T(8,128)(2,1)S(1)} %pad_maximum_fusion.18), channel_id=1, source_target_pairs={{0,2},{1,3},{2,0},{3,1},{4,6},{5,7},{6,4},{7,5},{8,10},{9,11},{10,... | collective-permute-start | bytes 786440 | tf_op jit(solution)/shard_map/ppermute | solution.py:1423
  449.4 25.9 %collective-permute-start.32 = (bf16[512,256]{1,0:T(8,128)(2,1)S(1)}, bf16[512,256]{1,0:T(8,128)(2,1)S(1)}, u32[]{:S(2)}, u32[]{:S(2)}) collective-permute-start(bf16[512,256]{1,0:T(8,128)(2,1)S(1)} %pad_maximum_fusion.19), channel_id=1, source_target_pairs={{0,3},{1,0},{2,1},{3,2},{4,7},{5,4},{6,5},{7,6},{8,11},{9,8},{10,9... | collective-permute-start | bytes 786440 | tf_op jit(solution)/shard_map/ppermute | solution.py:1423
  451.6 12.3 %collective-permute-start.25 = (bf16[256,1024]{1,0:T(8,128)(2,1)S(1)}, bf16[256,1024]{1,0:T(8,128)(2,1)S(1)}, u32[]{:S(2)}, u32[]{:S(2)}) collective-permute-start(bf16[256,1024]{1,0:T(8,128)(2,1)S(1)} %get-tuple-element.169), channel_id=1, source_target_pairs={{0,8},{4,12},{8,0},{12,4},{16,24},{20,28},{24,16},{28,20},{1,9},{5... | collective-permute-start | bytes 1572872 | tf_op jit(solution)/shard_map/ppermute | solution.py:1407
  453.0 11.9 %collective-permute-start.26 = (bf16[256,1024]{1,0:T(8,128)(2,1)S(1)}, bf16[256,1024]{1,0:T(8,128)(2,1)S(1)}, u32[]{:S(2)}, u32[]{:S(2)}) collective-permute-start(bf16[256,1024]{1,0:T(8,128)(2,1)S(1)} %get-tuple-element.170), channel_id=1, source_target_pairs={{0,16},{4,20},{8,24},{12,28},{16,0},{20,4},{24,8},{28,12},{1,17},{... | collective-permute-start | bytes 1572872 | tf_op jit(solution)/shard_map/ppermute | solution.py:1407
  463.9 25.2 %collective-permute-start.33 = (bf16[512,1024]{1,0:T(8,128)(2,1)S(1)}, bf16[512,1024]{1,0:T(8,128)(2,1)S(1)}, u32[]{:S(2)}, u32[]{:S(2)}) collective-permute-start(bf16[512,1024]{1,0:T(8,128)(2,1)S(1)} %fusion.37), channel_id=1, source_target_pairs={{0,4},{4,0},{8,12},{12,8},{16,20},{20,16},{24,28},{28,24},{1,5},{5... | collective-permute-start | bytes 3145736 | tf_op jit(solution)/shard_map/ppermute | solution.py:1236
  467.3 21.8 %copy-start.16 = (f32[512,1024]{1,0:T(8,128)S(1)}, f32[512,1024]{1,0:T(8,128)}, u32[]{:S(2)}) copy-start(f32[512,1024]{1,0:T(8,128)} %get-tuple-element.214) | copy-start | bytes 6291460
  467.3 11.2 %collective-permute-start.27 = (bf16[256,512]{1,0:T(8,128)(2,1)S(1)}, bf16[256,512]{1,0:T(8,128)(2,1)S(1)}, u32[]{:S(2)}, u32[]{:S(2)}) collective-permute-start(bf16[256,512]{1,0:T(8,128)(2,1)S(1)} %pad_maximum_fusion.14), channel_id=1, source_target_pairs={{0,1},{1,2},{2,3},{3,0},{4,5},{5,6},{6,7},{7,4},{8,9},{9,10},{10,1... | collective-permute-start | bytes 786440 | tf_op jit(solution)/shard_map/ppermute | solution.py:1423
  467.5 21.5 %collective-permute-start.28 = (bf16[256,512]{1,0:T(8,128)(2,1)S(1)}, bf16[256,512]{1,0:T(8,128)(2,1)S(1)}, u32[]{:S(2)}, u32[]{:S(2)}) collective-permute-start(bf16[256,512]{1,0:T(8,128)(2,1)S(1)} %pad_maximum_fusion.15), channel_id=1, source_target_pairs={{0,2},{1,3},{2,0},{3,1},{4,6},{5,7},{6,4},{7,5},{8,10},{9,11},{10,... | collective-permute-start | bytes 786440 | tf_op jit(solution)/shard_map/ppermute | solution.py:1423
  469.8 19.2 %collective-permute-start.29 = (bf16[256,512]{1,0:T(8,128)(2,1)S(1)}, bf16[256,512]{1,0:T(8,128)(2,1)S(1)}, u32[]{:S(2)}, u32[]{:S(2)}) collective-permute-start(bf16[256,512]{1,0:T(8,128)(2,1)S(1)} %pad_maximum_fusion.16), channel_id=1, source_target_pairs={{0,3},{1,0},{2,1},{3,2},{4,7},{5,4},{6,5},{7,6},{8,11},{9,8},{10,9... | collective-permute-start | bytes 786440 | tf_op jit(solution)/shard_map/ppermute | solution.py:1423
  (67 other events, 254.1 us)

commit v6 on v5

--- a/solution.py
+++ b/solution.py
@@ -669,7 +669,7 @@
             start_second(tick - 4)
         if tick == TOKEN_TICK:
             token_copies(0, x_ref, u_out)
-        if tick == count - 1:
+        if tick == count + 1:
             for k in (1, 2, 3):
                 cp = remote(
                     small_ref, smalls.at[depth], sm_s.at[k - 1], sm_r.at[k - 1],
@@ -697,7 +697,7 @@
         cp.wait_send()
 
 
-TOKEN_TICK = 9
+TOKEN_TICK = 8
 
 
 def gather_all(q, k, v, proj, inner, outer, small, x_rolled, g_rolled):
@@ -935,12 +935,12 @@
         sb[step + 1] = sb[step] + sg[slot]
 
     sb[0] = small_ref[...]
+    token_copies(0, gi_ref, gi_out)
     for group in range(2):
         start_first(group)
     small_send(0, 0, mate, depth)
     send_core(OUTER)
     send_core(INNER)
-    token_copies(0, gi_ref, gi_out)
     small_add(0, 0)
     small_send(1, 1, x_row, depth)
     finish(OUTER)

time: 566 us -> 566 us (level)
  transfers between devices with their start and end apart: 34 -> 34, of which waited for: 12 -> 12; matrix products, arithmetic and copies ran while one was open for 16% -> 16% of each run, Pallas kernels for 32% -> 31%
where the time goes in v6:
time: 566 us; the launch traced here: 559 us
  Pallas kernels  289 us (51%)
  matrix products  127 us (22%)
  starting transfers between devices  40.2 us (7%)
  other arithmetic  38.1 us (7%)
  waiting for transfers between devices  28.8 us (5%)
  local copies, waits for them, and re-layouts  27.3 us (5%)
  between operations  8.98 us (2%)
    pallas_call x1, Pallas kernels, gather_all(): pl.pallas_call(gather_kernel, out_shape=(sd((1024, 1536), BF16), sd((512,...  125 us
    pallas_call x1, Pallas kernels, scatter_all(): pl.pallas_call(scatter_kernel, out_shape=tuple((sd(size, F32) for size in...  59.4 us
    dot_general x17, matrix products, over_tokens(): lax.dot_general(left, right, (((0,), (0,)), ((), ())), preferred_element_...  55 us
    pallas_call x3, Pallas kernels, attend_back(): pl.pallas_call(attend_back_kernel, out_shape=(shape, shape, shape), grid_...  50.2 us
    dot_general x12, matrix products, against(): lax.dot_general(left, right, (((1,), (1,)), ((), ())), preferred_element_...  40 us
    dot_general x10, matrix products, matmul(): return jnp.dot(left, right, preferred_element_type=jnp.float32)  31.8 us
    pallas_call x2, Pallas kernels, ffn_in(): pl.pallas_call(ffn_in_kernel, out_shape=(shape, shape), grid=(hidden // c...  27.5 us
    pallas_call x2, Pallas kernels, attend(): pl.pallas_call(attend_kernel, out_shape=(jax.ShapeDtypeStruct((tokens, wi...  26.5 us
  transfers between devices with their start and end apart: 34, of which 12 were waited for; matrix products, arithmetic and copies ran while one was open for 16% of the time, Pallas kernels for 31%

profile of v6, /device:TPU:0, one launch (start us, length us, event | category | flops | bytes accessed | tf_op | source)
XLA Modules:
  0.0 558.9 jit_solution(17171937884360466934)
XLA Ops:
  5.0 5.3 fusion.101
  10.3 125.1 %shard_map.305 = (bf16[1024,1536]{1,0:T(8,128)(2,1)}, bf16[512,1024]{1,0:T(8,128)(2,1)}, bf16[1024,2048]{1,0:T(8,128)(2,1)}, bf16[2048,1024]{1,0:T(8,128)(2,1)},...) custom-call(bf16[128,256]{1,0:T(8,128)(2,1)} %q_ref.1, bf16[128,256]{1,0:T(8,128)(2,1)} %k_ref.1, ...), custom_call_target="tpu_custom_call" | custom-call | tf_op jit(solution)/shard_map/pallas_call | solution.py:706
  136.3 7.6 %add_convert_fusion.2.q_ref.k_ref.v_ref = bf16[1024,1536]{1,0:T(8,128)(2,1)} fusion(bf16[1024,1024]{1,0:T(8,128)(2,1)} %get-tuple-element.100, bf16[1024,1536]{1,0:T(8,128)(2,1)} %get-tuple-element.101, f32[1536]{0:T(1024)S(1)} %fusion.120), kind=kOutput, calls=%fused_computation.6 | convolution fusion | flops 3224371200 | bytes 8394752 | tf_op jit(solution)/shard_map/dot_general | solution.py:26
  147.3 13.3 %attend.2 = (bf16[1024,512]{1,0:T(8,128)(2,1)S(1)}, f32[1024,512]{1,0:T(8,128)S(1)}) custom-call(s32[1]{0:T(128)} %bitcast.1.flag_ref, bf16[1024,1536]{1,0:T(8,128)(2,1)} %add_convert_fusion.2.q_ref.k_ref.v_ref, bf16[1024,1536]{1,0:T(8,128)(2,1)} %add_convert_fusion.2.q_ref.k_ref.v_ref, bf16[1024,1536]{1,0:T(8,128)(2,1)} %add_convert_fusion.2.q_ref.k_ref.v_ref, ...), custom_call_target="tpu_custom_call" | custom-call | flops 20000000000 | bytes 8000000 | tf_op jit(solution)/shard_map/attend/pallas_call | solution.py:1062
  169.9 2.8 collective-permute-done.2
  174.5 13.8 %ffn_in.2 = (bf16[1024,2048]{1,0:T(8,128)(2,1)}, bf16[1024,2048]{1,0:T(8,128)(2,1)}) custom-call(bf16[1024,1024]{1,0:T(8,128)(2,1)S(1)} %pad_maximum_fusion.2.x_ref, bf16[1024,2048]{1,0:T(8,128)(2,1)} %get-tuple-element.109.w_ref, f32[1,2048]{1,0:T(1,128)S(1)} %reshape.282.b_ref), custom_call_target="tpu_custom_call" | custom-call | flops 14000000000 | bytes 14000000 | tf_op jit(solution)/shard_map/ffn_in/pallas_call | solution.py:1214
  191.1 4.7 fusion.40
  196.0 2.3 fusion.147
  200.3 2.4 collective-permute-done.4
  203.7 5.6 %add_convert_fusion.1.q_ref.k_ref.v_ref = bf16[1024,1536]{1,0:T(8,128)(2,1)} fusion(bf16[1024,1536]{1,0:T(8,128)(2,1)S(1)} %copy-done.70, f32[1536]{0:T(1024)S(1)} %fusion.120, bf16[512,1024]{1,0:T(8,128)(2,1)S(1)} %collective-permute-done.4, bf16[512,1024]{1,0:T(8,128)(2,1)S(1)} %fusion.16), kind=kOutput, calls=%fused_computation.5 | convolution fusion | flops 3228565504 | bytes 8394752 | tf_op jit(solution)/shard_map/dot_general | solution.py:26
  209.3 13.3 %attend.3 = (bf16[1024,512]{1,0:T(8,128)(2,1)S(1)}, f32[1024,512]{1,0:T(8,128)S(1)}) custom-call(s32[1]{0:T(128)} %bitcast.1.flag_ref, bf16[1024,1536]{1,0:T(8,128)(2,1)} %add_convert_fusion.1.q_ref.k_ref.v_ref, bf16[1024,1536]{1,0:T(8,128)(2,1)} %add_convert_fusion.1.q_ref.k_ref.v_ref, bf16[1024,1536]{1,0:T(8,128)(2,1)} %add_convert_fusion.1.q_ref.k_ref.v_ref, ...), custom_call_target="tpu_custom_call" | custom-call | flops 20000000000 | bytes 8000000 | tf_op jit(solution)/shard_map/attend/pallas_call | solution.py:1062
  227.9 2.4 collective-permute-done.6
  231.3 13.7 %ffn_in.3 = (bf16[1024,2048]{1,0:T(8,128)(2,1)}, bf16[1024,2048]{1,0:T(8,128)(2,1)}) custom-call(bf16[1024,1024]{1,0:T(8,128)(2,1)S(1)} %pad_maximum_fusion.4.x_ref, bf16[1024,2048]{1,0:T(8,128)(2,1)} %get-tuple-element.109.w_ref, f32[1,2048]{1,0:T(1,128)S(1)} %reshape.282.b_ref), custom_call_target="tpu_custom_call" | custom-call | flops 14000000000 | bytes 14000000 | tf_op jit(solution)/shard_map/ffn_in/pallas_call | solution.py:1214
  245.1 4.1 fusion.43
  249.8 2.3 fusion.149
  255.4 2.4 collective-permute-done.12
  257.9 5.3 convert_reduce_fusion.1
  263.2 3.4 fusion.46
  270.4 9.6 %convolution_convert_fusion = bf16[2048,1024]{1,0:T(8,128)(2,1)} fusion(bf16[1024,2048]{1,0:T(8,128)(2,1)} %get-tuple-element.121, bf16[512,1024]{1,0:T(8,128)(2,1)} %copy-done.75, bf16[512,1024]{1,0:T(8,128)(2,1)} %copy-done.44), kind=kOutput, calls=%fused_computation.7 | convolution fusion | flops 4301258752 | bytes 10485760 | tf_op jit(solution)/shard_map/dot_general | solution.py:30
  280.0 4.9 multiply_reduce_fusion.2
  288.1 6.5 %fusion.137 = bf16[1024,2048]{1,0:T(8,128)(2,1)} fusion(bf16[1024,2048]{1,0:T(8,128)(2,1)S(1)} %copy-done.37, bf16[512,1024]{1,0:T(8,128)(2,1)S(1)} %copy-done.43, bf16[512,1024]{1,0:T(8,128)(2,1)S(1)} %copy-done.27), kind=kOutput, calls=%fused_computation.319 | convolution fusion | flops 4299161600 | bytes 10485760 | tf_op jit(solution)/shard_map/dot_general | solution.py:30
  294.8 8.6 %collective-permute-start.11 = (bf16[512,256]{1,0:T(8,128)(2,1)S(1)}, bf16[512,256]{1,0:T(8,128)(2,1)S(1)}, u32[]{:S(2)}, u32[]{:S(2)}) collective-permute-start(bf16[512,256]{1,0:T(8,128)(2,1)S(1)} %get-tuple-element.232), channel_id=1, source_target_pairs={{0,3},{1,1},{2,7},{3,5},{4,0},{5,2},{6,4},{7,6},{8,11},{9,9},{10,1... | collective-permute-start | bytes 786440 | tf_op jit(solution)/shard_map/ppermute | solution.py:1440
  303.9 3.5 collective-permute-start.9
  309.6 24.4 %attend_back.3 = (bf16[1024,512]{1,0:T(8,128)(2,1)S(1)}, bf16[1024,512]{1,0:T(8,128)(2,1)S(1)}, bf16[1024,512]{1,0:T(8,128)(2,1)S(1)}) custom-call(s32[1]{0:T(128)} %bitcast.1.flag_ref, bf16[1024,1536]{1,0:T(8,128)(2,1)} %add_convert_fusion.1.q_ref.k_ref.v_ref, bf16[1024,1536]{1,0:T(8,128)(2,1)} %add_convert_fusion.1.q_ref.k_ref.v_ref, ...), custom_call_target="tpu_custom_call" | custom-call | flops 40000000000 | bytes 10000000 | tf_op jit(solution)/shard_map/attend_back/pallas_call | solution.py:1147
  343.3 2.3 convert_reduce_fusion.3
  348.6 8.7 %convert_reduce_fusion = (f32[2048]{0:T(1024)S(1)}, bf16[1024,2048]{1,0:T(8,128)(2,1)S(1)}) fusion(bf16[1024,2048]{1,0:T(8,128)(2,1)} %get-tuple-element.143, bf16[2048,1024]{1,0:T(8,128)(2,1)} %get-tuple-element.111, bf16[512,1024]{1,0:T(8,128)(2,1)} %collective-permute-done.16, bf16[512,1024]{1,0:T(8,128)(2,1)} %get-tuple-element.208), kind=kOutput, calls=%fused_computation | convolution fusion | flops 4309645312 | bytes 14688256 | tf_op jit(solution)/shard_map/dot_general | solution.py:36
  357.4 3.4 fusion.49
  362.3 4.8 add_convert_fusion.7
  368.7 4.1 add_convert_fusion.8
  373.4 2.4 fusion.151
  377.3 2.3 convert_reduce_fusion.5
  380.8 6.5 %add_convert_fusion = bf16[1024,2048]{1,0:T(8,128)(2,1)S(1)} fusion(bf16[1024,2048]{1,0:T(8,128)(2,1)S(1)} %copy-done.77, bf16[1024,2048]{1,0:T(8,128)(2,1)S(1)} %copy-done.39, bf16[512,1024]{1,0:T(8,128)(2,1)} %collective-permute-done.2, bf16[512,1024]{1,0:T(8,128)(2,1)} %fusion.15), kind=kOutput, calls=%fused_computation.2 | convolution fusion | flops 4305453056 | bytes 14680064 | tf_op jit(solution)/shard_map/dot_general | solution.py:30
  393.1 3.3 convolution_convert_fusion.1.do_ref
  396.4 12.8 %attend_back.4 = (bf16[1024,256]{1,0:T(8,128)(2,1)S(1)}, bf16[1024,256]{1,0:T(8,128)(2,1)S(1)}, bf16[1024,256]{1,0:T(8,128)(2,1)S(1)}) custom-call(s32[1]{0:T(128)} %bitcast.1.flag_ref, bf16[1024,1536]{1,0:T(8,128)(2,1)} %add_convert_fusion.2.q_ref.k_ref.v_ref, bf16[1024,1536]{1,0:T(8,128)(2,1)} %add_convert_fusion.2.q_ref.k_ref.v_ref, ...), custom_call_target="tpu_custom_call" | custom-call | flops 20000000000 | bytes 5000000 | tf_op jit(solution)/shard_map/attend_back/pallas_call | solution.py:1147
  409.2 3.0 fusion.90
  416.4 13.0 %attend_back.5 = (bf16[1024,256]{1,0:T(8,128)(2,1)S(1)}, bf16[1024,256]{1,0:T(8,128)(2,1)S(1)}, bf16[1024,256]{1,0:T(8,128)(2,1)S(1)}) custom-call(s32[1]{0:T(128)} %bitcast.1.flag_ref, bf16[1024,1536]{1,0:T(8,128)(2,1)} %add_convert_fusion.2.q_ref.k_ref.v_ref, bf16[1024,1536]{1,0:T(8,128)(2,1)} %add_convert_fusion.2.q_ref.k_ref.v_ref, ...), custom_call_target="tpu_custom_call" | custom-call | flops 20000000000 | bytes 5000000 | tf_op jit(solution)/shard_map/attend_back/pallas_call | solution.py:1147
  431.5 3.0 fusion.86
  443.9 2.3 fusion.93
  446.3 2.9 collective-permute-start.30
  449.7 2.2 collective-permute-start.32
  456.0 2.3 add_convert_fusion.5.refs_2_
  458.3 2.3 add_convert_fusion.4.refs_3_
  467.9 2.3 collective-permute-start.28
  470.2 5.4 collective-permute-start.29
  475.8 3.1 collective-permute-done.27
  478.9 10.4 %collective-permute-done.28 = bf16[256,512]{1,0:T(8,128)(2,1)S(1)} collective-permute-done((bf16[256,512]{1,0:T(8,128)(2,1)S(1)}, bf16[256,512]{1,0:T(8,128)(2,1)S(1)}, u32[]{:S(2)}, u32[]{:S(2)}) %collective-permute-start.28) | collective-permute-done | bytes 262176 | tf_op jit(solution)/shard_map/ppermute | solution.py:1423
  491.1 59.4 %shard_map.306 = (f32[256,128]{1,0:T(8,128)S(1)}, f32[128,256]{1,0:T(8,128)S(1)}, f32[128,256]{1,0:T(8,128)S(1)}, f32[128,256]{1,0:T(8,128)S(1)}, f32[128,1024]{...) custom-call(bf16[512,1024]{1,0:T(8,128)(2,1)S(1)} %add_convert_fusion.9.refs_0_, ...), custom_call_target="tpu_custom_call" | custom-call | tf_op jit(solution)/shard_map/pallas_call | solution.py:995
  551.2 2.6 fusion.100
  (402 shorter events, 97.8 us)
Async XLA Ops:
  0.8 143.1 %collective-permute-start = (s32[2048]{0:T(1024)}, s32[2048]{0:T(1024)S(1)}, u32[]{:S(2)}, u32[]{:S(2)}) collective-permute-start(s32[2048]{0:T(1024)} %bitcast.156), channel_id=1, source_target_pairs={{0,4},{4,0},{8,12},{12,8},{16,20},{20,16},{24,28},{28,24},{1,5},{5... | collective-permute-start | bytes 24584 | tf_op jit(solution)/shard_map/ppermute | solution.py:1236
  147.3 62.0 %copy-start.2 = (s32[1,1024]{0,1:T(8,128)}, s32[1,1024]{0,1:T(8,128)S(1)}, u32[]{:S(2)}) copy-start(s32[1,1024]{0,1:T(8,128)S(1)} %copy.53) | copy-start | bytes 12292
  147.3 14.3 %copy-start.18 = (bf16[512,1024]{1,0:T(8,128)(2,1)S(1)}, bf16[512,1024]{1,0:T(8,128)(2,1)}, u32[]{:S(2)}) copy-start(bf16[512,1024]{1,0:T(8,128)(2,1)} %get-tuple-element.104) | copy-start | bytes 3145732
  163.2 3.0 collective-permute-start.1
  168.1 30.4 %copy-start.10 = (f32[512,1024]{1,0:T(8,128)}, f32[512,1024]{1,0:T(8,128)S(1)}, u32[]{:S(2)}) copy-start(f32[512,1024]{1,0:T(8,128)S(1)} %get-tuple-element.224) | copy-start | bytes 6291460
  168.1 30.4 %copy-start.49 = (f32[512]{0:T(512)}, f32[512]{0:T(512)S(1)}, u32[]{:S(2)}) copy-start(f32[512]{0:T(512)S(1)} %get-tuple-element.310) | copy-start | bytes 6148
  168.1 30.4 %copy-start.51 = (f32[512]{0:T(512)}, f32[512]{0:T(512)S(1)}, u32[]{:S(2)}) copy-start(f32[512]{0:T(512)S(1)} %get-tuple-element.311) | copy-start | bytes 6148
  169.8 3.0 collective-permute-start.2
  195.8 2.7 collective-permute-start.3
  199.5 26.6 %copy-start.12 = (f32[512,1024]{1,0:T(8,128)}, f32[512,1024]{1,0:T(8,128)S(1)}, u32[]{:S(2)}) copy-start(f32[512,1024]{1,0:T(8,128)S(1)} %get-tuple-element.223) | copy-start | bytes 6291460
  200.0 2.7 collective-permute-start.4
  209.3 13.4 %copy-start.19 = (bf16[512,1024]{1,0:T(8,128)(2,1)S(1)}, bf16[512,1024]{1,0:T(8,128)(2,1)}, u32[]{:S(2)}) copy-start(bf16[512,1024]{1,0:T(8,128)(2,1)} %get-tuple-element.104) | copy-start | bytes 3145732
  223.4 2.7 collective-permute-start.5
  227.6 2.7 collective-permute-start.6
  231.3 13.7 %copy-start.69 = (bf16[2048,1024]{1,0:T(8,128)(2,1)S(1)}, bf16[2048,1024]{1,0:T(8,128)(2,1)}, u32[]{:S(2)}) copy-start(bf16[2048,1024]{1,0:T(8,128)(2,1)} %get-tuple-element.111) | copy-start | bytes 12582916
  249.5 2.7 collective-permute-start.7
  255.1 2.7 collective-permute-start.12
  268.1 11.9 %collective-permute-start.13 = (bf16[512,1024]{1,0:T(8,128)(2,1)}, bf16[512,1024]{1,0:T(8,128)(2,1)}, u32[]{:S(2)}, u32[]{:S(2)}) collective-permute-start(bf16[512,1024]{1,0:T(8,128)(2,1)} %fusion.46), channel_id=1, source_target_pairs={{0,4},{4,0},{8,12},{12,8},{16,20},{20,16},{24,28},{28,24},{1,5},{5... | collective-permute-start | bytes 3145736 | tf_op jit(solution)/shard_map/ppermute | solution.py:1236
  270.3 9.6 %copy-start.15 = (f32[512,1024]{1,0:T(8,128)S(1)}, f32[512,1024]{1,0:T(8,128)}, u32[]{:S(2)}) copy-start(f32[512,1024]{1,0:T(8,128)} %copy-done.14) | copy-start | bytes 6291460
  285.7 22.5 %copy-start.22 = (bf16[512,1024]{1,0:T(8,128)(2,1)}, bf16[512,1024]{1,0:T(8,128)(2,1)S(1)}, u32[]{:S(2)}) copy-start(bf16[512,1024]{1,0:T(8,128)(2,1)S(1)} %get-tuple-element.216) | copy-start | bytes 3145732
  285.7 22.5 %collective-permute-start.14 = (bf16[512,1024]{1,0:T(8,128)(2,1)S(1)}, bf16[512,1024]{1,0:T(8,128)(2,1)S(1)}, u32[]{:S(2)}, u32[]{:S(2)}) collective-permute-start(bf16[512,1024]{1,0:T(8,128)(2,1)S(1)} %get-tuple-element.216), channel_id=1, source_target_pairs={{0,4},{4,0},{8,12},{12,8},{16,20},{20,16},{24,28},{28,24},{1,5},{5... | collective-permute-start | bytes 3145736 | tf_op jit(solution)/shard_map/ppermute | solution.py:1236
  294.6 13.6 %copy-start.20 = (bf16[512,1024]{1,0:T(8,128)(2,1)S(1)}, bf16[512,1024]{1,0:T(8,128)(2,1)}, u32[]{:S(2)}) copy-start(bf16[512,1024]{1,0:T(8,128)(2,1)} %get-tuple-element.104) | copy-start | bytes 3145732
  294.8 39.2 %collective-permute-start.11 = (bf16[512,256]{1,0:T(8,128)(2,1)S(1)}, bf16[512,256]{1,0:T(8,128)(2,1)S(1)}, u32[]{:S(2)}, u32[]{:S(2)}) collective-permute-start(bf16[512,256]{1,0:T(8,128)(2,1)S(1)} %get-tuple-element.232), channel_id=1, source_target_pairs={{0,3},{1,1},{2,7},{3,5},{4,0},{5,2},{6,4},{7,6},{8,11},{9,9},{10,1... | collective-permute-start | bytes 786440 | tf_op jit(solution)/shard_map/ppermute | solution.py:1440
  303.4 30.6 %collective-permute-start.10 = (bf16[512,256]{1,0:T(8,128)(2,1)S(1)}, bf16[512,256]{1,0:T(8,128)(2,1)S(1)}, u32[]{:S(2)}, u32[]{:S(2)}) collective-permute-start(bf16[512,256]{1,0:T(8,128)(2,1)S(1)} %get-tuple-element.233), channel_id=1, source_target_pairs={{0,2},{1,0},{2,6},{3,4},{4,3},{5,1},{6,7},{7,5},{8,10},{9,8},{10,1... | collective-permute-start | bytes 786440 | tf_op jit(solution)/shard_map/ppermute | solution.py:1440
  303.9 30.2 %collective-permute-start.9 = (bf16[512,256]{1,0:T(8,128)(2,1)S(1)}, bf16[512,256]{1,0:T(8,128)(2,1)S(1)}, u32[]{:S(2)}, u32[]{:S(2)}) collective-permute-start(bf16[512,256]{1,0:T(8,128)(2,1)S(1)} %get-tuple-element.234), channel_id=1, source_target_pairs={{0,1},{1,3},{2,5},{3,7},{4,2},{5,0},{6,6},{7,4},{8,9},{9,11},{10,1... | collective-permute-start | bytes 786440 | tf_op jit(solution)/shard_map/ppermute | solution.py:1440
  307.4 26.6 %collective-permute-start.8 = (bf16[512,256]{1,0:T(8,128)(2,1)S(1)}, bf16[512,256]{1,0:T(8,128)(2,1)S(1)}, u32[]{:S(2)}, u32[]{:S(2)}) collective-permute-start(bf16[512,256]{1,0:T(8,128)(2,1)S(1)} %get-tuple-element.235), channel_id=1, source_target_pairs={{0,0},{1,2},{2,4},{3,6},{4,1},{5,3},{6,5},{7,7},{8,8},{9,10},{10,1... | collective-permute-start | bytes 786440 | tf_op jit(solution)/shard_map/ppermute | solution.py:1440
  338.1 3.7 collective-permute-start.15
  345.6 3.0 collective-permute-start.16
  367.1 42.1 %collective-permute-start.20 = (bf16[1024,512]{1,0:T(8,128)(2,1)}, bf16[1024,512]{1,0:T(8,128)(2,1)}, u32[]{:S(2)}, u32[]{:S(2)}) collective-permute-start(bf16[1024,512]{1,0:T(8,128)(2,1)} %add_convert_fusion.7), channel_id=1, source_target_pairs={{0,8},{4,12},{8,0},{12,4},{16,24},{20,28},{24,16},{28,20},{1,9},{5... | collective-permute-start | bytes 3145736 | tf_op jit(solution)/shard_map/ppermute | solution.py:1399
  368.6 7.2 %collective-permute-start.17 = (bf16[512,1024]{1,0:T(8,128)(2,1)S(1)}, bf16[512,1024]{1,0:T(8,128)(2,1)S(1)}, u32[]{:S(2)}, u32[]{:S(2)}) collective-permute-start(bf16[512,1024]{1,0:T(8,128)(2,1)S(1)} %copy-done.76), channel_id=1, source_target_pairs={{0,4},{4,0},{8,12},{12,8},{16,20},{20,16},{24,28},{28,24},{1,5},{5... | collective-permute-start | bytes 3145736 | tf_op jit(solution)/shard_map/ppermute | solution.py:1236
  372.8 36.4 %collective-permute-start.19 = (bf16[1024,512]{1,0:T(8,128)(2,1)}, bf16[1024,512]{1,0:T(8,128)(2,1)}, u32[]{:S(2)}, u32[]{:S(2)}) collective-permute-start(bf16[1024,512]{1,0:T(8,128)(2,1)} %add_convert_fusion.8), channel_id=1, source_target_pairs={{0,16},{4,20},{8,24},{12,28},{16,0},{20,4},{24,8},{28,12},{1,17},{... | collective-permute-start | bytes 3145736 | tf_op jit(solution)/shard_map/ppermute | solution.py:1399
  379.6 13.4 %collective-permute-start.18 = (bf16[512,1024]{1,0:T(8,128)(2,1)}, bf16[512,1024]{1,0:T(8,128)(2,1)}, u32[]{:S(2)}, u32[]{:S(2)}) collective-permute-start(bf16[512,1024]{1,0:T(8,128)(2,1)} %get-tuple-element.213), channel_id=1, source_target_pairs={{0,4},{4,0},{8,12},{12,8},{16,20},{20,16},{24,28},{28,24},{1,5},{5... | collective-permute-start | bytes 3145736 | tf_op jit(solution)/shard_map/ppermute | solution.py:1236
  390.8 38.6 %collective-permute-start.22 = (bf16[512,1024]{1,0:T(8,128)(2,1)}, bf16[512,1024]{1,0:T(8,128)(2,1)}, u32[]{:S(2)}, u32[]{:S(2)}) collective-permute-start(bf16[512,1024]{1,0:T(8,128)(2,1)} %get-tuple-element.229), channel_id=1, source_target_pairs={{0,8},{4,12},{8,0},{12,4},{16,24},{20,28},{24,16},{28,20},{1,9},{5... | collective-permute-start | bytes 3145736 | tf_op jit(solution)/shard_map/ppermute | solution.py:1399
  392.3 37.2 %collective-permute-start.21 = (bf16[512,1024]{1,0:T(8,128)(2,1)}, bf16[512,1024]{1,0:T(8,128)(2,1)}, u32[]{:S(2)}, u32[]{:S(2)}) collective-permute-start(bf16[512,1024]{1,0:T(8,128)(2,1)} %get-tuple-element.230), channel_id=1, source_target_pairs={{0,16},{4,20},{8,24},{12,28},{16,0},{20,4},{24,8},{28,12},{1,17},{... | collective-permute-start | bytes 3145736 | tf_op jit(solution)/shard_map/ppermute | solution.py:1399
  396.4 12.8 %copy-start.33 = (bf16[1024,2048]{1,0:T(8,128)(2,1)S(1)}, bf16[1024,2048]{1,0:T(8,128)(2,1)}, u32[]{:S(2)}) copy-start(bf16[1024,2048]{1,0:T(8,128)(2,1)} %get-tuple-element.110) | copy-start | bytes 12582916
  414.3 21.5 %collective-permute-start.23 = (bf16[1024,256]{1,0:T(8,128)(2,1)}, bf16[1024,256]{1,0:T(8,128)(2,1)S(1)}, u32[]{:S(2)}, u32[]{:S(2)}) collective-permute-start(bf16[1024,256]{1,0:T(8,128)(2,1)} %fusion.90), channel_id=1, source_target_pairs={{0,8},{4,12},{8,0},{12,4},{16,24},{20,28},{24,16},{28,20},{1,9},{5... | collective-permute-start | bytes 1572872 | tf_op jit(solution)/shard_map/ppermute | solution.py:1407
  415.9 20.0 %collective-permute-start.24 = (bf16[1024,256]{1,0:T(8,128)(2,1)S(1)}, bf16[1024,256]{1,0:T(8,128)(2,1)S(1)}, u32[]{:S(2)}, u32[]{:S(2)}) collective-permute-start(bf16[1024,256]{1,0:T(8,128)(2,1)S(1)} %fusion.87), channel_id=1, source_target_pairs={{0,16},{4,20},{8,24},{12,28},{16,0},{20,4},{24,8},{28,12},{1,17},{... | collective-permute-start | bytes 1572872 | tf_op jit(solution)/shard_map/ppermute | solution.py:1407
  443.9 10.1 %copy-start.72 = (bf16[1024,1536]{1,0:T(8,128)(2,1)S(1)}, bf16[1024,1536]{1,0:T(8,128)(2,1)}, u32[]{:S(2)}) copy-start(bf16[1024,1536]{1,0:T(8,128)(2,1)} %get-tuple-element.101) | copy-start | bytes 9437188
  446.3 21.5 %collective-permute-start.30 = (bf16[512,256]{1,0:T(8,128)(2,1)S(1)}, bf16[512,256]{1,0:T(8,128)(2,1)S(1)}, u32[]{:S(2)}, u32[]{:S(2)}) collective-permute-start(bf16[512,256]{1,0:T(8,128)(2,1)S(1)} %pad_maximum_fusion.17), channel_id=1, source_target_pairs={{0,1},{1,2},{2,3},{3,0},{4,5},{5,6},{6,7},{7,4},{8,9},{9,10},{10,1... | collective-permute-start | bytes 786440 | tf_op jit(solution)/shard_map/ppermute | solution.py:1423
  449.2 21.0 %collective-permute-start.31 = (bf16[512,256]{1,0:T(8,128)(2,1)S(1)}, bf16[512,256]{1,0:T(8,128)(2,1)S(1)}, u32[]{:S(2)}, u32[]{:S(2)}) collective-permute-start(bf16[512,256]{1,0:T(8,128)(2,1)S(1)} %pad_maximum_fusion.18), channel_id=1, source_target_pairs={{0,2},{1,3},{2,0},{3,1},{4,6},{5,7},{6,4},{7,5},{8,10},{9,11},{10,... | collective-permute-start | bytes 786440 | tf_op jit(solution)/shard_map/ppermute | solution.py:1423
  449.7 25.9 %collective-permute-start.32 = (bf16[512,256]{1,0:T(8,128)(2,1)S(1)}, bf16[512,256]{1,0:T(8,128)(2,1)S(1)}, u32[]{:S(2)}, u32[]{:S(2)}) collective-permute-start(bf16[512,256]{1,0:T(8,128)(2,1)S(1)} %pad_maximum_fusion.19), channel_id=1, source_target_pairs={{0,3},{1,0},{2,1},{3,2},{4,7},{5,4},{6,5},{7,6},{8,11},{9,8},{10,9... | collective-permute-start | bytes 786440 | tf_op jit(solution)/shard_map/ppermute | solution.py:1423
  452.0 12.4 %collective-permute-start.25 = (bf16[256,1024]{1,0:T(8,128)(2,1)S(1)}, bf16[256,1024]{1,0:T(8,128)(2,1)S(1)}, u32[]{:S(2)}, u32[]{:S(2)}) collective-permute-start(bf16[256,1024]{1,0:T(8,128)(2,1)S(1)} %get-tuple-element.169), channel_id=1, source_target_pairs={{0,8},{4,12},{8,0},{12,4},{16,24},{20,28},{24,16},{28,20},{1,9},{5... | collective-permute-start | bytes 1572872 | tf_op jit(solution)/shard_map/ppermute | solution.py:1407
  453.5 11.9 %collective-permute-start.26 = (bf16[256,1024]{1,0:T(8,128)(2,1)S(1)}, bf16[256,1024]{1,0:T(8,128)(2,1)S(1)}, u32[]{:S(2)}, u32[]{:S(2)}) collective-permute-start(bf16[256,1024]{1,0:T(8,128)(2,1)S(1)} %get-tuple-element.170), channel_id=1, source_target_pairs={{0,16},{4,20},{8,24},{12,28},{16,0},{20,4},{24,8},{28,12},{1,17},{... | collective-permute-start | bytes 1572872 | tf_op jit(solution)/shard_map/ppermute | solution.py:1407
  464.3 25.2 %collective-permute-start.33 = (bf16[512,1024]{1,0:T(8,128)(2,1)S(1)}, bf16[512,1024]{1,0:T(8,128)(2,1)S(1)}, u32[]{:S(2)}, u32[]{:S(2)}) collective-permute-start(bf16[512,1024]{1,0:T(8,128)(2,1)S(1)} %fusion.37), channel_id=1, source_target_pairs={{0,4},{4,0},{8,12},{12,8},{16,20},{20,16},{24,28},{28,24},{1,5},{5... | collective-permute-start | bytes 3145736 | tf_op jit(solution)/shard_map/ppermute | solution.py:1236
  467.7 21.8 %copy-start.16 = (f32[512,1024]{1,0:T(8,128)S(1)}, f32[512,1024]{1,0:T(8,128)}, u32[]{:S(2)}) copy-start(f32[512,1024]{1,0:T(8,128)} %get-tuple-element.214) | copy-start | bytes 6291460
  467.7 11.2 %collective-permute-start.27 = (bf16[256,512]{1,0:T(8,128)(2,1)S(1)}, bf16[256,512]{1,0:T(8,128)(2,1)S(1)}, u32[]{:S(2)}, u32[]{:S(2)}) collective-permute-start(bf16[256,512]{1,0:T(8,128)(2,1)S(1)} %pad_maximum_fusion.14), channel_id=1, source_target_pairs={{0,1},{1,2},{2,3},{3,0},{4,5},{5,6},{6,7},{7,4},{8,9},{9,10},{10,1... | collective-permute-start | bytes 786440 | tf_op jit(solution)/shard_map/ppermute | solution.py:1423
  467.9 21.5 %collective-permute-start.28 = (bf16[256,512]{1,0:T(8,128)(2,1)S(1)}, bf16[256,512]{1,0:T(8,128)(2,1)S(1)}, u32[]{:S(2)}, u32[]{:S(2)}) collective-permute-start(bf16[256,512]{1,0:T(8,128)(2,1)S(1)} %pad_maximum_fusion.15), channel_id=1, source_target_pairs={{0,2},{1,3},{2,0},{3,1},{4,6},{5,7},{6,4},{7,5},{8,10},{9,11},{10,... | collective-permute-start | bytes 786440 | tf_op jit(solution)/shard_map/ppermute | solution.py:1423
  470.2 19.1 %collective-permute-start.29 = (bf16[256,512]{1,0:T(8,128)(2,1)S(1)}, bf16[256,512]{1,0:T(8,128)(2,1)S(1)}, u32[]{:S(2)}, u32[]{:S(2)}) collective-permute-start(bf16[256,512]{1,0:T(8,128)(2,1)S(1)} %pad_maximum_fusion.16), channel_id=1, source_target_pairs={{0,3},{1,0},{2,1},{3,2},{4,7},{5,4},{6,5},{7,6},{8,11},{9,8},{10,9... | collective-permute-start | bytes 786440 | tf_op jit(solution)/shard_map/ppermute | solution.py:1423
  (67 other events, 254.1 us)
